TPU v7x, 32 devices: a whole 2x2x4 slice. The times are simulated.
32 devices in a mesh: seq: 16 (over z, y, x), mp: 2 (over core).
Axes of the slice: x: 2, y: 2, z: 4, core: 2. Of those that a mesh axis runs over, the one named last changes fastest.
Arguments:
- layer_input: bfloat16 [2, 4096, 2048], P(None, 'seq'), may hold values from -6 to 6
- cotangent: bfloat16 [2, 4096, 2048], P(None, 'seq'), may hold values from -8 to 8
- teacher: bfloat16 [2, 4096, 2048], P(None, 'seq'), may hold values from -12 to 12
- target_slot: int32 [2, 4096], P(None, 'seq'), may hold values from 0 to 4095, as said below
- seq_start: int32 [2, 2], replicated, may hold values from 0 to 4032, as said below
- seq_len: int32 [2, 2], replicated, may hold values from 1 to 4096, as said below
- w_query: bfloat16 [2048, 1024], P('seq', 'mp'), may hold values from -0.125 to 0.125
- w_key: bfloat16 [2048, 1024], P('seq', 'mp'), may hold values from -0.125 to 0.125
- w_value: bfloat16 [2048, 2048], P('seq', 'mp'), may hold values from -0.125 to 0.125
- w_gate_out: bfloat16 [2048, 2048], P('seq', 'mp'), may hold values from -0.125 to 0.125
- w_out: bfloat16 [2048, 2048], P('seq', 'mp'), may hold values from -0.25 to 0.25
- w_ffn_gate: bfloat16 [2048, 5632], P('seq', 'mp'), may hold values from -0.125 to 0.125
- w_ffn_up: bfloat16 [2048, 5632], P('seq', 'mp'), may hold values from -0.125 to 0.125
- w_ffn_down: bfloat16 [2048, 5632], P('seq', 'mp'), may hold values from -0.15625 to 0.15625
- w_rank_down: bfloat16 [2048, 16], P('seq'), may hold values from -0.125 to 0.125
- w_rank_up: bfloat16 [16, 1024], P(None, 'mp'), may hold values from -1.5 to 1.5
- decay_bias: bfloat16 [1024], P('mp'), may hold values from 1 to 9
- gain_attn: bfloat16 [2048], P('seq'), may hold values from 0.5 to 1.5
- gain_ffn: bfloat16 [2048], P('seq'), may hold values from 0.5 to 1.5
- gain_head: bfloat16 [512], replicated, may hold values from 0.5 to 1.5
Outputs:
- output: bfloat16 [2, 4096, 2048], P(None, 'seq')
- loss: float32 [], replicated
- input_grad: bfloat16 [2, 4096, 2048], P(None, 'seq')
- grad_w_query: float32 [2048, 1024], P('seq', 'mp')
- grad_w_key: float32 [2048, 1024], P('seq', 'mp')
- grad_w_value: float32 [2048, 2048], P('seq', 'mp')
- grad_w_gate_out: float32 [2048, 2048], P('seq', 'mp')
- grad_w_out: float32 [2048, 2048], P('seq', 'mp')
- grad_w_ffn_gate: float32 [2048, 5632], P('seq', 'mp')
- grad_w_ffn_up: float32 [2048, 5632], P('seq', 'mp')
- grad_w_ffn_down: float32 [2048, 5632], P('seq', 'mp')
- grad_w_rank_down: float32 [2048, 16], P('seq')
- grad_w_rank_up: float32 [16, 1024], P(None, 'mp')
- grad_decay_bias: float32 [1024], P('mp')
- grad_gain_attn: float32 [2048], P('seq')
- grad_gain_ffn: float32 [2048], P('seq')
- grad_gain_head: float32 [512], replicated
Inputs may be any that keep to these rules, and one draw needn't show every extreme that they name: `target_slot`: for each micro-batch a permutation of the layout slots; the tokens that one index of seq holds go in groups of exactly 32 to half of the indices of seq and to no others, which ones drawn from the seed. `seq_start`: in each micro-batch the sequences lie one after another from layout slot 0, each beginning at a multiple of 64, the first at 0, the last region ending at 4096; one sequence of each micro-batch, drawn from the seed, begins on the first index of seq and has valid tokens on the last. The maximum bounds the range and is not a buffer bound. `seq_len`: A sequence's valid tokens fill its region from the front and leave fewer than 64 slots at its end. The maximum bounds the range and is not a buffer bound.
All inputs are finite; a program needn't handle non-finite values.
Results may differ from a plain program's by a relative error of at most 0.014.
The roundings to bfloat16 on the way count: a program that leaves them out, or rounds other values in their place, can miss the bound.
Values may be sent and summed in bfloat16 or wider, within the bound.
A program may use at most 448 MiB of HBM per device.

v0:
```python
import jax
import jax.numpy as jnp
from jax import lax
from jax.sharding import PartitionSpec as P

SPAN = 64
HEAD_K = 256


eps = 1e-06
highest = lax.Precision.HIGHEST
contract_last = (((1,), (1,)), ((), ()))
contract_rows = (((0,), (0,)), ((), ()))


def carried_in(value, axis, join, neutral, backward):
    count, mine = (lax.axis_size(axis), lax.axis_index(axis))
    pieces = jax.tree.map(lambda part: lax.all_gather(part, axis), value)
    if backward:
        pieces = jax.tree.map(lambda part: part[::-1], pieces)
        mine = count - 1 - mine
    running = jax.tree.map(
        lambda part, zero: jnp.full_like(part, 0) + jnp.asarray(zero, part.dtype), value, neutral
    )

    def step(position, running):
        longer = join(running, jax.tree.map(lambda part: part[position], pieces))
        return jax.tree.map(lambda new, old: jnp.where(position < mine, new, old), longer, running)

    return lax.fori_loop(0, count - 1, step, running)


def rms_scale(values):
    return lax.rsqrt(jnp.mean(values * values, axis=-1, keepdims=True) + eps)


def head_scale(values):
    square_mean = jnp.mean(values * values, axis=-1, keepdims=True)
    return (lax.rsqrt(jnp.maximum(square_mean, 1.0)), (square_mean > 1.0).astype(jnp.float32))


def layout_flags(starts, lengths, positions):
    begun = (positions[:, None] >= starts[None, :]).astype(jnp.int32)
    owner = jnp.sum(begun, axis=1) - 1
    picked = (owner[:, None] == jnp.arange(starts.shape[0], dtype=jnp.int32)[None, :]).astype(
        jnp.int32
    )
    own_start = jnp.sum(picked * starts[None, :], axis=1)
    own_length = jnp.sum(picked * lengths[None, :], axis=1)
    valid = (positions - own_start < own_length).astype(jnp.float32)
    boundary = jnp.any(positions[:, None] == starts[None, :], axis=1).astype(jnp.float32)
    return (valid, boundary)


def span_step(carried, pieces):
    queries, key_rows, value_rows, decays, reset = pieces
    before = carried * (1.0 - reset)
    cumul = jnp.cumsum(decays, axis=0)
    lifted = queries * jnp.exp(cumul)
    lowered = key_rows * jnp.exp(-cumul)
    scores = jnp.einsum("thc,shc->hts", lifted, lowered, precision=highest)
    length = decays.shape[0]
    causal = (jnp.arange(length)[:, None] >= jnp.arange(length)[None, :]).astype(jnp.float32)
    mixed = jnp.einsum("hts,shv->thv", scores * causal[None], value_rows, precision=highest)
    mixed = mixed + jnp.einsum("thc,hcv->thv", lifted, before, precision=highest)
    final = cumul[-1]
    faded = key_rows * jnp.exp(final[None] - cumul)
    after = jnp.exp(final)[:, :, None] * before + jnp.einsum(
        "thc,thv->hcv", faded, value_rows, precision=highest
    )
    return (after, mixed)


def run_local(queries, key_rows, value_rows, decays, resets, entering):
    rows, heads, key_width = queries.shape
    value_width = value_rows.shape[-1]
    blocks = rows // SPAN
    pieces = (
        queries.reshape(blocks, SPAN, heads, key_width),
        key_rows.reshape(blocks, SPAN, heads, key_width),
        value_rows.reshape(blocks, SPAN, heads, value_width),
        decays.reshape(blocks, SPAN, heads, key_width),
        resets,
    )
    leaving, mixed = lax.scan(span_step, entering, pieces)
    return (mixed.reshape(rows, heads, value_width), leaving)


def combine_affine(earlier, later):
    return (earlier[0] * later[0], later[0][..., None] * earlier[1] + later[1])


def project(left, right):
    return jnp.dot(left, right, preferred_element_type=jnp.float32)


def project_back(left, right):
    return lax.dot_general(left, right, contract_last, preferred_element_type=jnp.float32)


def outer_sum(left, right):
    return lax.dot_general(left, right, contract_rows, preferred_element_type=jnp.float32)


def norm_back(grad_unit, unit, scaling):
    return scaling * (grad_unit - unit * jnp.mean(grad_unit * unit, axis=-1, keepdims=True))


def local(
    layer_input,
    cotangent,
    teacher,
    target_slot,
    seq_start,
    seq_len,
    w_query,
    w_key,
    w_value,
    w_gate_out,
    w_out,
    w_ffn_gate,
    w_ffn_up,
    w_ffn_down,
    w_rank_down,
    w_rank_up,
    decay_bias,
    gain_attn,
    gain_ffn,
    gain_head,
):
    devices = lax.axis_size("seq")
    device = lax.axis_index("seq")
    micro_count, tok_rows, width = layer_input.shape
    per_pair = 2 * tok_rows // devices
    per_device = micro_count * per_pair
    shards = (
        w_query,
        w_key,
        w_value,
        w_gate_out,
        w_out,
        w_ffn_gate,
        w_ffn_up,
        w_ffn_down,
        w_rank_down,
        gain_attn,
        gain_ffn,
    )
    rank_up = w_rank_up.astype(jnp.float32)
    bias_local = decay_bias.astype(jnp.float32)
    head_gain = gain_head.astype(jnp.float32)
    heads_here = w_query.shape[1] // HEAD_K
    query_scaling = HEAD_K ** (-0.5)
    source_ids = jnp.arange(devices, dtype=jnp.int32)
    slot_list = []
    for micro_index in range(micro_count):
        destination = target_slot[micro_index] // tok_rows
        matches = (destination[:, None] == source_ids[None, :]).astype(jnp.int32)
        arrival = jnp.sum(jnp.cumsum(matches, axis=0) * matches, axis=1) - 1
        slot_list.append(destination * per_device + micro_index * per_pair + arrival)
    send_slots = jnp.stack(slot_list)
    flat_slots = send_slots.reshape(-1)
    empty_rows = jnp.zeros((devices * per_device, width), jnp.bfloat16)
    sent_inputs = empty_rows.at[flat_slots].set(layer_input.reshape(-1, width))
    sent_grads = empty_rows.at[flat_slots].set(cotangent.reshape(-1, width))
    sent_offsets = (
        jnp.full((devices * per_device,), tok_rows, jnp.int32)
        .at[flat_slots]
        .set((target_slot % tok_rows).reshape(-1))
    )
    got_inputs, got_grads, got_offsets = (
        lax.all_to_all(sent_inputs, "seq", split_axis=0, concat_axis=0, tiled=True),
        lax.all_to_all(sent_grads, "seq", split_axis=0, concat_axis=0, tiled=True),
        lax.all_to_all(sent_offsets, "seq", split_axis=0, concat_axis=0, tiled=True),
    )

    def unpack(received, micro_index):
        shaped = received.reshape((devices, micro_count, per_pair) + received.shape[1:])
        return shaped[:, micro_index].reshape((devices * per_pair,) + received.shape[1:])

    def fetch():
        return (
            lax.all_gather(shards[0], "seq", axis=0, tiled=True),
            lax.all_gather(shards[1], "seq", axis=0, tiled=True),
            lax.all_gather(shards[2], "seq", axis=0, tiled=True),
            lax.all_gather(shards[3], "seq", axis=0, tiled=True),
            lax.all_gather(shards[4], "seq", axis=0, tiled=True),
            lax.all_gather(shards[5], "seq", axis=0, tiled=True),
            lax.all_gather(shards[6], "seq", axis=0, tiled=True),
            lax.all_gather(shards[7], "seq", axis=0, tiled=True),
            lax.all_gather(shards[8], "seq", axis=0, tiled=True),
            lax.all_gather(shards[9], "seq", axis=0, tiled=True),
            lax.all_gather(shards[10], "seq", axis=0, tiled=True),
        )

    results = []
    input_grads = []
    totals = None
    small_totals = None
    for micro_index in range(micro_count):
        places = unpack(got_offsets, micro_index)
        blank = jnp.zeros((tok_rows, width), jnp.bfloat16)
        layout_in = blank.at[places].set(unpack(got_inputs, micro_index), mode="drop")
        layout_grad = blank.at[places].set(unpack(got_grads, micro_index), mode="drop")
        positions = device * tok_rows + jnp.arange(tok_rows, dtype=jnp.int32)
        valid, boundary = layout_flags(seq_start[micro_index], seq_len[micro_index], positions)
        resets = boundary.reshape(-1, SPAN)[:, 0]
        wq, wk, wv, wr, wo, wgate, wup, wdown, wa, gain_one, gain_two = fetch()
        gain_one = gain_one.astype(jnp.float32)
        gain_two = gain_two.astype(jnp.float32)
        inputs = layout_in.astype(jnp.float32)
        scale_one = rms_scale(inputs)
        unit_one = inputs * scale_one
        normed = (unit_one * gain_one).astype(jnp.bfloat16)
        query_proj = project(normed, wq)
        key_proj = project(normed, wk)
        value_proj = project(normed, wv)
        gate_pre = project(normed, wr)
        rank_rows = project(normed, wa)
        logits = jnp.dot(rank_rows, rank_up, precision=highest) + bias_local
        decays = (jax.nn.log_sigmoid(logits) / 16.0).reshape(tok_rows, heads_here, HEAD_K)
        queries = (query_proj * query_scaling).reshape(tok_rows, heads_here, HEAD_K)
        key_rows = key_proj.reshape(tok_rows, heads_here, HEAD_K)
        value_rows = value_proj.reshape(tok_rows, heads_here, -1)
        zero_state = jnp.zeros((heads_here, HEAD_K, value_rows.shape[-1]), jnp.float32)
        mixed_local, leaving = run_local(queries, key_rows, value_rows, decays, resets, zero_state)
        opened = jnp.repeat((jnp.cumsum(resets) == 0).astype(jnp.float32), SPAN)
        lifting = jnp.exp(jnp.cumsum(decays, axis=0)) * opened[:, None, None]
        through = lifting[-1]
        _, entering = carried_in(
            (through, leaving),
            "seq",
            combine_affine,
            (jnp.ones_like(through), jnp.zeros_like(leaving)),
            False,
        )
        reach = queries * lifting
        mixed = mixed_local + jnp.einsum("thc,hcv->thv", reach, entering, precision=highest)
        scale_head, free_head = head_scale(mixed)
        unit_head = mixed * scale_head
        head_normed = (unit_head * head_gain).reshape(tok_rows, -1)
        gate_sig = jax.nn.sigmoid(gate_pre)
        gate_act = gate_pre * gate_sig
        gated = (head_normed * gate_act).astype(jnp.bfloat16)
        attended = lax.psum(project_back(gated, wo), "mp")
        hidden = inputs + attended
        scale_two = rms_scale(hidden)
        unit_two = hidden * scale_two
        normed_two = (unit_two * gain_two).astype(jnp.bfloat16)
        gating = project(normed_two, wgate)
        upward = project(normed_two, wup)
        up_sig = jax.nn.sigmoid(gating)
        gate_silu = gating * up_sig
        product = (gate_silu * upward).astype(jnp.bfloat16)
        ffn_out = lax.psum(project_back(product, wdown).astype(jnp.bfloat16), "mp").astype(
            jnp.float32
        )
        results.append(((hidden + ffn_out) * valid[:, None]).astype(jnp.bfloat16))
        wq, wk, wv, wr, wo, wgate, wup, wdown, wa, gain_one, gain_two = fetch()
        gain_one = gain_one.astype(jnp.float32)
        gain_two = gain_two.astype(jnp.float32)
        upstream = layout_grad.astype(jnp.float32) * valid[:, None]
        ffn_grad = upstream.astype(jnp.bfloat16)
        d_product = project(ffn_grad, wdown)
        grad_down = outer_sum(ffn_grad, product)
        d_gating = (d_product * upward * up_sig * (1.0 + gating * (1.0 - up_sig))).astype(
            jnp.bfloat16
        )
        d_upward = (d_product * gate_silu).astype(jnp.bfloat16)
        grad_gate = outer_sum(normed_two, d_gating)
        grad_up = outer_sum(normed_two, d_upward)
        second_part = project_back(d_gating, wgate) + project_back(d_upward, wup)
        d_normed_two = lax.psum(second_part, "mp")
        grad_gain_two = jnp.sum(d_normed_two * unit_two, axis=0)
        d_hidden = upstream + norm_back(d_normed_two * gain_two, unit_two, scale_two)
        attn_grad = d_hidden.astype(jnp.bfloat16)
        d_gated = project(attn_grad, wo)
        grad_out = outer_sum(attn_grad, gated)
        d_head = (d_gated * gate_act).reshape(tok_rows, heads_here, -1)
        d_gate_pre = (
            d_gated * head_normed * gate_sig * (1.0 + gate_pre * (1.0 - gate_sig))
        ).astype(jnp.bfloat16)
        grad_head_part = jnp.sum(d_head * unit_head, axis=(0, 1))
        scaled_head = d_head * head_gain
        d_mixed = scale_head * (
            scaled_head
            - free_head * unit_head * jnp.mean(scaled_head * unit_head, axis=-1, keepdims=True)
        )
        pulled = jnp.einsum("thc,thv->hcv", reach, d_mixed, precision=highest)
        _, later_grad = carried_in(
            (through, pulled),
            "seq",
            combine_affine,
            (jnp.ones_like(through), jnp.zeros_like(pulled)),
            True,
        )

        def local_pass(queries_in, keys_in, values_in, decays_in):
            return run_local(queries_in, keys_in, values_in, decays_in, resets, entering)

        _, pullback = jax.vjp(local_pass, queries, key_rows, value_rows, decays)
        d_queries, d_keys, d_values, d_decays = pullback((d_mixed, later_grad))
        query_grad = (d_queries * query_scaling).reshape(tok_rows, -1).astype(jnp.bfloat16)
        key_grad = d_keys.reshape(tok_rows, -1).astype(jnp.bfloat16)
        value_grad = d_values.reshape(tok_rows, -1).astype(jnp.bfloat16)
        d_logits = d_decays.reshape(tok_rows, -1) / 16.0 * jax.nn.sigmoid(-logits)
        grad_rank_up = lax.dot_general(rank_rows, d_logits, contract_rows, precision=highest)
        grad_bias = jnp.sum(d_logits, axis=0)
        rank_part = lax.dot_general(d_logits, rank_up, contract_last, precision=highest)
        first_part = (
            project_back(query_grad, wq)
            + project_back(key_grad, wk)
            + project_back(value_grad, wv)
            + project_back(d_gate_pre, wr)
        )
        d_normed, d_rank, grad_head = (
            lax.psum(first_part.astype(jnp.bfloat16), "mp").astype(jnp.float32),
            lax.psum(rank_part.astype(jnp.bfloat16), "mp").astype(jnp.float32),
            lax.psum(grad_head_part.astype(jnp.bfloat16), "mp").astype(jnp.float32),
        )
        rank_grad = d_rank.astype(jnp.bfloat16)
        d_normed = d_normed + project_back(rank_grad, wa)
        grad_gain_one = jnp.sum(d_normed * unit_one, axis=0)
        d_inputs = d_hidden + norm_back(d_normed * gain_one, unit_one, scale_one)
        input_grads.append(d_inputs.astype(jnp.bfloat16))
        batch_grads = (
            outer_sum(normed, query_grad),
            outer_sum(normed, key_grad),
            outer_sum(normed, value_grad),
            outer_sum(normed, d_gate_pre),
            grad_out,
            grad_gate,
            grad_up,
            grad_down,
            outer_sum(normed, rank_grad),
            grad_gain_one,
            grad_gain_two,
        )
        totals = batch_grads if totals is None else jax.tree.map(jnp.add, totals, batch_grads)
        small_batch = (grad_rank_up, grad_bias, grad_head)
        small_totals = (
            small_batch
            if small_totals is None
            else jax.tree.map(jnp.add, small_totals, small_batch)
        )
    totals = lax.psum_scatter(totals, "seq", scatter_dimension=0, tiled=True)
    back_outputs = []
    back_grads = []
    for micro_index in range(micro_count):
        places = unpack(got_offsets, micro_index)
        present = (places < tok_rows)[:, None]
        safe = jnp.minimum(places, tok_rows - 1)
        chosen_out = jnp.where(present, jnp.take(results[micro_index], safe, axis=0), 0)
        chosen_grad = jnp.where(present, jnp.take(input_grads[micro_index], safe, axis=0), 0)
        back_outputs.append(chosen_out.reshape(devices, per_pair, width))
        back_grads.append(chosen_grad.reshape(devices, per_pair, width))
    out_send = jnp.stack(back_outputs, axis=1).reshape(-1, width)
    grad_send = jnp.stack(back_grads, axis=1).reshape(-1, width)
    home_out, home_grad = (
        lax.all_to_all(out_send, "seq", split_axis=0, concat_axis=0, tiled=True),
        lax.all_to_all(grad_send, "seq", split_axis=0, concat_axis=0, tiled=True),
    )
    output = jnp.take(home_out, flat_slots, axis=0).reshape(micro_count, tok_rows, width)
    input_grad = jnp.take(home_grad, flat_slots, axis=0).reshape(micro_count, tok_rows, width)
    loss_part = jnp.zeros((), jnp.float32)
    for micro_index in range(micro_count):
        home_valid, _ = layout_flags(
            seq_start[micro_index], seq_len[micro_index], target_slot[micro_index]
        )
        difference = output[micro_index].astype(jnp.float32) - teacher[micro_index].astype(
            jnp.float32
        )
        loss_part = loss_part + jnp.sum(home_valid[:, None] * difference * difference)
    summed_rank_up, summed_bias, summed_head, summed_loss = lax.psum(
        (small_totals[0], small_totals[1], small_totals[2], loss_part), "seq"
    )
    count = jnp.sum(seq_len).astype(jnp.float32)
    loss = summed_loss / (count * width)
    return (
        output,
        loss,
        input_grad,
        totals[0],
        totals[1],
        totals[2],
        totals[3],
        totals[4],
        totals[5],
        totals[6],
        totals[7],
        totals[8],
        summed_rank_up,
        summed_bias,
        totals[9],
        totals[10],
        summed_head,
    )


def solution(mesh):
    placed = (
        P(None, "seq", None),
        P(None, "seq", None),
        P(None, "seq", None),
        P(None, "seq"),
        P(),
        P(),
        P("seq", "mp"),
        P("seq", "mp"),
        P("seq", "mp"),
        P("seq", "mp"),
        P("seq", "mp"),
        P("seq", "mp"),
        P("seq", "mp"),
        P("seq", "mp"),
        P("seq", None),
        P(None, "mp"),
        P("mp"),
        P("seq"),
        P("seq"),
        P(),
    )
    return jax.shard_map(
        local,
        mesh=mesh,
        in_specs=placed,
        out_specs=(
            P(None, "seq", None),
            P(),
            P(None, "seq", None),
            P("seq", "mp"),
            P("seq", "mp"),
            P("seq", "mp"),
            P("seq", "mp"),
            P("seq", "mp"),
            P("seq", "mp"),
            P("seq", "mp"),
            P("seq", "mp"),
            P("seq", None),
            P(None, "mp"),
            P("mp"),
            P("seq"),
            P("seq"),
            P(),
        ),
        check_vma=False,
    )
```

profile of v0, /device:TPU:0, one launch (start us, length us, event | category | flops | bytes accessed | tf_op | source)
XLA Modules:
  0.0 4428.2 jit_solution(14208158995080053299)
XLA Ops:
  40.7 117.7 %all-gather.4 = bf16[16,1,128]{2,1,0:T(2,128)(2,1)S(1)} all-gather(bf16[1,1,128]{2,1,0:T(2,128)(2,1)S(1)} %bitcast.1055), channel_id=1, replica_groups=mesh['seq'=16,'mp'=2] {'seq'}, dimensions={0}, use_global_device_ids=true | all-gather | bytes 4352 | tf_op jit(solution)/shard_map/all_gather | solution.py:192
  159.1 57.5 %all_gather.43 = bf16[2048,16]{0,1:T(8,128)(2,1)S(1)} all-gather(bf16[128,16]{0,1:T(8,128)(2,1)S(1)} %copy-done.146), channel_id=1, replica_groups=mesh['seq'=16,'mp'=2] {'seq'}, dimensions={0}, use_global_device_ids=true | all-gather | bytes 69632 | tf_op jit(solution)/shard_map/all_gather | solution.py:191
  245.4 28.9 all-gather.19.cloned.1.call-done
  280.6 35.7 while.200
  350.3 35.9 while.198
  395.9 39.7 all_gather.112
  442.8 37.2 all_gather.47
  482.5 26.4 all-gather.37.cloned.1.call-done
  508.9 23.1 while.201
  536.8 165.1 %all-gather.35.cloned.1.call-done = f32[32,256,512]{2,1,0:T(8,128)} async-done(((f32[2,256,512]{2,1,0:T(8,128)}), f32[32,256,512]{2,1,0:T(8,128)}) %all-gather.35.cloned.1.call-update) | async-done | bytes 16777232 | tf_op jit(solution)/shard_map/all_gather | solution.py:18
  701.9 23.0 while.199
  735.1 43.7 all-gather.25.cloned.1.call-done
  786.6 69.8 %all-gather.27.cloned.1.call-done = bf16[2048,1024]{1,0:T(8,128)(2,1)} async-done(((bf16[128,1024]{1,0:T(8,128)(2,1)}), bf16[2048,1024]{1,0:T(8,128)(2,1)}) %all-gather.27.cloned.1.call-update) | async-done | bytes 4194320 | tf_op jit(solution)/shard_map/all_gather | solution.py:187
  878.3 124.1 %all-gather.5 = bf16[16,1,128]{2,1,0:T(2,128)(2,1)S(1)} all-gather(bf16[1,1,128]{2,1,0:T(2,128)(2,1)S(1)} %bitcast.1056), channel_id=1, replica_groups=mesh['seq'=16,'mp'=2] {'seq'}, dimensions={0}, use_global_device_ids=true | all-gather | bytes 4352 | tf_op jit(solution)/shard_map/all_gather | solution.py:193
  1025.4 65.7 %all-gather.29.cloned.1.call-done = bf16[2048,2816]{1,0:T(8,128)(2,1)} async-done(((bf16[128,2816]{1,0:T(8,128)(2,1)}), bf16[2048,2816]{1,0:T(8,128)(2,1)}) %all-gather.29.cloned.1.call-update) | async-done | bytes 11534352 | tf_op jit(solution)/shard_map/all_gather | solution.py:188
  1100.1 134.3 %all-gather.31.cloned.1.call-done = bf16[2048,2816]{1,0:T(8,128)(2,1)} async-done(((bf16[128,2816]{1,0:T(8,128)(2,1)}), bf16[2048,2816]{1,0:T(8,128)(2,1)}) %all-gather.31.cloned.1.call-update) | async-done | bytes 11534352 | tf_op jit(solution)/shard_map/all_gather | solution.py:189
  1234.4 9.1 fusion.313
  1253.1 124.8 %all-gather.33.cloned.1.call-done = bf16[2048,2816]{1,0:T(8,128)(2,1)} async-done(((bf16[128,2816]{1,0:T(8,128)(2,1)}), bf16[2048,2816]{1,0:T(8,128)(2,1)}) %all-gather.33.cloned.1.call-update) | async-done | bytes 11534352 | tf_op jit(solution)/shard_map/all_gather | solution.py:190
  1377.9 10.8 multiply_convert_fusion
  1396.2 9.4 multiply_convert_fusion.2
  1430.5 26.7 all-reduce.13.cloned.1.call-done
  1497.2 38.7 while.194
  1549.6 41.2 while.196
  1620.0 61.7 %all-gather.39.cloned.1.call-done = f32[32,256,512]{2,1,0:T(8,128)} async-done(((f32[2,256,512]{2,1,0:T(8,128)}), f32[32,256,512]{2,1,0:T(8,128)}) %all-gather.39.cloned.1.call-update) | async-done | bytes 16777232 | tf_op jit(solution)/shard_map/all_gather | solution.py:18
  1681.7 11.8 rev.13
  1693.5 23.0 while.202
  1720.0 75.3 %while.195 = (s32[]{:T(128)}, f32[2,256,512]{2,1,0:T(8,128)S(1)}, f32[4,64,2,256]{3,2,1,0:T(2,128)}, bf16[4,64,2,256]{3,1,2,0:T(8,128)(2,1)}, bf16[4,64,2,512]{3...) while((s32[]{:T(128)}, f32[2,256,512]{2,1,0:T(8,128)S(1)}, ...), condition=%wide.region_68.71_spmd.clone, body=%wide.region_64.70_spmd.clone.sunk | while | flops 960380928 | bytes 40742804 | solution.py:85
  1795.4 78.8 %all-gather.41.cloned.1.call-done = f32[32,256,512]{2,1,0:T(8,128)} async-done(((f32[2,256,512]{2,1,0:T(8,128)}), f32[32,256,512]{2,1,0:T(8,128)}) %all-gather.41.cloned.1.call-update) | async-done | bytes 16777232 | tf_op jit(solution)/shard_map/all_gather | solution.py:18
  1874.2 11.6 rev.15
  1885.8 23.0 while.203
  1911.6 71.5 %while.197 = (s32[]{:T(128)}, f32[2,256,512]{2,1,0:T(8,128)S(1)}, f32[4,64,2,256]{3,2,1,0:T(2,128)}, bf16[4,64,2,256]{3,1,2,0:T(8,128)(2,1)S(1)}, bf16[4,64,2,51...) while((s32[]{:T(128)}, f32[2,256,512]{2,1,0:T(8,128)S(1)}, ...), condition=%wide.region_85.88_spmd.clone, body=%wide.region_81.87_spmd.clone.sunk | while | flops 960380928 | bytes 36581240 | solution.py:85
  2037.7 12.8 fusion.322
  2050.5 15.0 convolution_add_fusion.12
  2065.6 12.8 fusion.323
  2078.4 15.1 convolution_add_fusion.11
  2094.1 12.9 fusion.237
  2107.0 14.9 convolution_add_fusion.10
  2173.4 85.9 %all-to-all-done.2 = bf16[16,64,2048]{2,1,0:T(8,128)(2,1)} async-done(((bf16[16,64,2048]{2,1,0:T(8,128)(2,1)}), bf16[16,64,2048]{2,1,0:T(8,128)(2,1)}, u32[]{:S(2)}, u32[]{:S(2)}) %all-to-all-start.2) | async-done | bytes 4194336 | tf_op jit(solution)/shard_map/all_to_all | solution.py:360
  2259.4 48.1 %all-to-all-start.4 = ((bf16[16,64,2048]{2,1,0:T(8,128)(2,1)}), bf16[16,64,2048]{2,1,0:T(8,128)(2,1)}, u32[]{:S(2)}, u32[]{:S(2)}) async-start(bf16[16,64,2048]{2,1,0:T(8,128)(2,1)} %bitcast.953), calls=%async_computation.4 | async-start | bytes 8388608 | tf_op jit(solution)/shard_map/all_to_all | solution.py:361
  2318.2 84.0 %all-to-all-done.4 = bf16[16,64,2048]{2,1,0:T(8,128)(2,1)} async-done(((bf16[16,64,2048]{2,1,0:T(8,128)(2,1)}), bf16[16,64,2048]{2,1,0:T(8,128)(2,1)}, u32[]{:S(2)}, u32[]{:S(2)}) %all-to-all-start.4) | async-done | bytes 4194336 | tf_op jit(solution)/shard_map/all_to_all | solution.py:361
  2416.9 113.7 %all-reduce.4 = (f32[]{:T(128)}, f32[16,512]{1,0:T(8,128)}, f32[512]{0:T(512)}, f32[2048]{0:T(1024)S(1)}, f32[2048]{0:T(1024)S(1)}, /*index=5*/f32[512]{0:T(512)}) all-reduce(f32[]{:T(128)S(6)} %add.597, f32[16,512]{1,0:T(8,128)S(1)} %convolution_add_fusion.27, f32[512]{0:T(512)S(1)} %add.628, ...), channel_id=1, replica_groups=mesh['seq'=16,'mp'=2] {'seq'}, use_global_device_ids=true, to_apply=%region_52.55 | all-reduce | flops 13313 | bytes 106504 | tf_op jit(solution)/shard_map/psum | solution.py:374
  2532.4 67.6 %reduce-scatter.26.cloned.1.call-done = f32[128,16]{0,1:T(8,128)} async-done(((f32[2048,16]{0,1:T(8,128)}), f32[128,16]{0,1:T(8,128)}) %reduce-scatter.26.cloned.1.call-update) | async-done | bytes 8208 | tf_op jit(solution)/shard_map/reduce_scatter | solution.py:346
  2600.0 94.4 %reduce-scatter.12.cloned.1.call-done = f32[128,512]{1,0:T(8,128)} async-done(((f32[2048,512]{1,0:T(8,128)}), f32[128,512]{1,0:T(8,128)}) %reduce-scatter.12.cloned.1.call-update) | async-done | bytes 262160 | tf_op jit(solution)/shard_map/reduce_scatter | solution.py:346
  2694.4 97.4 %reduce-scatter.10.cloned.1.call-done = f32[128,512]{1,0:T(8,128)} async-done(((f32[2048,512]{1,0:T(8,128)}), f32[128,512]{1,0:T(8,128)}) %reduce-scatter.10.cloned.1.call-update) | async-done | bytes 262160 | tf_op jit(solution)/shard_map/reduce_scatter | solution.py:346
  2791.8 475.5 %reduce-scatter.20.cloned.1.call-done = f32[128,2816]{1,0:T(8,128)} async-done(((f32[2048,2816]{1,0:T(8,128)}), f32[128,2816]{1,0:T(8,128)}) %reduce-scatter.20.cloned.1.call-update) | async-done | bytes 1441808 | tf_op jit(solution)/shard_map/reduce_scatter | solution.py:346
  3267.4 482.7 %reduce-scatter.22.cloned.1.call-done = f32[128,2816]{1,0:T(8,128)} async-done(((f32[2048,2816]{1,0:T(8,128)}), f32[128,2816]{1,0:T(8,128)}) %reduce-scatter.22.cloned.1.call-update) | async-done | bytes 1441808 | tf_op jit(solution)/shard_map/reduce_scatter | solution.py:346
  3750.0 482.7 %reduce-scatter.24.cloned.1.call-done = f32[128,2816]{1,0:T(8,128)} async-done(((f32[2048,2816]{1,0:T(8,128)}), f32[128,2816]{1,0:T(8,128)}) %reduce-scatter.24.cloned.1.call-update) | async-done | bytes 1441808 | tf_op jit(solution)/shard_map/reduce_scatter | solution.py:346
  4232.7 187.4 %reduce-scatter.14.cloned.1.call-done = f32[128,1024]{1,0:T(8,128)} async-done(((f32[2048,1024]{1,0:T(8,128)}), f32[128,1024]{1,0:T(8,128)}) %reduce-scatter.14.cloned.1.call-update) | async-done | bytes 524304 | tf_op jit(solution)/shard_map/reduce_scatter | solution.py:346
  (1232 shorter events, 840.2 us)
Async XLA Ops:
  7.2 223.0 %copy-start = (bf16[16,512]{1,0:T(8,128)(2,1)S(1)}, bf16[16,512]{1,0:T(8,128)(2,1)}, u32[]{:S(2)}) copy-start(bf16[16,512]{1,0:T(8,128)(2,1)} %param.59) | copy-start | bytes 49156
  7.2 225.7 %all-gather.23.cloned.1.call-start = ((), (), s32[]{:S(2)}) async-start(), calls=%async_computation.16 | async-start | bytes 2228224 | tf_op jit(solution)/shard_map/all_gather | solution.py:183
  7.9 228.5 %all-gather.21.cloned.1.call-start = ((), (), s32[]{:S(2)}) async-start(), calls=%async_computation.15 | async-start | bytes 4456448 | tf_op jit(solution)/shard_map/all_gather | solution.py:185
  17.1 15.6 all-to-all-start
  32.7 125.6 %copy-start.160 = (bf16[512]{0:T(512)(128)(2,1)S(1)}, bf16[512]{0:T(512)(128)(2,1)}, u32[]{:S(2)}) copy-start(bf16[512]{0:T(512)(128)(2,1)} %param.60) | copy-start | bytes 3076
  32.7 125.7 %copy-start.161 = (s32[2,2]{1,0:T(2,128)S(1)}, s32[2,2]{1,0:T(2,128)}, u32[]{:S(2)}) copy-start(s32[2,2]{1,0:T(2,128)} %param.48) | copy-start | bytes 52
  32.7 126.4 %copy-start.146 = (bf16[128,16]{0,1:T(8,128)(2,1)S(1)}, bf16[128,16]{0,1:T(8,128)(2,1)}, u32[]{:S(2)}) copy-start(bf16[128,16]{0,1:T(8,128)(2,1)} %param.58) | copy-start | bytes 12292
  32.7 186.6 %all-to-all-start.1 = ((bf16[16,64,2048]{2,1,0:T(8,128)(2,1)}), bf16[16,64,2048]{2,1,0:T(8,128)(2,1)}, u32[]{:S(2)}, u32[]{:S(2)}) async-start(bf16[16,64,2048]{2,1,0:T(8,128)(2,1)} %bitcast.954), calls=%async_computation.1 | async-start | bytes 8388608 | tf_op jit(solution)/shard_map/all_to_all | solution.py:172
  39.8 234.4 %all-gather.19.cloned.1.call-start = ((), (), s32[]{:S(2)}) async-start(), calls=%async_computation.14 | async-start | bytes 2228224 | tf_op jit(solution)/shard_map/all_gather | solution.py:184
  40.6 468.3 %all-gather.37.cloned.1.call-start = ((), (), s32[]{:S(2)}) async-start(), calls=%async_computation.32 | async-start | bytes 17825792 | tf_op jit(solution)/shard_map/all_gather | solution.py:18
  158.3 115.9 %copy-start.64 = (f32[16,1,128]{2,1,0:T(1,128)}, f32[16,1,128]{2,1,0:T(1,128)S(1)}, u32[]{:S(2)}) copy-start(f32[16,1,128]{2,1,0:T(1,128)S(1)} %convert_element_type.414) | copy-start | bytes 24580
  158.4 71.9 %copy-start.155 = (f32[512]{0:T(512)}, f32[512]{0:T(512)S(1)}, u32[]{:S(2)}) copy-start(f32[512]{0:T(512)S(1)} %convert_element_type.333) | copy-start | bytes 6148
  159.1 58.6 %copy-start.166 = (pred[4,64]{1,0:T(4,128)(4,1)}, pred[4,64]{1,0:T(4,128)(4,1)S(1)}, u32[]{:S(2)}) copy-start(pred[4,64]{1,0:T(4,128)(4,1)S(1)} %convert_element_type.349) | copy-start | bytes 772
  229.4 790.7 %copy-start.8 = (bf16[256,2048]{1,0:T(8,128)(2,1)}, bf16[256,2048]{1,0:T(8,128)(2,1)S(1)}, u32[]{:S(2)}) copy-start(bf16[256,2048]{1,0:T(8,128)(2,1)S(1)} %scatter_custom_fusion.3) | copy-start | bytes 3145732
  317.4 384.5 %all-gather.35.cloned.1.call-start = ((), (), s32[]{:S(2)}) async-start(), calls=%async_computation.31 | async-start | bytes 17825792 | tf_op jit(solution)/shard_map/all_gather | solution.py:18
  387.2 391.6 %all-gather.25.cloned.1.call-start = ((), (), s32[]{:S(2)}) async-start(), calls=%async_computation.17 | async-start | bytes 4456448 | tf_op jit(solution)/shard_map/all_gather | solution.py:186
  387.8 468.6 %all-gather.27.cloned.1.call-start = ((), (), s32[]{:S(2)}) async-start(), calls=%async_computation.18 | async-start | bytes 4456448 | tf_op jit(solution)/shard_map/all_gather | solution.py:187
  388.5 631.6 %all-reduce.15.cloned.1.call-start = ((), (), s32[]{:S(2)}) async-start(), calls=%async_computation.36 | async-start | bytes 8388608 | tf_op jit(solution)/shard_map/psum | solution.py:245
  864.1 227.0 %all-gather.29.cloned.1.call-start = ((), (), s32[]{:S(2)}) async-start(), calls=%async_computation.19 | async-start | bytes 12255232 | tf_op jit(solution)/shard_map/all_gather | solution.py:188
  864.8 369.6 %all-gather.31.cloned.1.call-start = ((), (), s32[]{:S(2)}) async-start(), calls=%async_computation.20 | async-start | bytes 12255232 | tf_op jit(solution)/shard_map/all_gather | solution.py:189
  865.4 512.5 %all-gather.33.cloned.1.call-start = ((), (), s32[]{:S(2)}) async-start(), calls=%async_computation.21 | async-start | bytes 12255232 | tf_op jit(solution)/shard_map/all_gather | solution.py:190
  873.5 128.9 %copy-start.126 = (s32[1,256]{1,0:T(1,128)S(1)}, s32[1,256]{1,0:T(1,128)}, u32[]{:S(2)}) copy-start(s32[1,256]{1,0:T(1,128)} %copy-done.125) | copy-start | bytes 3076
  873.5 128.9 %copy-start.129 = (s32[1,256]{1,0:T(1,128)S(1)}, s32[1,256]{1,0:T(1,128)}, u32[]{:S(2)}) copy-start(s32[1,256]{1,0:T(1,128)} %copy-done.128) | copy-start | bytes 3076
  873.5 128.9 %copy-start.140 = (s32[2]{0:T(128)S(1)}, s32[2]{0:T(128)}, u32[]{:S(2)}) copy-start(s32[2]{0:T(128)} %copy-done.139) | copy-start | bytes 28
  873.5 128.9 %copy-start.142 = (s32[2]{0:T(128)S(1)}, s32[2]{0:T(128)}, u32[]{:S(2)}) copy-start(s32[2]{0:T(128)} %copy-done.141) | copy-start | bytes 28
  873.5 128.9 %copy-start.154 = (s32[256]{0:T(256)S(1)}, s32[256]{0:T(256)}, u32[]{:S(2)}) copy-start(s32[256]{0:T(256)} %copy-done.153) | copy-start | bytes 3076
  873.5 129.1 %copy-start.147 = (s32[2,2]{1,0:T(2,128)S(1)}, s32[2,2]{1,0:T(2,128)}, u32[]{:S(2)}) copy-start(s32[2,2]{1,0:T(2,128)} %param.49) | copy-start | bytes 52
  873.5 130.4 %all-to-all-start.3 = ((bf16[16,64,2048]{2,1,0:T(8,128)(2,1)}), bf16[16,64,2048]{2,1,0:T(8,128)(2,1)}, u32[]{:S(2)}, u32[]{:S(2)}) async-start(bf16[16,64,2048]{2,1,0:T(8,128)(2,1)} %bitcast.955), calls=%async_computation.3 | async-start | bytes 8388608 | tf_op jit(solution)/shard_map/all_to_all | solution.py:173
  878.2 579.0 %all-reduce.13.cloned.1.call-start = ((), (), s32[]{:S(2)}) async-start(), calls=%async_computation.35 | async-start | bytes 8388608 | tf_op jit(solution)/shard_map/psum | solution.py:273
  1003.9 456.8 %copy-start.123 = (f32[256]{0:T(256)}, f32[256]{0:T(256)S(1)}, u32[]{:S(2)}) copy-start(f32[256]{0:T(256)S(1)} %compare_convert_fusion.8) | copy-start | bytes 3076
  1003.9 466.5 %copy-start.117 = (f32[256]{0:T(256)}, f32[256]{0:T(256)S(1)}, u32[]{:S(2)}) copy-start(f32[256]{0:T(256)S(1)} %compare_convert_fusion.9) | copy-start | bytes 3076
  1025.4 209.0 %copy-start.28 = (bf16[256,2048]{1,0:T(8,128)(2,1)}, bf16[256,2048]{1,0:T(8,128)(2,1)S(1)}, u32[]{:S(2)}) copy-start(bf16[256,2048]{1,0:T(8,128)(2,1)S(1)} %get-tuple-element.2748) | copy-start | bytes 3145732
  1025.4 222.9 %copy-start.38 = (bf16[256,2048]{1,0:T(8,128)(2,1)}, bf16[256,2048]{1,0:T(8,128)(2,1)S(1)}, u32[]{:S(2)}) copy-start(bf16[256,2048]{1,0:T(8,128)(2,1)S(1)} %get-tuple-element.2747) | copy-start | bytes 3145732
  1248.3 129.6 %copy-start.39 = (bf16[256,2048]{1,0:T(8,128)(2,1)S(1)}, bf16[256,2048]{1,0:T(8,128)(2,1)}, u32[]{:S(2)}) copy-start(bf16[256,2048]{1,0:T(8,128)(2,1)} %scatter_custom_fusion.6) | copy-start | bytes 3145732
  1430.3 251.4 %all-gather.39.cloned.1.call-start = ((), (), s32[]{:S(2)}) async-start(), calls=%async_computation.33 | async-start | bytes 17825792 | tf_op jit(solution)/shard_map/all_gather | solution.py:18
  1488.8 385.4 %all-gather.41.cloned.1.call-start = ((), (), s32[]{:S(2)}) async-start(), calls=%async_computation.34 | async-start | bytes 17825792 | tf_op jit(solution)/shard_map/all_gather | solution.py:18
  1540.3 589.0 %all-reduce.17.cloned.1.call-start = ((), (), s32[]{:S(2)}) async-start(), calls=%async_computation.37 | async-start | bytes 8388608 | tf_op jit(solution)/shard_map/psum | solution.py:255
  1997.5 534.9 %reduce-scatter.18.cloned.1.call-start = ((), (), s32[]{:S(2)}) async-start(), calls=%async_computation.26 | async-start | bytes 8912896 | tf_op jit(solution)/shard_map/reduce_scatter | solution.py:346
  2007.0 525.4 %reduce-scatter.16.cloned.1.call-start = ((), (), s32[]{:S(2)}) async-start(), calls=%async_computation.25 | async-start | bytes 8912896 | tf_op jit(solution)/shard_map/reduce_scatter | solution.py:346
  2015.6 584.4 %reduce-scatter.26.cloned.1.call-start = ((), (), s32[]{:S(2)}) async-start(), calls=%async_computation.30 | async-start | bytes 139264 | tf_op jit(solution)/shard_map/reduce_scatter | solution.py:346
  2028.4 666.0 %reduce-scatter.12.cloned.1.call-start = ((), (), s32[]{:S(2)}) async-start(), calls=%async_computation.23 | async-start | bytes 4456448 | tf_op jit(solution)/shard_map/reduce_scatter | solution.py:346
  2033.6 758.3 %reduce-scatter.10.cloned.1.call-start = ((), (), s32[]{:S(2)}) async-start(), calls=%async_computation.22 | async-start | bytes 4456448 | tf_op jit(solution)/shard_map/reduce_scatter | solution.py:346
  2037.5 1229.9 %reduce-scatter.20.cloned.1.call-start = ((), (), s32[]{:S(2)}) async-start(), calls=%async_computation.27 | async-start | bytes 24510464 | tf_op jit(solution)/shard_map/reduce_scatter | solution.py:346
  2065.5 1684.5 %reduce-scatter.22.cloned.1.call-start = ((), (), s32[]{:S(2)}) async-start(), calls=%async_computation.28 | async-start | bytes 24510464 | tf_op jit(solution)/shard_map/reduce_scatter | solution.py:346
  2093.5 2139.2 %reduce-scatter.24.cloned.1.call-start = ((), (), s32[]{:S(2)}) async-start(), calls=%async_computation.29 | async-start | bytes 24510464 | tf_op jit(solution)/shard_map/reduce_scatter | solution.py:346
  2121.9 2298.2 %reduce-scatter.14.cloned.1.call-start = ((), (), s32[]{:S(2)}) async-start(), calls=%async_computation.24 | async-start | bytes 8912896 | tf_op jit(solution)/shard_map/reduce_scatter | solution.py:346
  2164.6 94.7 %all-to-all-start.2 = ((bf16[16,64,2048]{2,1,0:T(8,128)(2,1)}), bf16[16,64,2048]{2,1,0:T(8,128)(2,1)}, u32[]{:S(2)}, u32[]{:S(2)}) async-start(bf16[16,64,2048]{2,1,0:T(8,128)(2,1)} %bitcast.956), calls=%async_computation.2 | async-start | bytes 8388608 | tf_op jit(solution)/shard_map/all_to_all | solution.py:360
  2259.4 142.8 %all-to-all-start.4 = ((bf16[16,64,2048]{2,1,0:T(8,128)(2,1)}), bf16[16,64,2048]{2,1,0:T(8,128)(2,1)}, u32[]{:S(2)}, u32[]{:S(2)}) async-start(bf16[16,64,2048]{2,1,0:T(8,128)(2,1)} %bitcast.953), calls=%async_computation.4 | async-start | bytes 8388608 | tf_op jit(solution)/shard_map/all_to_all | solution.py:361
  (185 other events, 2061.6 us)
Sparse Core Ops, SparseCore 0:
  10.8 111.6 all-gather.22
  125.3 86.8 all-gather.20
  214.9 59.2 all-gather.18
  317.5 191.3 all-gather.36
  512.1 189.7 all-gather.34
  704.5 74.2 all-gather.24
  781.6 74.6 all-gather.26
  864.2 27.1 all-reduce.14
  894.5 196.5 all-gather.28
  1094.1 140.2 all-gather.30
  1237.5 140.3 all-gather.32
  1430.4 26.7 all-reduce.12
  1488.9 192.7 all-gather.38
  1684.3 189.7 all-gather.40
  1997.6 26.9 all-reduce.16
  2027.4 218.3 reduce-scatter.17
  2248.6 263.1 reduce-scatter.15
  2514.6 85.4 reduce-scatter.25
  2602.9 91.4 reduce-scatter.11
  2697.1 94.6 reduce-scatter.9
  2794.7 472.5 reduce-scatter.19
  3270.2 479.7 reduce-scatter.21
  3752.9 479.7 reduce-scatter.23
  4235.4 184.5 reduce-scatter.13
where the time goes:
time: 4450 us; the launch traced here: 4430 us
  waiting for transfers between devices  2890 us (65%)
  blocking collectives  494 us (11%)
  matrix products  425 us (10%)
  local copies, waits for them, and re-layouts  283 us (6%)
  other arithmetic  232 us (5%)
  starting transfers between devices  75.9 us (2%)
    reduce_scatter x9, waiting for transfers between devices, local(): totals = lax.psum_scatter(totals, 'seq', scatter_dimension=0, tiled=True)  1890 us
    all_gather x4, waiting for transfers between devices, carried_in(): pieces = jax.tree.map(lambda part: lax.all_gather(part, axis), value)  332 us
    all_gather x1, waiting for transfers between devices, fetch(): lax.all_gather(shards[6], 'seq', axis=0, tiled=True)  134 us
    all_gather x1, waiting for transfers between devices, fetch(): lax.all_gather(shards[7], 'seq', axis=0, tiled=True)  125 us
    all_gather x1, blocking collectives, fetch(): lax.all_gather(shards[10], 'seq', axis=0, tiled=True)  124 us
    dot_general x18, matrix products, outer_sum(): lax.dot_general(left, right, contract_rows, preferred_element_type=jnp.fl...  118 us
    all_gather x1, blocking collectives, fetch(): lax.all_gather(shards[9], 'seq', axis=0, tiled=True)  118 us
    psum x1, blocking collectives, local(): lax.psum((small_totals[0], small_totals[1], small_totals[2], loss_part),...  114 us
  transfers between devices with their start and end apart: 29, of which 20 were waited for; matrix products, arithmetic and copies ran while one was open for 15% of the time, Pallas kernels for 0%

commit v1 on v0

v1 whole, which is shorter than its diff:
```python
import functools

import jax
import jax.numpy as jnp
from jax import lax
from jax.experimental import pallas as pl
from jax.experimental.pallas import tpu as pltpu
from jax.sharding import Mesh
from jax.sharding import PartitionSpec as P

SPAN = 64
HEAD_K = 256
HEAD_V = 512
GROUP = 4
LANES = 128

eps = 1e-06
highest = lax.Precision.HIGHEST
contract_last = (((1,), (1,)), ((), ()))
contract_rows = (((0,), (0,)), ((), ()))
bf16 = jnp.bfloat16
f32 = jnp.float32


def rms_scale(values):
    return lax.rsqrt(jnp.mean(values * values, axis=-1, keepdims=True) + eps)


def layout_valid(starts, lengths, positions):
    begun = (positions[:, None] >= starts[None, :]).astype(jnp.int32)
    owner = jnp.sum(begun, axis=1) - 1
    ids = jnp.arange(starts.shape[0], dtype=jnp.int32)
    picked = (owner[:, None] == ids[None, :]).astype(jnp.int32)
    own_start = jnp.sum(picked * starts[None, :], axis=1)
    own_length = jnp.sum(picked * lengths[None, :], axis=1)
    return (positions - own_start < own_length).astype(f32)


def project(left, right):
    return jnp.dot(left, right, preferred_element_type=f32)


def project_back(left, right):
    return lax.dot_general(left, right, contract_last, preferred_element_type=f32)


def outer_sum(left, right):
    return lax.dot_general(left, right, contract_rows, preferred_element_type=f32)


def norm_back(grad_unit, unit, scaling):
    return scaling * (grad_unit - unit * jnp.mean(grad_unit * unit, axis=-1, keepdims=True))


def exact(left, right, dims):
    return lax.dot_general(left, right, dims, precision=highest, preferred_element_type=f32)


plain = (((1,), (0,)), ((), ()))


def triangle(upper):
    row = lax.broadcasted_iota(jnp.int32, (SPAN, SPAN), 0)
    col = lax.broadcasted_iota(jnp.int32, (SPAN, SPAN), 1)
    return jnp.where(col >= row if upper else row >= col, 1.0, 0.0).astype(f32)


def kept(resets, block):
    return jnp.where(resets[block] == 1, 0.0, 1.0)


def states_kernel(order, resets, key_ref, value_ref, decay_ref, cumul_ref, left_ref, state, through):
    block = pl.program_id(0)

    @pl.when(block == 0)
    def _():
        state[...] = jnp.zeros_like(state)
        through[...] = jnp.ones_like(through)

    cumul = exact(triangle(False), decay_ref[...], plain)
    cumul_ref[...] = cumul
    last = cumul[SPAN - 1 : SPAN, :]
    faded = key_ref[...] * jnp.exp(last - cumul)
    fade = jnp.exp(last) * kept(resets, block)
    state[...] = state[...] * fade + exact(value_ref[...], faded, contract_rows)
    through[...] = through[...] * fade

    @pl.when(block == pl.num_programs(0) - 1)
    def _():
        left_ref[:HEAD_V, :] = state[...]
        left_ref[HEAD_V:, :] = through[...]


def mix_kernel(
    order, resets, query_ref, key_ref, value_ref, gate_ref, cumul_ref, gain_ref, enter_ref,
    gated_ref, mixed_ref, saved_ref, state,
):
    block = pl.program_id(0)

    @pl.when(block == 0)
    def _():
        state[...] = enter_ref[...]

    cumul = cumul_ref[...]
    last = cumul[SPAN - 1 : SPAN, :]
    key_rows = key_ref[...]
    value_rows = value_ref[...]
    lifted = query_ref[...] * (HEAD_K ** (-0.5)) * jnp.exp(cumul)
    lowered = key_rows * jnp.exp(-cumul)
    before = state[...] * kept(resets, block)
    saved_ref[0] = before
    scores = exact(lifted, lowered, contract_last) * triangle(False)
    mixed = exact(scores, value_rows, plain) + exact(lifted, before, contract_last)
    mixed_ref[...] = mixed
    faded = key_rows * jnp.exp(last - cumul)
    state[...] = before * jnp.exp(last) + exact(value_rows, faded, contract_rows)
    square = jnp.mean(mixed * mixed, axis=-1, keepdims=True)
    unit = mixed * lax.rsqrt(jnp.maximum(square, 1.0))
    gate = gate_ref[...]
    gated_ref[...] = (unit * gain_ref[...] * (gate * jax.nn.sigmoid(gate))).astype(bf16)


def pull_kernel(
    order, resets, query_ref, gate_ref, cumul_ref, mixed_ref, grad_ref, gain_ref,
    d_mixed_ref, d_gate_ref, head_ref, pulled_ref, through,
):
    block = pl.program_id(0)

    @pl.when(block == 0)
    def _():
        through[...] = jnp.ones_like(through)
        pulled_ref[...] = jnp.zeros_like(pulled_ref)
        head_ref[...] = jnp.zeros_like(head_ref)

    cumul = cumul_ref[...]
    mixed = mixed_ref[...]
    gate = gate_ref[...]
    grad = grad_ref[...]
    gain = gain_ref[...]
    square = jnp.mean(mixed * mixed, axis=-1, keepdims=True)
    scale = lax.rsqrt(jnp.maximum(square, 1.0))
    free = jnp.where(square > 1.0, 1.0, 0.0)
    unit = mixed * scale
    sig = jax.nn.sigmoid(gate)
    d_head = grad * (gate * sig)
    d_gate_ref[...] = (grad * (unit * gain) * sig * (1.0 + gate * (1.0 - sig))).astype(bf16)
    head_ref[...] += jnp.sum((d_head * unit).reshape(SPAN // 8, 8, HEAD_V), axis=0)
    scaled = d_head * gain
    d_mixed = scale * (scaled - free * unit * jnp.mean(scaled * unit, axis=-1, keepdims=True))
    d_mixed_ref[...] = d_mixed
    opened = through[...] * kept(resets, block)
    lifted = query_ref[...] * (HEAD_K ** (-0.5)) * jnp.exp(cumul)
    pulled_ref[...] += exact(d_mixed, lifted * opened[:1, :], contract_rows)
    through[...] = opened * jnp.exp(cumul[SPAN - 1 : SPAN, :])


def back_kernel(
    order, resets, query_ref, key_ref, value_ref, cumul_ref, saved_ref, d_mixed_ref, d_gate_ref, later_ref,
    grads_ref, d_decay_ref, state,
):
    step = pl.program_id(0)
    block = pl.num_programs(0) - 1 - step

    @pl.when(step == 0)
    def _():
        state[...] = later_ref[...]

    cumul = cumul_ref[...]
    last = cumul[SPAN - 1 : SPAN, :]
    key_rows = key_ref[...]
    value_rows = value_ref[...]
    d_mixed = d_mixed_ref[...]
    before = saved_ref[0]
    d_after = state[...]
    up = jnp.exp(cumul)
    down = jnp.exp(-cumul)
    rest = jnp.exp(last - cumul)
    lifted = query_ref[...] * (HEAD_K ** (-0.5)) * up
    lowered = key_rows * down
    faded = key_rows * rest
    causal = triangle(False)
    scores = exact(lifted, lowered, contract_last) * causal
    d_scores = exact(d_mixed, value_rows, contract_last) * causal
    d_value = exact(scores, d_mixed, contract_rows) + exact(faded, d_after, contract_last)
    d_lifted = exact(d_scores, lowered, plain) + exact(d_mixed, before, plain)
    d_lowered = exact(d_scores, lifted, contract_rows)
    d_faded = exact(value_rows, d_after, plain)
    leak = d_faded * faded
    d_cumul = d_lifted * lifted - d_lowered * lowered - leak
    d_last = jnp.sum(leak, axis=0, keepdims=True) + jnp.exp(last) * jnp.sum(
        before * d_after, axis=0, keepdims=True
    )
    d_decay_ref[...] = exact(triangle(True), d_cumul, plain) + d_last
    grads_ref[:, :HEAD_K] = (d_lifted * up * (HEAD_K ** (-0.5))).astype(bf16)
    grads_ref[:, HEAD_K : 2 * HEAD_K] = (d_lowered * down + d_faded * rest).astype(bf16)
    grads_ref[:, 2 * HEAD_K : 2 * HEAD_K + HEAD_V] = d_value.astype(bf16)
    grads_ref[:, 2 * HEAD_K + HEAD_V :] = d_gate_ref[...]
    d_before = exact(d_mixed, lifted, contract_rows) + d_after * jnp.exp(last)
    state[...] = d_before * kept(resets, block)


def rows_of(width, column=0, backward=False):
    def place(step, order, resets):
        at = order.shape[0] - 1 - step if backward else step
        return (order[at], column)

    return pl.BlockSpec((SPAN, width), place)


def saved_of(backward=False):
    def place(step, order, resets):
        at = order.shape[0] - 1 - step if backward else step
        return (order[at], 0, 0)

    return pl.BlockSpec((1, HEAD_V, HEAD_K), place)


def whole_of(shape):
    return pl.BlockSpec(shape, lambda step, order, resets: (0,) * len(shape))


def over_blocks(kernel, order, resets, operands, in_specs, outs, out_specs, scratch, flops, moved):
    return pl.pallas_call(
        kernel,
        out_shape=outs,
        grid_spec=pltpu.PrefetchScalarGridSpec(
            num_scalar_prefetch=2,
            grid=(order.shape[0],),
            in_specs=in_specs,
            out_specs=out_specs,
            scratch_shapes=scratch,
        ),
        compiler_params=pltpu.CompilerParams(
            dimension_semantics=("arbitrary",), vmem_limit_bytes=40 << 20
        ),
        cost_estimate=pl.CostEstimate(flops=flops, bytes_accessed=moved, transcendentals=0),
    )(order, resets, *operands)


def shape_of(shape, dtype=f32):
    return jax.ShapeDtypeStruct(shape, dtype)


def swapped(value):
    return lax.ppermute(value, "c", [(0, 1), (1, 0)])


def neighbour(value, distance):
    return lax.ppermute(value, "t", [(i, i ^ distance) for i in range(GROUP)])


def plane_gather(value):
    arrived = [neighbour(value, distance) for distance in (3, 1, 2)]
    return jnp.concatenate([value, arrived[1], arrived[2], arrived[0]], axis=0)


def plane_sum(produce):
    arrived = [neighbour(produce(distance).astype(bf16), distance) for distance in (3, 1, 2)]
    total = produce(0)
    for part in arrived:
        total = total + part.astype(f32)
    return total


def deal_pairs(turn):
    pairs = []
    for t in range(GROUP):
        for c in range(2):
            pairs.append((t * 2 + c, (2 * c + (t + turn) % 2) * 2 + t // 2))
    return pairs


def local(
    layer_input, cotangent, teacher, target_slot, seq_start, seq_len,
    w_query, w_key, w_value, w_gate_out, w_out, w_ffn_gate, w_ffn_up, w_ffn_down,
    w_rank_down, w_rank_up, decay_bias, gain_attn, gain_ffn, gain_head,
):
    planes = lax.axis_size("o")
    devices = planes * GROUP
    o, t, c = (lax.axis_index("o"), lax.axis_index("t"), lax.axis_index("c"))
    even = t % 2 == 0
    _, rows, width = layer_input.shape
    shard = w_query.shape[0]
    rank = w_rank_down.shape[1]
    hidden_here = w_ffn_gate.shape[1] // 2
    tokens = GROUP * rows
    blocks = tokens // SPAN
    pair = 2 * rows // devices
    half = width // 2

    def mine(value):
        return lax.dynamic_index_in_dim(value, c, 0, keepdims=False)

    def arranged(value):
        shaped = value.reshape(value.shape[0], planes, 2, 2 * shard)
        return shaped.transpose(0, 2, 1, 3).reshape(value.shape)

    def restored(value):
        shaped = value.reshape(value.shape[0], 2, planes, 2 * shard)
        return shaped.transpose(0, 2, 1, 3).reshape(value.shape)

    def either(first, second):
        return (jnp.where(even, first, second), jnp.where(even, second, first))

    def fetch(first, second):
        sent = either(first, second)
        got = [lax.ppermute(sent[turn], ("t", "c"), deal_pairs(turn)) for turn in range(2)]
        return lax.all_gather(jnp.concatenate(either(*got), axis=0), ("c", "o"), axis=0, tiled=True)

    def deliver(left, right):
        theirs = lax.dynamic_slice_in_dim(left, (1 - c) * half, half, 1)
        ours = lax.dynamic_slice_in_dim(left, c * half, half, 1)
        arrived = swapped(outer_sum(theirs, right).astype(bf16))
        total = (outer_sum(ours, right) + arrived.astype(f32)).astype(bf16)
        part = lax.psum_scatter(total, "o", scatter_dimension=0, tiled=True)
        sent = either(part[:shard], part[shard:])
        got = [lax.ppermute(sent[turn], ("t", "c"), deal_pairs(turn)) for turn in range(2)]
        return [piece.astype(f32) for piece in either(*got)]

    targets = mine(target_slot)
    destination = targets // rows
    offset = targets % rows
    ids = jnp.arange(devices, dtype=jnp.int32)
    matches = (destination[:, None] == ids[None, :]).astype(bf16)
    index = jnp.arange(rows, dtype=jnp.int32)
    earlier = (index[:, None] > index[None, :]).astype(bf16)
    arrival = jnp.sum(project(earlier, matches) * matches.astype(f32), axis=1).astype(jnp.int32)
    slot = destination * pair + arrival
    pack = (jnp.arange(devices * pair, dtype=jnp.int32)[:, None] == slot[None, :]).astype(bf16)

    def exchange(value):
        return lax.all_to_all(value, ("o", "t"), split_axis=0, concat_axis=0, tiled=True)

    tag = jnp.pad((offset + 1).astype(bf16)[:, None], ((0, 0), (0, LANES - 1)))
    home_in = jnp.concatenate([arranged(mine(layer_input)), tag], axis=1)
    got_in = exchange(project(pack, home_in).astype(bf16))
    got_tag = got_in[:, width].astype(jnp.int32) - 1
    unpack = (got_tag[:, None] == index[None, :]).astype(bf16)
    layout_in = outer_sum(unpack, got_in[:, :width]).astype(bf16)
    got_grad = exchange(project(pack, arranged(mine(cotangent))).astype(bf16))
    layout_grad = outer_sum(unpack, got_grad).astype(bf16)

    def slice_of(weight, which):
        wide = weight.shape[1] // 2
        return weight[:, which * wide : (which + 1) * wide]

    extras = jnp.concatenate(
        [
            w_rank_down,
            gain_attn[:, None],
            gain_ffn[:, None],
            jnp.zeros((shard, LANES - rank - 2), bf16),
        ],
        axis=1,
    )
    first_pieces = [
        jnp.concatenate(
            [slice_of(w, which) for w in (w_query, w_key, w_value, w_gate_out)] + [extras], axis=1
        )
        for which in range(2)
    ]
    wide_first = first_pieces[0].shape[1] - LANES
    w_first = fetch(*first_pieces)
    wo = fetch(slice_of(w_out, 0), slice_of(w_out, 1))
    w_gate_up = fetch(
        *[
            jnp.concatenate([slice_of(w_ffn_gate, which), slice_of(w_ffn_up, which)], axis=1)
            for which in range(2)
        ]
    )
    w_down = fetch(slice_of(w_ffn_down, 0), slice_of(w_ffn_down, 1))
    rank_down = w_first[:, wide_first : wide_first + rank]
    gain_one = w_first[:, wide_first + rank].astype(f32)
    gain_two = w_first[:, wide_first + rank + 1].astype(f32)
    ranked = jnp.concatenate([w_rank_up, decay_bias[None, :]], axis=0)
    other_ranked = swapped(ranked)
    ranked = jnp.where(t // 2 == c, ranked, other_ranked).astype(f32)
    ranked = jnp.where(even, ranked[:, :HEAD_K], ranked[:, HEAD_K:])
    rank_up, bias = (ranked[:rank], ranked[rank])
    head_gain = gain_head.astype(f32)[None, :]

    starts, lengths = (mine(seq_start), mine(seq_len))
    own_positions = (o * GROUP + t) * rows + index
    own_valid = layout_valid(starts, lengths, own_positions)[:, None]
    block_ids = jnp.arange(blocks, dtype=jnp.int32)
    block_first = o * tokens + block_ids * SPAN
    resets = jnp.any(block_first[:, None] == starts[None, :], axis=1).astype(jnp.int32)
    per_member = rows // SPAN
    order = ((block_ids // per_member) ^ t) * per_member + block_ids % per_member

    inputs = layout_in.astype(f32)
    scale_one = rms_scale(inputs)
    unit_one = inputs * scale_one
    plane_in = plane_gather(layout_in).astype(f32)
    normed = (plane_in * rms_scale(plane_in) * gain_one).astype(bf16)
    upstream = layout_grad.astype(f32) * own_valid
    ffn_grad = plane_gather(upstream.astype(bf16))
    projected = project(normed, w_first)
    rank_rows = projected[:, wide_first : wide_first + rank]
    logits = jnp.dot(rank_rows, rank_up, precision=highest) + bias
    decays = jax.nn.log_sigmoid(logits) / 16.0
    state_shape = pltpu.VMEM((HEAD_V, HEAD_K), f32)
    through_shape = pltpu.VMEM((8, HEAD_K), f32)
    key_spec = functools.partial(rows_of, HEAD_K, 1)
    value_spec = functools.partial(rows_of, HEAD_V, 1)
    gate_spec = functools.partial(rows_of, HEAD_V, 2)
    narrow = functools.partial(rows_of, HEAD_K, 0)
    broad = functools.partial(rows_of, HEAD_V, 0)
    cumul, left = over_blocks(
        states_kernel, order, resets,
        (projected, projected, decays),
        [key_spec(), value_spec(), narrow()],
        (shape_of((tokens, HEAD_K)), shape_of((HEAD_V + 8, HEAD_K))),
        (narrow(), whole_of((HEAD_V + 8, HEAD_K))),
        [state_shape, through_shape],
        1 << 30, 6 << 20,
    )
    leaving, through = (left[:HEAD_V], left[HEAD_V : HEAD_V + 1])

    def shifted(value, distance):
        reach = planes - abs(distance)
        if distance > 0:
            hops = [(i, i + distance) for i in range(reach)]
        else:
            hops = [(i - distance, i) for i in range(reach)]
        return lax.ppermute(value, "o", hops)

    passed = [shifted(left, d) for d in range(1, planes)]
    entering = passed[-1][:HEAD_V]
    for d in range(planes - 2, 0, -1):
        entering = entering * passed[d - 1][HEAD_V : HEAD_V + 1] + passed[d - 1][:HEAD_V]
    gated, mixed, saved = over_blocks(
        mix_kernel, order, resets,
        (projected, projected, projected, projected, cumul, head_gain, entering),
        [narrow(), key_spec(), value_spec(), gate_spec(), narrow(), whole_of((1, HEAD_V)), whole_of((HEAD_V, HEAD_K))],
        (shape_of((tokens, HEAD_V), bf16), shape_of((tokens, HEAD_V)), shape_of((blocks, HEAD_V, HEAD_K))),
        (broad(), broad(), saved_of()),
        [state_shape],
        4 << 30, 16 << 20,
    )

    def member(value, distance):
        return value[distance * rows : (distance + 1) * rows]

    attended = plane_sum(lambda d: project_back(member(gated, d), wo))
    hidden = inputs + attended

    scale_two = rms_scale(hidden)
    unit_two = hidden * scale_two
    normed_two = plane_gather((unit_two * gain_two).astype(bf16))
    gate_up = project(normed_two, w_gate_up)
    gating, upward = (gate_up[:, :hidden_here], gate_up[:, hidden_here:])
    up_sig = jax.nn.sigmoid(gating)
    gate_silu = gating * up_sig
    product = (gate_silu * upward).astype(bf16)
    ffn_out = plane_sum(lambda d: project_back(member(product, d), w_down))
    result = ((hidden + ffn_out) * own_valid).astype(bf16)

    def homeward(value):
        back = exchange(project(unpack, value).astype(bf16))
        return restored(outer_sum(pack, back).astype(bf16))

    own_output = homeward(result)
    d_product = project(ffn_grad, w_down)
    d_gating = d_product * upward * up_sig * (1.0 + gating * (1.0 - up_sig))
    d_upward = d_product * gate_silu
    d_gate_up = jnp.concatenate([d_gating.astype(bf16), d_upward.astype(bf16)], axis=1)
    d_normed_two = plane_sum(lambda d: project_back(member(d_gate_up, d), w_gate_up))
    grad_down = deliver(ffn_grad, product)
    grad_gate_up = deliver(normed_two, d_gate_up)
    grad_gain_two = jnp.sum(d_normed_two * unit_two, axis=0)
    d_hidden = upstream + norm_back(d_normed_two * gain_two, unit_two, scale_two)

    attn_grad = plane_gather(d_hidden.astype(bf16))
    d_gated = project(attn_grad, wo)
    grad_out = deliver(attn_grad, gated)
    d_mixed, d_gate_pre, head_part, pulled = over_blocks(
        pull_kernel, order, resets,
        (projected, projected, cumul, mixed, d_gated, head_gain),
        [narrow(), gate_spec(), narrow(), broad(), broad(), whole_of((1, HEAD_V))],
        (
            shape_of((tokens, HEAD_V)),
            shape_of((tokens, HEAD_V), bf16),
            shape_of((8, HEAD_V)),
            shape_of((HEAD_V, HEAD_K)),
        ),
        (broad(), broad(), whole_of((8, HEAD_V)), whole_of((HEAD_V, HEAD_K))),
        [through_shape],
        1 << 30, 12 << 20,
    )
    pulled_ext = jnp.concatenate([pulled, left[HEAD_V:]], axis=0)
    returned = [shifted(pulled_ext, -d) for d in range(1, planes)]
    later = returned[-1][:HEAD_V]
    for d in range(planes - 2, 0, -1):
        later = later * returned[d - 1][HEAD_V : HEAD_V + 1] + returned[d - 1][:HEAD_V]
    flip = functools.partial
    grads, d_decays = over_blocks(
        back_kernel, order, resets,
        (projected, projected, projected, cumul, saved, d_mixed, d_gate_pre, later),
        [
            narrow(backward=True), key_spec(backward=True), value_spec(backward=True), narrow(backward=True),
            saved_of(True), broad(backward=True), broad(backward=True), whole_of((HEAD_V, HEAD_K)),
        ],
        (shape_of((tokens, wide_first), bf16), shape_of((tokens, HEAD_K))),
        (rows_of(wide_first, 0, True), narrow(backward=True)),
        [state_shape],
        8 << 30, 24 << 20,
    )
    d_logits = d_decays / 16.0 * jax.nn.sigmoid(-logits)
    grad_rank_up = lax.dot_general(rank_rows, d_logits, contract_rows, precision=highest)
    grad_bias = jnp.sum(d_logits, axis=0, keepdims=True)
    rank_part = lax.dot_general(d_logits, rank_up, contract_last, precision=highest)
    rank_part = jnp.pad(rank_part, ((0, 0), (0, LANES - rank)))

    def first_part(d):
        product_part = project_back(member(grads, d), w_first[:, :wide_first])
        return jnp.concatenate([product_part, member(rank_part, d)], axis=1)

    summed = plane_sum(first_part)
    grad_first = deliver(normed, grads)
    rank_grad = summed[:, width : width + rank].astype(bf16)
    d_normed = summed[:, :width] + project_back(rank_grad, rank_down)
    grad_gain_one = jnp.sum(d_normed * unit_one, axis=0)
    d_inputs = d_hidden + norm_back(d_normed * gain_one, unit_one, scale_one)
    own_input_grad = homeward(d_inputs.astype(bf16))
    own_normed = (unit_one * gain_one).astype(bf16)
    grad_rank_down = outer_sum(rank_grad, own_normed)

    home_valid = layout_valid(starts, lengths, targets)[:, None]
    difference = own_output.astype(f32) - mine(teacher).astype(f32)
    loss_part = jnp.sum(home_valid * difference * difference)
    small = jnp.concatenate([grad_rank_up, grad_bias], axis=0)
    member_ids = jnp.arange(GROUP, dtype=jnp.int32)[:, None, None]
    small = jnp.where(member_ids == t, small[None], 0.0).reshape(-1, HEAD_K)
    wide_rows = jnp.concatenate([grad_rank_down, grad_gain_one[None], grad_gain_two[None]], axis=0)
    everything = jnp.concatenate(
        [
            small,
            jnp.sum(head_part, axis=0).reshape(-1, HEAD_K),
            jnp.full((1, HEAD_K), loss_part, f32),
            wide_rows.reshape(-1, HEAD_K),
        ],
        axis=0,
    )
    everything = everything + swapped(everything)
    for distance in (1, 2):
        everything = everything + neighbour(everything, distance)
    distance = 1
    while distance < planes:
        hops = [(i, i ^ distance) for i in range(planes)]
        everything = everything + lax.ppermute(everything, "o", hops)
        distance *= 2
    used = GROUP * (rank + 1)
    summed_small = everything[:used].reshape(GROUP, rank + 1, HEAD_K)
    pair_small = lax.dynamic_slice_in_dim(summed_small, 2 * c, 2, 0)
    pair_small = jnp.concatenate([pair_small[0], pair_small[1]], axis=1)
    head_rows = HEAD_V // HEAD_K
    summed_head = everything[used : used + head_rows].reshape(-1)
    summed_loss = everything[used + head_rows, 0]
    wide_sum = everything[used + head_rows + 1 :].reshape(rank + 2, width)
    own_column = (t // 2) * half + (o * 2 + t % 2) * shard
    own_wide = lax.dynamic_slice_in_dim(wide_sum, own_column, shard, 1)
    loss = summed_loss / (jnp.sum(seq_len).astype(f32) * width)

    def both(value):
        other = swapped(value)
        return jnp.stack([jnp.where(c == 0, value, other), jnp.where(c == 0, other, value)])

    def columns(pair_of, start, size):
        return jnp.concatenate([piece[:, start : start + size] for piece in pair_of], axis=1)

    return (
        both(own_output),
        loss,
        both(own_input_grad),
        columns(grad_first, 0, HEAD_K),
        columns(grad_first, HEAD_K, HEAD_K),
        columns(grad_first, 2 * HEAD_K, HEAD_V),
        columns(grad_first, 2 * HEAD_K + HEAD_V, HEAD_V),
        columns(grad_out, 0, HEAD_V),
        columns(grad_gate_up, 0, hidden_here),
        columns(grad_gate_up, hidden_here, hidden_here),
        columns(grad_down, 0, hidden_here),
        own_wide[:rank].T,
        pair_small[:rank],
        pair_small[rank],
        own_wide[rank],
        own_wide[rank + 1],
        summed_head,
    )


def solution(mesh):
    seq = ("o", "t")
    count = mesh.devices.shape[0]
    split = Mesh(mesh.devices.reshape(count // GROUP, GROUP, 2), ("o", "t", "c"))
    tokens = P(None, seq, None)
    weight = P(seq, "c")
    placed = (
        (tokens, tokens, tokens, P(None, seq), P(), P())
        + (weight,) * 8
        + (P(seq, None), P(None, "c"), P("c"), P(seq), P(seq), P())
    )
    return jax.shard_map(
        local,
        mesh=split,
        in_specs=placed,
        out_specs=(tokens, P(), tokens)
        + (weight,) * 8
        + (P(seq, None), P(None, "c"), P("c"), P(seq), P(seq), P()),
        check_vma=False,
    )
```

time: 4450 us -> 1150 us (0.26)
  waiting for transfers between devices: 2890 us -> 578 us
  blocking collectives: 494 us -> 0 us
  local copies, waits for them, and re-layouts: 283 us -> 49.5 us
  matrix products: 425 us -> 205 us
  other arithmetic: 232 us -> 54.3 us
  Pallas kernels: 0 us -> 89.9 us
  starting transfers between devices: 75.9 us -> 141 us
    reduce_scatter x9 -> x4, waiting for transfers between devices: 1890 us -> 0.01 us  [deliver(): part = lax.psum_scatter(total, 'o', scatter_dimension=0, tiled=True)]
    all_gather x12 -> x4, waiting for transfers between devices: 799 us -> 0.03 us  [fetch(): lax.all_gather(jnp.concatenate(either(*got), axis=0), ('c', 'o'), axis=0,...]
    ppermute x0 -> x58, waiting for transfers between devices: none -> 520 us  [the longest x26 292 us: neighbour(): return lax.ppermute(value, 't', [(i, i ^ distance) for i in range(GROUP)])]
    all_gather x5 -> x0, blocking collectives: 376 us -> none  [the longest x1 124 us: fetch(): lax.all_gather(shards[10], 'seq', axis=0, tiled=True)]
    dot_general x172 -> x39, matrix products: 423 us -> 202 us  [the longest x16 72.9 us: project_back(): lax.dot_general(left, right, contract_last, preferred_element_type=f32)]
    psum x2 -> x0, blocking collectives: 118 us -> none  [the longest x1 114 us: local(): lax.psum((small_totals[0], small_totals[1], small_totals[2], loss_part),...]
    all_to_all x5 -> x4, waiting for transfers between devices: 170 us -> 58.1 us  [exchange(): lax.all_to_all(value, ('o', 't'), split_axis=0, concat_axis=0, tiled=True)]
    select_n x73 -> x17, other arithmetic: 98.5 us -> 8.44 us  [the longest x14 8.35 us: either(): return (jnp.where(even, first, second), jnp.where(even, second, first))]
  transfers between devices with their start and end apart: 29 -> 70, of which waited for: 20 -> 34; matrix products, arithmetic and copies ran while one was open for 15% -> 21% of each run, Pallas kernels for 0% -> 8%
where the time goes in v1:
time: 1150 us; the launch traced here: 1140 us
  waiting for transfers between devices  578 us (50%)
  matrix products  205 us (18%)
  starting transfers between devices  141 us (12%)
  Pallas kernels  89.9 us (8%)
  other arithmetic  54.3 us (5%)
  local copies, waits for them, and re-layouts  49.5 us (4%)
  between operations  18.3 us (2%)
    ppermute x26, waiting for transfers between devices, neighbour(): return lax.ppermute(value, 't', [(i, i ^ distance) for i in range(GROUP)])  292 us
    ppermute x6, waiting for transfers between devices, shifted(): return lax.ppermute(value, 'o', hops)  115 us
    pallas_call x4, Pallas kernels, over_blocks(): pl.pallas_call(kernel, out_shape=outs, grid_spec=pltpu.PrefetchScalarGrid...  89.9 us
    dot_general x16, matrix products, project_back(): lax.dot_general(left, right, contract_last, preferred_element_type=f32)  72.9 us
    ppermute x2, waiting for transfers between devices, local(): everything = everything + lax.ppermute(everything, 'o', hops)  72.6 us
    dot_general x9, matrix products, project(): return jnp.dot(left, right, preferred_element_type=f32)  65.2 us
    dot_general x13, matrix products, outer_sum(): lax.dot_general(left, right, contract_rows, preferred_element_type=f32)  61.1 us
    all_to_all x4, waiting for transfers between devices, exchange(): lax.all_to_all(value, ('o', 't'), split_axis=0, concat_axis=0, tiled=True)  58.1 us
  transfers between devices with their start and end apart: 70, of which 34 were waited for; matrix products, arithmetic and copies ran while one was open for 21% of the time, Pallas kernels for 8%

profile of v1, /device:TPU:0, one launch (start us, length us, event | category | flops | bytes accessed | tf_op | source)
XLA Modules:
  0.0 1136.0 jit_solution(15777788048544885815)
XLA Ops:
  16.0 8.5 collective-permute-done.4
  36.1 9.6 collective-permute-done.18
  54.9 19.4 %all-to-all-start = ((bf16[16,32,2176]{2,1,0:T(8,128)(2,1)}), bf16[16,32,2176]{2,1,0:T(8,128)(2,1)}, u32[]{:S(2)}, u32[]{:S(2)}) async-start(bf16[16,32,2176]{2,1,0:T(8,128)(2,1)} %bitcast.117), calls=%async_computation | async-start | bytes 4456448 | tf_op jit(solution)/shard_map/all_to_all | solution.py:332
  80.2 58.1 %all-to-all-done = bf16[16,32,2176]{2,1,0:T(8,128)(2,1)} async-done(((bf16[16,32,2176]{2,1,0:T(8,128)(2,1)}), bf16[16,32,2176]{2,1,0:T(8,128)(2,1)}, u32[]{:S(2)}, u32[]{:S(2)}) %all-to-all-start) | async-done | bytes 2228256 | tf_op jit(solution)/shard_map/all_to_all | solution.py:332
  149.6 19.1 %collective-permute-done = bf16[256,2048]{1,0:T(8,128)(2,1)} collective-permute-done((bf16[256,2048]{1,0:T(8,128)(2,1)S(1)}, bf16[256,2048]{1,0:T(8,128)(2,1)}, u32[]{:S(2)}, u32[]{:S(2)}) %collective-permute-start) | collective-permute-done | bytes 1048608 | tf_op jit(solution)/shard_map/ppermute | solution.py:249
  168.7 23.2 %collective-permute-done.1 = bf16[256,2048]{1,0:T(8,128)(2,1)} collective-permute-done((bf16[256,2048]{1,0:T(8,128)(2,1)S(1)}, bf16[256,2048]{1,0:T(8,128)(2,1)}, u32[]{:S(2)}, u32[]{:S(2)}) %collective-permute-start.1) | collective-permute-done | bytes 1048608 | tf_op jit(solution)/shard_map/ppermute | solution.py:249
  201.4 7.7 fusion.171.key_ref.value_ref.query_ref.gate_ref
  212.1 15.7 %shard_map.323 = (f32[1024,256]{1,0:T(8,128)S(1)}, f32[520,256]{1,0:T(8,128)}) custom-call(s32[16]{0:T(128)S(1)} %fusion.139.order, s32[16]{0:T(128)S(1)} %convert_element_type.294.resets, f32[1024,1664]{1,0:T(8,128)S(1)} %fusion.171.key_ref.value_ref.query_ref.gate_ref, f32[1024,1664]{1,0:T(8,128)S(1)} %fusion.171.key_ref.value_ref.query_ref.gate_ref, ...), custom_call_target="tpu_custom_call" | custom-call | flops 1073741824 | bytes 6291456 | tf_op jit(solution)/shard_map/pallas_call | solution.py:223
  227.8 13.6 %collective-permute-start.7 = (f32[520,256]{1,0:T(8,128)}, f32[520,256]{1,0:T(8,128)}, u32[]{:S(2)}, u32[]{:S(2)}) collective-permute-start(f32[520,256]{1,0:T(8,128)} %get-tuple-element.29), channel_id=1, source_target_pairs={{0,16},{8,24},{1,17},{9,25},{2,18},{10,26},{3,19},{11,27},{4,20},{... | collective-permute-start | bytes 1597448 | tf_op jit(solution)/shard_map/ppermute | solution.py:426
  258.6 6.2 collective-permute-done.7
  265.5 22.1 %collective-permute-done.8 = f32[520,256]{1,0:T(8,128)} collective-permute-done((f32[520,256]{1,0:T(8,128)}, f32[520,256]{1,0:T(8,128)}, u32[]{:S(2)}, u32[]{:S(2)}) %collective-permute-start.8) | collective-permute-done | bytes 532512 | tf_op jit(solution)/shard_map/ppermute | solution.py:426
  288.3 14.2 %collective-permute-done.6 = f32[520,256]{1,0:T(8,128)} collective-permute-done((f32[520,256]{1,0:T(8,128)}, f32[520,256]{1,0:T(8,128)}, u32[]{:S(2)}, u32[]{:S(2)}) %collective-permute-start.6) | collective-permute-done | bytes 532512 | tf_op jit(solution)/shard_map/ppermute | solution.py:426
  306.9 21.1 %shard_map.324 = (bf16[1024,512]{1,0:T(8,128)(2,1)S(1)}, f32[1024,512]{1,0:T(8,128)S(1)}, f32[16,512,256]{2,1,0:T(8,128)}) custom-call(s32[16]{0:T(128)S(1)} %fusion.139.order, s32[16]{0:T(128)S(1)} %convert_element_type.294.resets, f32[1024,1664]{1,0:T(8,128)S(1)} %copy-done.3, f32[1024,1664]{1,0:T(8,128)S(1)} %copy-done.3, f32[1024,1664]{1,0:T(8,128)S(1)} %copy-done.3, ...), custom_call_target="tpu_custom_call" | custom-call | flops 4294967296 | bytes 16777216 | tf_op jit(solution)/shard_map/pallas_call | solution.py:223
  341.3 20.3 %collective-permute-done.11 = bf16[256,2048]{1,0:T(8,128)(2,1)} collective-permute-done((bf16[256,2048]{1,0:T(8,128)(2,1)}, bf16[256,2048]{1,0:T(8,128)(2,1)}, u32[]{:S(2)}, u32[]{:S(2)}) %collective-permute-start.11) | collective-permute-done | bytes 1048608 | tf_op jit(solution)/shard_map/ppermute | solution.py:249
  361.6 20.3 %collective-permute-done.12 = bf16[256,2048]{1,0:T(8,128)(2,1)} collective-permute-done((bf16[256,2048]{1,0:T(8,128)(2,1)}, bf16[256,2048]{1,0:T(8,128)(2,1)}, u32[]{:S(2)}, u32[]{:S(2)}) %collective-permute-start.12) | collective-permute-done | bytes 1048608 | tf_op jit(solution)/shard_map/ppermute | solution.py:249
  399.1 15.8 %collective-permute-done.14 = bf16[256,2048]{1,0:T(8,128)(2,1)} collective-permute-done((bf16[256,2048]{1,0:T(8,128)(2,1)}, bf16[256,2048]{1,0:T(8,128)(2,1)}, u32[]{:S(2)}, u32[]{:S(2)}) %collective-permute-start.14) | collective-permute-done | bytes 1048608 | tf_op jit(solution)/shard_map/ppermute | solution.py:249
  417.1 21.7 %collective-permute-done.15 = bf16[256,2048]{1,0:T(8,128)(2,1)} collective-permute-done((bf16[256,2048]{1,0:T(8,128)(2,1)}, bf16[256,2048]{1,0:T(8,128)(2,1)}, u32[]{:S(2)}, u32[]{:S(2)}) %collective-permute-start.15) | collective-permute-done | bytes 1048608 | tf_op jit(solution)/shard_map/ppermute | solution.py:249
  438.8 21.3 %fusion.154 = f32[1024,2816]{1,0:T(8,128)} fusion(bf16[2048,2816]{1,0:T(8,128)(2,1)} %all-gather.9.cloned.1.call-done, bf16[256,2048]{1,0:T(8,128)(2,1)} %collective-permute-done.16, bf16[256,2048]{1,0:T(8,128)(2,1)} %collective-permute-done.15, bf16[256,2048]{1,0:T(8,128)(2,1)} %collective-permute-done.14, bf16[256,2048]{1,0:T(8,128)(2,1)} %multiply_convert_fusion.3), kind=kOutput, calls=%fused_computation.329 | convolution fusion | flops 11827937280 | bytes 27262976 | tf_op jit(solution)/shard_map/dot_general | solution.py:40
  460.1 22.3 %collective-permute-done.26 = bf16[256,2048]{1,0:T(8,128)(2,1)} collective-permute-done((bf16[256,2048]{1,0:T(8,128)(2,1)}, bf16[256,2048]{1,0:T(8,128)(2,1)}, u32[]{:S(2)}, u32[]{:S(2)}) %collective-permute-start.26) | collective-permute-done | bytes 1048608 | tf_op jit(solution)/shard_map/ppermute | solution.py:249
  482.4 16.5 %multiply_convert_fusion = (bf16[1024,1408]{1,0:T(8,128)(2,1)S(1)}, bf16[1024,1408]{1,0:T(8,128)(2,1)}, bf16[1024,1408]{1,0:T(8,128)(2,1)}) fusion(f32[1024,2816]{1,0:T(8,128)} %fusion.154, bf16[2048,1408]{1,0:T(8,128)(2,1)} %all-gather.11.cloned.1.call-done, bf16[256,2048]{1,0:T(8,128)(2,1)} %collective-permute-done.27, ...), kind=kOutput, calls=%fused_computation.17 | convolution fusion | flops 5943984128 | bytes 30146560 | tf_op jit(solution)/shard_map/dot_general | solution.py:40
  498.8 8.7 convolution_convert_fusion.10
  509.2 7.7 convolution_convert_fusion.9
  518.4 7.9 convolution_convert_fusion.8
  526.9 7.8 collective-permute-done.28
  534.7 20.4 %collective-permute-done.29 = bf16[256,2048]{1,0:T(8,128)(2,1)S(1)} collective-permute-done((bf16[256,2048]{1,0:T(8,128)(2,1)S(1)}, bf16[256,2048]{1,0:T(8,128)(2,1)S(1)}, u32[]{:S(2)}, u32[]{:S(2)}) %collective-permute-start.29) | collective-permute-done | bytes 1048608 | tf_op jit(solution)/shard_map/ppermute | solution.py:249
  556.0 9.0 multiply_reduce_fusion.1
  580.4 13.3 %collective-permute-done.31 = bf16[256,2048]{1,0:T(8,128)(2,1)} collective-permute-done((bf16[256,2048]{1,0:T(8,128)(2,1)}, bf16[256,2048]{1,0:T(8,128)(2,1)}, u32[]{:S(2)}, u32[]{:S(2)}) %collective-permute-start.31) | collective-permute-done | bytes 1048608 | tf_op jit(solution)/shard_map/ppermute | solution.py:249
  593.7 21.8 %collective-permute-done.32 = bf16[256,2048]{1,0:T(8,128)(2,1)} collective-permute-done((bf16[256,2048]{1,0:T(8,128)(2,1)}, bf16[256,2048]{1,0:T(8,128)(2,1)}, u32[]{:S(2)}, u32[]{:S(2)}) %collective-permute-start.32) | collective-permute-done | bytes 1048608 | tf_op jit(solution)/shard_map/ppermute | solution.py:249
  627.8 5.3 fusion.172.grad_ref
  633.2 16.2 %shard_map.325 = (f32[1024,512]{1,0:T(8,128)S(1)}, bf16[1024,512]{1,0:T(8,128)(2,1)S(1)}, f32[8,512]{1,0:T(8,128)S(1)}, f32[512,256]{1,0:T(8,128)S(1)}) custom-call(s32[16]{0:T(128)S(1)} %fusion.139.order, s32[16]{0:T(128)S(1)} %convert_element_type.294.resets, f32[1024,1664]{1,0:T(8,128)} %copy-done.2, f32[1024,1664]{1,0:T(8,128)} %copy-done.2, ...), custom_call_target="tpu_custom_call" | custom-call | flops 1073741824 | bytes 12582912 | tf_op jit(solution)/shard_map/pallas_call | solution.py:223
  656.7 68.0 %collective-permute-done.35 = f32[520,256]{1,0:T(8,128)S(1)} collective-permute-done((f32[520,256]{1,0:T(8,128)}, f32[520,256]{1,0:T(8,128)S(1)}, u32[]{:S(2)}, u32[]{:S(2)}) %collective-permute-start.35) | collective-permute-done | bytes 532512 | tf_op jit(solution)/shard_map/ppermute | solution.py:426
  725.7 6.2 add_convert_fusion.2
  738.8 36.9 %shard_map.326 = (bf16[1024,1536]{1,0:T(8,128)(2,1)S(1)}, f32[1024,256]{1,0:T(8,128)S(1)}) custom-call(s32[16]{0:T(128)S(1)} %fusion.139.order, s32[16]{0:T(128)S(1)} %convert_element_type.294.resets, f32[1024,1664]{1,0:T(8,128)} %copy-done.2, f32[1024,1664]{1,0:T(8,128)} %copy-done.2, f32[1024,1664]{1,0:T(8,128)} %copy-done.2, ...), custom_call_target="tpu_custom_call" | custom-call | flops 8589934592 | bytes 25165824 | tf_op jit(solution)/shard_map/pallas_call | solution.py:223
  786.1 7.3 convolution_convert_fusion.19
  802.5 8.0 convolution_convert_fusion
  810.5 6.4 add_convert_fusion.1
  820.5 22.3 %collective-permute-done.22 = bf16[256,2048]{1,0:T(8,128)(2,1)} collective-permute-done((bf16[256,2048]{1,0:T(8,128)(2,1)}, bf16[256,2048]{1,0:T(8,128)(2,1)}, u32[]{:S(2)}, u32[]{:S(2)}) %collective-permute-start.22) | collective-permute-done | bytes 1048608 | tf_op jit(solution)/shard_map/ppermute | solution.py:249
  842.7 7.4 convolution_convert_fusion.6
  850.1 22.5 %all-to-all-start.1 = ((bf16[16,32,2048]{2,1,0:T(8,128)(2,1)}), bf16[16,32,2048]{2,1,0:T(8,128)(2,1)}, u32[]{:S(2)}, u32[]{:S(2)}) async-start(bf16[16,32,2048]{2,1,0:T(8,128)(2,1)} %bitcast.118), calls=%async_computation.1 | async-start | bytes 4194304 | tf_op jit(solution)/shard_map/all_to_all | solution.py:332
  889.8 10.3 add_convert_fusion
  907.1 19.4 %collective-permute-done.37 = bf16[256,2176]{1,0:T(8,128)(2,1)} collective-permute-done((bf16[256,2176]{1,0:T(8,128)(2,1)S(1)}, bf16[256,2176]{1,0:T(8,128)(2,1)}, u32[]{:S(2)}, u32[]{:S(2)}) %collective-permute-start.37) | collective-permute-done | bytes 1114144 | tf_op jit(solution)/shard_map/ppermute | solution.py:249
  926.5 29.4 %collective-permute-done.38 = bf16[256,2176]{1,0:T(8,128)(2,1)} collective-permute-done((bf16[256,2176]{1,0:T(8,128)(2,1)}, bf16[256,2176]{1,0:T(8,128)(2,1)}, u32[]{:S(2)}, u32[]{:S(2)}) %collective-permute-start.38) | collective-permute-done | bytes 1114144 | tf_op jit(solution)/shard_map/ppermute | solution.py:249
  981.6 5.7 collective-permute-done.41
  993.7 5.5 collective-permute-done.42
  1000.7 46.2 %collective-permute-done.43 = f32[215,256]{1,0:T(8,128)S(1)} collective-permute-done((f32[215,256]{1,0:T(8,128)S(1)}, f32[215,256]{1,0:T(8,128)S(1)}, u32[]{:S(2)}, u32[]{:S(2)}) %collective-permute-start.43) | collective-permute-done | bytes 220192 | tf_op jit(solution)/shard_map/ppermute | solution.py:551
  1055.0 26.4 %collective-permute-done.44 = f32[215,256]{1,0:T(8,128)S(1)} collective-permute-done((f32[215,256]{1,0:T(8,128)S(1)}, f32[215,256]{1,0:T(8,128)S(1)}, u32[]{:S(2)}, u32[]{:S(2)}) %collective-permute-start.44) | collective-permute-done | bytes 220192 | tf_op jit(solution)/shard_map/ppermute | solution.py:551
  1102.0 6.3 collective-permute-done.48
  1116.1 8.8 collective-permute-done.54
  (446 shorter events, 279.8 us)
Async XLA Ops:
  7.2 188.2 %all-gather.5.cloned.1.call-start = ((), (), s32[]{:S(2)}) async-start(), calls=%async_computation.8 | async-start | bytes 7667712 | tf_op jit(solution)/shard_map/all_gather | solution.py:308
  25.6 304.8 %all-gather.7.cloned.1.call-start = ((), (), s32[]{:S(2)}) async-start(), calls=%async_computation.9 | async-start | bytes 2359296 | tf_op jit(solution)/shard_map/all_gather | solution.py:308
  32.9 405.9 %all-gather.9.cloned.1.call-start = ((), (), s32[]{:S(2)}) async-start(), calls=%async_computation.10 | async-start | bytes 12976128 | tf_op jit(solution)/shard_map/all_gather | solution.py:308
  54.9 83.4 %all-to-all-start = ((bf16[16,32,2176]{2,1,0:T(8,128)(2,1)}), bf16[16,32,2176]{2,1,0:T(8,128)(2,1)}, u32[]{:S(2)}, u32[]{:S(2)}) async-start(bf16[16,32,2176]{2,1,0:T(8,128)(2,1)} %bitcast.117), calls=%async_computation | async-start | bytes 4456448 | tf_op jit(solution)/shard_map/all_to_all | solution.py:332
  74.3 408.0 %all-gather.11.cloned.1.call-start = ((), (), s32[]{:S(2)}) async-start(), calls=%async_computation.11 | async-start | bytes 6488064 | tf_op jit(solution)/shard_map/all_gather | solution.py:308
  74.4 72.6 %collective-permute-start.5 = (bf16[17,512]{1,0:T(8,128)(2,1)S(1)}, bf16[17,512]{1,0:T(8,128)(2,1)}, u32[]{:S(2)}, u32[]{:S(2)}) collective-permute-start(bf16[17,512]{1,0:T(8,128)(2,1)S(1)} %constant_dynamic-update-slice_fusion), channel_id=1, source_target_pairs={{0,1},{1,0},{2,3},{3,2},{4,5},{5,4},{6,7},{7,6},{8,9},{9,8},{10,11... | collective-permute-start | bytes 52232 | tf_op jit(solution)/shard_map/ppermute | solution.py:245
  76.1 71.4 %collective-permute-start.19 = (bf16[128,1408]{1,0:T(8,128)(2,1)}, bf16[128,1408]{1,0:T(8,128)(2,1)S(1)}, u32[]{:S(2)}, u32[]{:S(2)}) collective-permute-start(bf16[128,1408]{1,0:T(8,128)(2,1)} %get-tuple-element.121), channel_id=1, source_target_pairs={{0,0},{1,4},{2,2},{3,6},{4,1},{5,5},{6,3},{7,7},{8,8},{9,12},{10,1... | collective-permute-start | bytes 1081352 | tf_op jit(solution)/shard_map/ppermute | solution.py:307
  77.9 69.6 %collective-permute-start.20 = (bf16[128,1408]{1,0:T(8,128)(2,1)}, bf16[128,1408]{1,0:T(8,128)(2,1)}, u32[]{:S(2)}, u32[]{:S(2)}) collective-permute-start(bf16[128,1408]{1,0:T(8,128)(2,1)} %get-tuple-element.122), channel_id=1, source_target_pairs={{0,2},{1,6},{2,0},{3,4},{4,3},{5,7},{6,1},{7,5},{8,10},{9,14},{10,... | collective-permute-start | bytes 1081352 | tf_op jit(solution)/shard_map/ppermute | solution.py:307
  143.5 48.3 %collective-permute-start.1 = (bf16[256,2048]{1,0:T(8,128)(2,1)S(1)}, bf16[256,2048]{1,0:T(8,128)(2,1)}, u32[]{:S(2)}, u32[]{:S(2)}) collective-permute-start(bf16[256,2048]{1,0:T(8,128)(2,1)S(1)} %get-tuple-element.154), channel_id=1, source_target_pairs={{0,4},{2,6},{4,0},{6,2},{1,5},{3,7},{5,1},{7,3},{8,12},{10,14},{12... | collective-permute-start | bytes 3145736 | tf_op jit(solution)/shard_map/ppermute | solution.py:249
  147.0 46.0 %collective-permute-start.2 = (bf16[256,2048]{1,0:T(8,128)(2,1)S(1)}, bf16[256,2048]{1,0:T(8,128)(2,1)}, u32[]{:S(2)}, u32[]{:S(2)}) collective-permute-start(bf16[256,2048]{1,0:T(8,128)(2,1)S(1)} %get-tuple-element.154), channel_id=1, source_target_pairs={{0,6},{2,4},{4,2},{6,0},{1,7},{3,5},{5,3},{7,1},{8,14},{10,12},{12... | collective-permute-start | bytes 3145736 | tf_op jit(solution)/shard_map/ppermute | solution.py:249
  227.8 37.0 %collective-permute-start.7 = (f32[520,256]{1,0:T(8,128)}, f32[520,256]{1,0:T(8,128)}, u32[]{:S(2)}, u32[]{:S(2)}) collective-permute-start(f32[520,256]{1,0:T(8,128)} %get-tuple-element.29), channel_id=1, source_target_pairs={{0,16},{8,24},{1,17},{9,25},{2,18},{10,26},{3,19},{11,27},{4,20},{... | collective-permute-start | bytes 1597448 | tf_op jit(solution)/shard_map/ppermute | solution.py:426
  241.5 46.2 %collective-permute-start.8 = (f32[520,256]{1,0:T(8,128)}, f32[520,256]{1,0:T(8,128)}, u32[]{:S(2)}, u32[]{:S(2)}) collective-permute-start(f32[520,256]{1,0:T(8,128)} %get-tuple-element.29), channel_id=1, source_target_pairs={{0,8},{8,16},{16,24},{1,9},{9,17},{17,25},{2,10},{10,18},{18,26},{... | collective-permute-start | bytes 1597448 | tf_op jit(solution)/shard_map/ppermute | solution.py:426
  245.8 56.7 %collective-permute-start.6 = (f32[520,256]{1,0:T(8,128)}, f32[520,256]{1,0:T(8,128)}, u32[]{:S(2)}, u32[]{:S(2)}) collective-permute-start(f32[520,256]{1,0:T(8,128)} %get-tuple-element.29), channel_id=1, source_target_pairs={{0,24},{1,25},{2,26},{3,27},{4,28},{5,29},{6,30},{7,31}} | collective-permute-start | bytes 1597448 | tf_op jit(solution)/shard_map/ppermute | solution.py:426
  253.6 138.5 %all-to-all-start.2 = ((bf16[16,32,2048]{2,1,0:T(8,128)(2,1)}), bf16[16,32,2048]{2,1,0:T(8,128)(2,1)}, u32[]{:S(2)}, u32[]{:S(2)}) async-start(bf16[16,32,2048]{2,1,0:T(8,128)(2,1)} %bitcast.108), calls=%async_computation.2 | async-start | bytes 4194304 | tf_op jit(solution)/shard_map/all_to_all | solution.py:332
  258.1 731.1 %reduce-scatter.7.cloned.1.call-start = ((), (), s32[]{:S(2)}) async-start(), calls=%async_computation.13 | async-start | bytes 1310720 | tf_op jit(solution)/shard_map/reduce_scatter | solution.py:315
  334.3 27.4 %collective-permute-start.11 = (bf16[256,2048]{1,0:T(8,128)(2,1)}, bf16[256,2048]{1,0:T(8,128)(2,1)}, u32[]{:S(2)}, u32[]{:S(2)}) collective-permute-start(bf16[256,2048]{1,0:T(8,128)(2,1)} %convolution_convert_fusion.15), channel_id=1, source_target_pairs={{0,6},{2,4},{4,2},{6,0},{1,7},{3,5},{5,3},{7,1},{8,14},{10,12},{12... | collective-permute-start | bytes 3145736 | tf_op jit(solution)/shard_map/ppermute | solution.py:249
  338.6 43.3 %collective-permute-start.12 = (bf16[256,2048]{1,0:T(8,128)(2,1)}, bf16[256,2048]{1,0:T(8,128)(2,1)}, u32[]{:S(2)}, u32[]{:S(2)}) collective-permute-start(bf16[256,2048]{1,0:T(8,128)(2,1)} %convolution_convert_fusion.14), channel_id=1, source_target_pairs={{0,2},{2,0},{4,6},{6,4},{1,3},{3,1},{5,7},{7,5},{8,10},{10,8},{12,... | collective-permute-start | bytes 3145736 | tf_op jit(solution)/shard_map/ppermute | solution.py:249
  340.9 41.0 %collective-permute-start.13 = (bf16[256,2048]{1,0:T(8,128)(2,1)}, bf16[256,2048]{1,0:T(8,128)(2,1)}, u32[]{:S(2)}, u32[]{:S(2)}) collective-permute-start(bf16[256,2048]{1,0:T(8,128)(2,1)} %convolution_convert_fusion.13), channel_id=1, source_target_pairs={{0,4},{2,6},{4,0},{6,2},{1,5},{3,7},{5,1},{7,3},{8,12},{10,14},{12... | collective-permute-start | bytes 3145736 | tf_op jit(solution)/shard_map/ppermute | solution.py:249
  389.9 48.9 %collective-permute-start.15 = (bf16[256,2048]{1,0:T(8,128)(2,1)}, bf16[256,2048]{1,0:T(8,128)(2,1)}, u32[]{:S(2)}, u32[]{:S(2)}) collective-permute-start(bf16[256,2048]{1,0:T(8,128)(2,1)} %multiply_convert_fusion.3), channel_id=1, source_target_pairs={{0,4},{2,6},{4,0},{6,2},{1,5},{3,7},{5,1},{7,3},{8,12},{10,14},{12... | collective-permute-start | bytes 3145736 | tf_op jit(solution)/shard_map/ppermute | solution.py:249
  391.4 47.4 %collective-permute-start.16 = (bf16[256,2048]{1,0:T(8,128)(2,1)}, bf16[256,2048]{1,0:T(8,128)(2,1)}, u32[]{:S(2)}, u32[]{:S(2)}) collective-permute-start(bf16[256,2048]{1,0:T(8,128)(2,1)} %multiply_convert_fusion.3), channel_id=1, source_target_pairs={{0,6},{2,4},{4,2},{6,0},{1,7},{3,5},{5,3},{7,1},{8,14},{10,12},{12... | collective-permute-start | bytes 3145736 | tf_op jit(solution)/shard_map/ppermute | solution.py:249
  396.2 63.9 %collective-permute-start.25 = (bf16[256,2048]{1,0:T(8,128)(2,1)}, bf16[256,2048]{1,0:T(8,128)(2,1)}, u32[]{:S(2)}, u32[]{:S(2)}) collective-permute-start(bf16[256,2048]{1,0:T(8,128)(2,1)} %get-tuple-element.148), channel_id=1, source_target_pairs={{0,2},{2,0},{4,6},{6,4},{1,3},{3,1},{5,7},{7,5},{8,10},{10,8},{12,... | collective-permute-start | bytes 3145736 | tf_op jit(solution)/shard_map/ppermute | solution.py:249
  397.7 84.7 %collective-permute-start.26 = (bf16[256,2048]{1,0:T(8,128)(2,1)}, bf16[256,2048]{1,0:T(8,128)(2,1)}, u32[]{:S(2)}, u32[]{:S(2)}) collective-permute-start(bf16[256,2048]{1,0:T(8,128)(2,1)} %get-tuple-element.148), channel_id=1, source_target_pairs={{0,4},{2,6},{4,0},{6,2},{1,5},{3,7},{5,1},{7,3},{8,12},{10,14},{12... | collective-permute-start | bytes 3145736 | tf_op jit(solution)/shard_map/ppermute | solution.py:249
  414.8 67.5 %collective-permute-start.27 = (bf16[256,2048]{1,0:T(8,128)(2,1)}, bf16[256,2048]{1,0:T(8,128)(2,1)}, u32[]{:S(2)}, u32[]{:S(2)}) collective-permute-start(bf16[256,2048]{1,0:T(8,128)(2,1)} %get-tuple-element.148), channel_id=1, source_target_pairs={{0,6},{2,4},{4,2},{6,0},{1,7},{3,5},{5,3},{7,1},{8,14},{10,12},{12... | collective-permute-start | bytes 3145736 | tf_op jit(solution)/shard_map/ppermute | solution.py:249
  507.5 27.1 %collective-permute-start.28 = (bf16[256,2048]{1,0:T(8,128)(2,1)S(1)}, bf16[256,2048]{1,0:T(8,128)(2,1)S(1)}, u32[]{:S(2)}, u32[]{:S(2)}) collective-permute-start(bf16[256,2048]{1,0:T(8,128)(2,1)S(1)} %convolution_convert_fusion.10), channel_id=1, source_target_pairs={{0,6},{2,4},{4,2},{6,0},{1,7},{3,5},{5,3},{7,1},{8,14},{10,12},{12... | collective-permute-start | bytes 3145736 | tf_op jit(solution)/shard_map/ppermute | solution.py:249
  516.9 38.1 %collective-permute-start.29 = (bf16[256,2048]{1,0:T(8,128)(2,1)S(1)}, bf16[256,2048]{1,0:T(8,128)(2,1)S(1)}, u32[]{:S(2)}, u32[]{:S(2)}) collective-permute-start(bf16[256,2048]{1,0:T(8,128)(2,1)S(1)} %convolution_convert_fusion.9), channel_id=1, source_target_pairs={{0,2},{2,0},{4,6},{6,4},{1,3},{3,1},{5,7},{7,5},{8,10},{10,8},{12,... | collective-permute-start | bytes 3145736 | tf_op jit(solution)/shard_map/ppermute | solution.py:249
  526.3 29.7 %collective-permute-start.30 = (bf16[256,2048]{1,0:T(8,128)(2,1)S(1)}, bf16[256,2048]{1,0:T(8,128)(2,1)}, u32[]{:S(2)}, u32[]{:S(2)}) collective-permute-start(bf16[256,2048]{1,0:T(8,128)(2,1)S(1)} %convolution_convert_fusion.8), channel_id=1, source_target_pairs={{0,4},{2,6},{4,0},{6,2},{1,5},{3,7},{5,1},{7,3},{8,12},{10,14},{12... | collective-permute-start | bytes 3145736 | tf_op jit(solution)/shard_map/ppermute | solution.py:249
  567.9 47.6 %collective-permute-start.32 = (bf16[256,2048]{1,0:T(8,128)(2,1)}, bf16[256,2048]{1,0:T(8,128)(2,1)}, u32[]{:S(2)}, u32[]{:S(2)}) collective-permute-start(bf16[256,2048]{1,0:T(8,128)(2,1)} %get-tuple-element.72), channel_id=1, source_target_pairs={{0,4},{2,6},{4,0},{6,2},{1,5},{3,7},{5,1},{7,3},{8,12},{10,14},{12... | collective-permute-start | bytes 3145736 | tf_op jit(solution)/shard_map/ppermute | solution.py:249
  569.4 46.1 %collective-permute-start.33 = (bf16[256,2048]{1,0:T(8,128)(2,1)}, bf16[256,2048]{1,0:T(8,128)(2,1)}, u32[]{:S(2)}, u32[]{:S(2)}) collective-permute-start(bf16[256,2048]{1,0:T(8,128)(2,1)} %get-tuple-element.72), channel_id=1, source_target_pairs={{0,6},{2,4},{4,2},{6,0},{1,7},{3,5},{5,3},{7,1},{8,14},{10,12},{12... | collective-permute-start | bytes 3145736 | tf_op jit(solution)/shard_map/ppermute | solution.py:249
  580.4 144.3 %collective-permute-start.55 = (bf16[1024,1408]{1,0:T(8,128)(2,1)}, bf16[1024,1408]{1,0:T(8,128)(2,1)}, u32[]{:S(2)}, u32[]{:S(2)}) collective-permute-start(bf16[1024,1408]{1,0:T(8,128)(2,1)} %convolution_convert_fusion.2), channel_id=1, source_target_pairs={{0,1},{1,0},{2,3},{3,2},{4,5},{5,4},{6,7},{7,6},{8,9},{9,8},{10,11... | collective-permute-start | bytes 8650760 | tf_op jit(solution)/shard_map/ppermute | solution.py:245
  627.8 462.0 %reduce-scatter.11.cloned.1.call-start = ((), (), s32[]{:S(2)}) async-start(), calls=%async_computation.15 | async-start | bytes 3604480 | tf_op jit(solution)/shard_map/reduce_scatter | solution.py:315
  651.6 73.1 %collective-permute-start.35 = (f32[520,256]{1,0:T(8,128)}, f32[520,256]{1,0:T(8,128)S(1)}, u32[]{:S(2)}, u32[]{:S(2)}) collective-permute-start(f32[520,256]{1,0:T(8,128)} %pad_maximum_fusion.19), channel_id=1, source_target_pairs={{16,0},{24,8},{17,1},{25,9},{18,2},{26,10},{19,3},{27,11},{20,4},{... | collective-permute-start | bytes 1597448 | tf_op jit(solution)/shard_map/ppermute | solution.py:426
  653.0 71.7 %collective-permute-start.36 = (f32[520,256]{1,0:T(8,128)}, f32[520,256]{1,0:T(8,128)S(1)}, u32[]{:S(2)}, u32[]{:S(2)}) collective-permute-start(f32[520,256]{1,0:T(8,128)} %pad_maximum_fusion.19), channel_id=1, source_target_pairs={{8,0},{16,8},{24,16},{9,1},{17,9},{25,17},{10,2},{18,10},{26,18},{... | collective-permute-start | bytes 1597448 | tf_op jit(solution)/shard_map/ppermute | solution.py:426
  655.4 80.7 %collective-permute-start.34 = (f32[520,256]{1,0:T(8,128)}, f32[520,256]{1,0:T(8,128)}, u32[]{:S(2)}, u32[]{:S(2)}) collective-permute-start(f32[520,256]{1,0:T(8,128)} %pad_maximum_fusion.19), channel_id=1, source_target_pairs={{24,0},{25,1},{26,2},{27,3},{28,4},{29,5},{30,6},{31,7}} | collective-permute-start | bytes 1597448 | tf_op jit(solution)/shard_map/ppermute | solution.py:426
  732.0 363.9 %reduce-scatter.5.cloned.1.call-start = ((), (), s32[]{:S(2)}) async-start(), calls=%async_computation.12 | async-start | bytes 3932160 | tf_op jit(solution)/shard_map/reduce_scatter | solution.py:315
  780.6 29.9 %collective-permute-start.46 = (bf16[1024,1536]{1,0:T(8,128)(2,1)}, bf16[1024,1536]{1,0:T(8,128)(2,1)}, u32[]{:S(2)}, u32[]{:S(2)}) collective-permute-start(bf16[1024,1536]{1,0:T(8,128)(2,1)} %convolution_convert_fusion.3), channel_id=1, source_target_pairs={{0,1},{1,0},{2,3},{3,2},{4,5},{5,4},{6,7},{7,6},{8,9},{9,8},{10,11... | collective-permute-start | bytes 9437192 | tf_op jit(solution)/shard_map/ppermute | solution.py:245
  793.3 27.1 %collective-permute-start.21 = (bf16[256,2048]{1,0:T(8,128)(2,1)}, bf16[256,2048]{1,0:T(8,128)(2,1)S(1)}, u32[]{:S(2)}, u32[]{:S(2)}) collective-permute-start(bf16[256,2048]{1,0:T(8,128)(2,1)} %convolution_convert_fusion.19), channel_id=1, source_target_pairs={{0,6},{2,4},{4,2},{6,0},{1,7},{3,5},{5,3},{7,1},{8,14},{10,12},{12... | collective-permute-start | bytes 3145736 | tf_op jit(solution)/shard_map/ppermute | solution.py:249
  798.5 44.2 %collective-permute-start.22 = (bf16[256,2048]{1,0:T(8,128)(2,1)}, bf16[256,2048]{1,0:T(8,128)(2,1)}, u32[]{:S(2)}, u32[]{:S(2)}) collective-permute-start(bf16[256,2048]{1,0:T(8,128)(2,1)} %convolution_convert_fusion.18), channel_id=1, source_target_pairs={{0,2},{2,0},{4,6},{6,4},{1,3},{3,1},{5,7},{7,5},{8,10},{10,8},{12,... | collective-permute-start | bytes 3145736 | tf_op jit(solution)/shard_map/ppermute | solution.py:249
  801.9 40.8 %collective-permute-start.23 = (bf16[256,2048]{1,0:T(8,128)(2,1)}, bf16[256,2048]{1,0:T(8,128)(2,1)}, u32[]{:S(2)}, u32[]{:S(2)}) collective-permute-start(bf16[256,2048]{1,0:T(8,128)(2,1)} %convolution_convert_fusion.17), channel_id=1, source_target_pairs={{0,4},{2,6},{4,0},{6,2},{1,5},{3,7},{5,1},{7,3},{8,12},{10,14},{12... | collective-permute-start | bytes 3145736 | tf_op jit(solution)/shard_map/ppermute | solution.py:249
  810.5 78.6 %collective-permute-start.52 = (bf16[1024,2816]{1,0:T(8,128)(2,1)}, bf16[1024,2816]{1,0:T(8,128)(2,1)}, u32[]{:S(2)}, u32[]{:S(2)}) collective-permute-start(bf16[1024,2816]{1,0:T(8,128)(2,1)} %convolution_convert_fusion), channel_id=1, source_target_pairs={{0,1},{1,0},{2,3},{3,2},{4,5},{5,4},{6,7},{7,6},{8,9},{9,8},{10,11... | collective-permute-start | bytes 17301512 | tf_op jit(solution)/shard_map/ppermute | solution.py:245
  850.1 114.2 %all-to-all-start.1 = ((bf16[16,32,2048]{2,1,0:T(8,128)(2,1)}), bf16[16,32,2048]{2,1,0:T(8,128)(2,1)}, u32[]{:S(2)}, u32[]{:S(2)}) async-start(bf16[16,32,2048]{2,1,0:T(8,128)(2,1)} %bitcast.118), calls=%async_computation.1 | async-start | bytes 4194304 | tf_op jit(solution)/shard_map/all_to_all | solution.py:332
  872.7 237.2 %reduce-scatter.9.cloned.1.call-start = ((), (), s32[]{:S(2)}) async-start(), calls=%async_computation.14 | async-start | bytes 7208960 | tf_op jit(solution)/shard_map/reduce_scatter | solution.py:315
  879.7 46.8 %collective-permute-start.37 = (bf16[256,2176]{1,0:T(8,128)(2,1)S(1)}, bf16[256,2176]{1,0:T(8,128)(2,1)}, u32[]{:S(2)}, u32[]{:S(2)}) collective-permute-start(bf16[256,2176]{1,0:T(8,128)(2,1)S(1)} %pad_maximum_fusion.12), channel_id=1, source_target_pairs={{0,6},{2,4},{4,2},{6,0},{1,7},{3,5},{5,3},{7,1},{8,14},{10,12},{12... | collective-permute-start | bytes 3342344 | tf_op jit(solution)/shard_map/ppermute | solution.py:249
  885.5 70.4 %collective-permute-start.38 = (bf16[256,2176]{1,0:T(8,128)(2,1)}, bf16[256,2176]{1,0:T(8,128)(2,1)}, u32[]{:S(2)}, u32[]{:S(2)}) collective-permute-start(bf16[256,2176]{1,0:T(8,128)(2,1)} %pad_maximum_fusion.13), channel_id=1, source_target_pairs={{0,2},{2,0},{4,6},{6,4},{1,3},{3,1},{5,7},{7,5},{8,10},{10,8},{12,... | collective-permute-start | bytes 3342344 | tf_op jit(solution)/shard_map/ppermute | solution.py:249
  888.9 67.0 %collective-permute-start.39 = (bf16[256,2176]{1,0:T(8,128)(2,1)}, bf16[256,2176]{1,0:T(8,128)(2,1)}, u32[]{:S(2)}, u32[]{:S(2)}) collective-permute-start(bf16[256,2176]{1,0:T(8,128)(2,1)} %pad_maximum_fusion.14), channel_id=1, source_target_pairs={{0,4},{2,6},{4,0},{6,2},{1,5},{3,7},{5,1},{7,3},{8,12},{10,14},{12... | collective-permute-start | bytes 3342344 | tf_op jit(solution)/shard_map/ppermute | solution.py:249
  964.3 118.9 %all-to-all-start.3 = ((bf16[16,32,2048]{2,1,0:T(8,128)(2,1)}), bf16[16,32,2048]{2,1,0:T(8,128)(2,1)}, u32[]{:S(2)}, u32[]{:S(2)}) async-start(bf16[16,32,2048]{2,1,0:T(8,128)(2,1)} %bitcast.109), calls=%async_computation.3 | async-start | bytes 4194304 | tf_op jit(solution)/shard_map/all_to_all | solution.py:332
  978.2 73.8 %collective-permute-start.24 = (bf16[256,2048]{0,1:T(8,128)(2,1)S(1)}, bf16[256,2048]{0,1:T(8,128)(2,1)S(1)}, u32[]{:S(2)}, u32[]{:S(2)}) collective-permute-start(bf16[256,2048]{0,1:T(8,128)(2,1)S(1)} %bitcast.110), channel_id=1, source_target_pairs={{0,1},{1,0},{2,3},{3,2},{4,5},{5,4},{6,7},{7,6},{8,9},{9,8},{10,11... | collective-permute-start | bytes 3145736 | tf_op jit(solution)/shard_map/ppermute | solution.py:245
  999.2 47.7 %collective-permute-start.43 = (f32[215,256]{1,0:T(8,128)S(1)}, f32[215,256]{1,0:T(8,128)S(1)}, u32[]{:S(2)}, u32[]{:S(2)}) collective-permute-start(f32[215,256]{1,0:T(8,128)S(1)} %add.320), channel_id=1, source_target_pairs={{0,8},{8,0},{16,24},{24,16},{1,9},{9,1},{17,25},{25,17},{2,10},{10... | collective-permute-start | bytes 660488 | tf_op jit(solution)/shard_map/ppermute | solution.py:551
  1046.9 34.5 %collective-permute-start.44 = (f32[215,256]{1,0:T(8,128)S(1)}, f32[215,256]{1,0:T(8,128)S(1)}, u32[]{:S(2)}, u32[]{:S(2)}) collective-permute-start(f32[215,256]{1,0:T(8,128)S(1)} %add.321), channel_id=1, source_target_pairs={{0,16},{8,24},{16,0},{24,8},{1,17},{9,25},{17,1},{25,9},{2,18},{10... | collective-permute-start | bytes 660488 | tf_op jit(solution)/shard_map/ppermute | solution.py:551
  (99 other events, 2535.8 us)
Sparse Core Ops, SparseCore 0:
  25.7 107.1 all-gather.4
  135.1 28.5 all-gather.6
  165.8 136.6 all-gather.8
  304.0 78.2 all-gather.10
  627.9 75.4 reduce-scatter.6
  732.1 76.3 reduce-scatter.10
  817.2 103.0 reduce-scatter.4
  922.6 147.0 reduce-scatter.8

commit v2 on v1

v2 whole, which is shorter than its diff:
```python
import functools

import jax
import jax.numpy as jnp
from jax import lax
from jax.experimental import pallas as pl
from jax.experimental.pallas import tpu as pltpu
from jax.sharding import Mesh
from jax.sharding import PartitionSpec as P

SPAN = 64
HEAD_K = 256
HEAD_V = 512
GROUP = 4
MEMBER = 256
LANES = 128

eps = 1e-06
highest = lax.Precision.HIGHEST
contract_last = (((1,), (1,)), ((), ()))
contract_rows = (((0,), (0,)), ((), ()))
bf16 = jnp.bfloat16
f32 = jnp.float32


def rms_scale(values):
    return lax.rsqrt(jnp.mean(values * values, axis=-1, keepdims=True) + eps)


def layout_valid(starts, lengths, positions):
    begun = (positions[:, None] >= starts[None, :]).astype(jnp.int32)
    owner = jnp.sum(begun, axis=1) - 1
    ids = jnp.arange(starts.shape[0], dtype=jnp.int32)
    picked = (owner[:, None] == ids[None, :]).astype(jnp.int32)
    own_start = jnp.sum(picked * starts[None, :], axis=1)
    own_length = jnp.sum(picked * lengths[None, :], axis=1)
    return (positions - own_start < own_length).astype(f32)


def project(left, right):
    return jnp.dot(left, right, preferred_element_type=f32)


def project_back(left, right):
    return lax.dot_general(left, right, contract_last, preferred_element_type=f32)


def outer_sum(left, right):
    return lax.dot_general(left, right, contract_rows, preferred_element_type=f32)


def norm_back(grad_unit, unit, scaling):
    return scaling * (grad_unit - unit * jnp.mean(grad_unit * unit, axis=-1, keepdims=True))


def exact(left, right, dims):
    return lax.dot_general(left, right, dims, precision=highest, preferred_element_type=f32)


def brief(left, right, dims):
    return lax.dot_general(left.astype(bf16), right.astype(bf16), dims, preferred_element_type=f32)


plain = (((1,), (0,)), ((), ()))


def triangle(upper, size=SPAN):
    row = lax.broadcasted_iota(jnp.int32, (size, size), 0)
    col = lax.broadcasted_iota(jnp.int32, (size, size), 1)
    causal = col >= row if upper else row >= col
    if size > SPAN:
        causal = causal & (row // SPAN == col // SPAN)
    return jnp.where(causal, 1.0, 0.0).astype(f32)


def kept(resets, block):
    return jnp.where(resets[block] == 1, 0.0, 1.0)


def spans(reverse=False):
    count = MEMBER // SPAN
    return range(count - 1, -1, -1) if reverse else range(count)


def part(index):
    return slice(index * SPAN, (index + 1) * SPAN)


def states_kernel(order, resets, key_ref, value_ref, decay_ref, cumul_ref, left_ref, state, through):
    member = pl.program_id(0)

    @pl.when(member == 0)
    def _():
        state[...] = jnp.zeros_like(state)
        through[...] = jnp.ones_like(through)

    cumul_all = exact(triangle(False, MEMBER), decay_ref[...], plain)
    cumul_ref[...] = cumul_all
    current = state[...]
    passing = through[...]
    for i in spans():
        cumul = cumul_all[part(i)]
        last = cumul[SPAN - 1 : SPAN, :]
        faded = key_ref[part(i), :] * jnp.exp(last - cumul)
        fade = jnp.exp(last) * kept(resets, member * (MEMBER // SPAN) + i)
        current = current * fade + brief(value_ref[part(i), :], faded, contract_rows)
        passing = passing * fade
    state[...] = current
    through[...] = passing

    @pl.when(member == pl.num_programs(0) - 1)
    def _():
        left_ref[:HEAD_V, :] = current
        left_ref[HEAD_V:, :] = passing


def mix_kernel(
    order, resets, query_ref, key_ref, value_ref, gate_ref, cumul_ref, gain_ref, enter_ref,
    gated_ref, mixed_ref, saved_ref, state,
):
    member = pl.program_id(0)

    @pl.when(member == 0)
    def _():
        state[...] = enter_ref[...]

    causal = triangle(False)
    current = state[...]
    for i in spans():
        cumul = cumul_ref[part(i), :]
        last = cumul[SPAN - 1 : SPAN, :]
        key_rows = key_ref[part(i), :]
        value_rows = value_ref[part(i), :]
        lifted = query_ref[part(i), :] * (HEAD_K ** (-0.5)) * jnp.exp(cumul)
        lowered = key_rows * jnp.exp(-cumul)
        before = current * kept(resets, member * (MEMBER // SPAN) + i)
        saved_ref[i] = before
        scores = brief(lifted, lowered, contract_last) * causal
        mixed = brief(scores, value_rows, plain) + brief(lifted, before, contract_last)
        mixed_ref[part(i), :] = mixed
        faded = key_rows * jnp.exp(last - cumul)
        current = before * jnp.exp(last) + brief(value_rows, faded, contract_rows)
        square = jnp.mean(mixed * mixed, axis=-1, keepdims=True)
        unit = mixed * lax.rsqrt(jnp.maximum(square, 1.0))
        gate = gate_ref[part(i), :]
        gated_ref[part(i), :] = (unit * gain_ref[...] * (gate * jax.nn.sigmoid(gate))).astype(bf16)
    state[...] = current


def pull_kernel(
    order, resets, query_ref, gate_ref, cumul_ref, mixed_ref, grad_ref, gain_ref,
    d_mixed_ref, d_gate_ref, head_ref, pulled_ref, through,
):
    member = pl.program_id(0)

    @pl.when(member == 0)
    def _():
        through[...] = jnp.ones_like(through)
        pulled_ref[...] = jnp.zeros_like(pulled_ref)
        head_ref[...] = jnp.zeros_like(head_ref)

    gain = gain_ref[...]
    passing = through[...]
    reach = []
    for i in spans():
        cumul = cumul_ref[part(i), :]
        mixed = mixed_ref[part(i), :]
        gate = gate_ref[part(i), :]
        grad = grad_ref[part(i), :]
        square = jnp.mean(mixed * mixed, axis=-1, keepdims=True)
        scale = lax.rsqrt(jnp.maximum(square, 1.0))
        free = jnp.where(square > 1.0, 1.0, 0.0)
        unit = mixed * scale
        sig = jax.nn.sigmoid(gate)
        d_head = grad * (gate * sig)
        d_gate_ref[part(i), :] = (grad * (unit * gain) * sig * (1.0 + gate * (1.0 - sig))).astype(bf16)
        head_ref[...] += jnp.sum((d_head * unit).reshape(SPAN // 8, 8, HEAD_V), axis=0)
        scaled = d_head * gain
        d_mixed = scale * (scaled - free * unit * jnp.mean(scaled * unit, axis=-1, keepdims=True))
        d_mixed_ref[part(i), :] = d_mixed
        opened = passing * kept(resets, member * (MEMBER // SPAN) + i)
        lifted = query_ref[part(i), :] * (HEAD_K ** (-0.5)) * jnp.exp(cumul)
        reach.append(lifted * opened[:1, :])
        passing = opened * jnp.exp(cumul[SPAN - 1 : SPAN, :])
    pulled_ref[...] += brief(d_mixed_ref[...], jnp.concatenate(reach, axis=0), contract_rows)
    through[...] = passing


def back_kernel(
    order, resets, query_ref, key_ref, value_ref, cumul_ref, saved_ref, d_mixed_ref, d_gate_ref, later_ref,
    grads_ref, d_decay_ref, state,
):
    step = pl.program_id(0)
    member = pl.num_programs(0) - 1 - step

    @pl.when(step == 0)
    def _():
        state[...] = later_ref[...]

    causal = triangle(False)
    d_after = state[...]
    for i in spans(True):
        cumul = cumul_ref[part(i), :]
        last = cumul[SPAN - 1 : SPAN, :]
        key_rows = key_ref[part(i), :]
        value_rows = value_ref[part(i), :]
        d_mixed = d_mixed_ref[part(i), :]
        before = saved_ref[i]
        up = jnp.exp(cumul)
        down = jnp.exp(-cumul)
        rest = jnp.exp(last - cumul)
        lifted = query_ref[part(i), :] * (HEAD_K ** (-0.5)) * up
        lowered = key_rows * down
        faded = key_rows * rest
        scores = brief(lifted, lowered, contract_last) * causal
        d_scores = brief(d_mixed, value_rows, contract_last) * causal
        d_value = brief(scores, d_mixed, contract_rows) + brief(faded, d_after, contract_last)
        d_lifted = brief(d_scores, lowered, plain) + brief(d_mixed, before, plain)
        d_lowered = brief(d_scores, lifted, contract_rows)
        d_faded = brief(value_rows, d_after, plain)
        leak = d_faded * faded
        d_cumul = d_lifted * lifted - d_lowered * lowered - leak
        d_last = jnp.sum(leak, axis=0, keepdims=True) + jnp.exp(last) * jnp.sum(
            before * d_after, axis=0, keepdims=True
        )
        d_decay_ref[part(i), :] = exact(triangle(True), d_cumul, plain) + d_last
        grads_ref[part(i), :HEAD_K] = (d_lifted * up * (HEAD_K ** (-0.5))).astype(bf16)
        grads_ref[part(i), HEAD_K : 2 * HEAD_K] = (d_lowered * down + d_faded * rest).astype(bf16)
        grads_ref[part(i), 2 * HEAD_K : 2 * HEAD_K + HEAD_V] = d_value.astype(bf16)
        grads_ref[part(i), 2 * HEAD_K + HEAD_V :] = d_gate_ref[part(i), :]
        d_before = brief(d_mixed, lifted, contract_rows) + d_after * jnp.exp(last)
        d_after = d_before * kept(resets, member * (MEMBER // SPAN) + i)
    state[...] = d_after


def deal_kernel(devices, per_device, spread, pieces, n_weights, n_shares, *refs):
    refs = list(refs)
    value_ref = refs.pop(0)
    block_ref = refs.pop(0) if spread else None
    weight_refs, refs = refs[:n_weights], refs[n_weights:]
    got_ref = refs.pop(0)
    plane_ref = refs.pop(0) if spread else None
    share_refs, refs = refs[:n_shares], refs[n_shares:]
    send_sem, arrive_sem, own_sem, give_sem, take_sem = refs[:5]
    o, t, c = (lax.axis_index("o"), lax.axis_index("t"), lax.axis_index("c"))
    me = o * GROUP + t
    shard = weight_refs[0].shape[0]
    mesh_ids = pl.DeviceIdType.MESH
    barrier = pltpu.get_barrier_semaphore()

    def place(turn):
        peer = lax.rem(me + turn, devices)
        return peer, (lax.div(peer, GROUP), lax.rem(peer, GROUP), c)

    def greet(turn, carry):
        _, there = place(turn)
        pl.semaphore_signal(barrier, inc=1, device_id=there, device_id_type=mesh_ids)
        return carry

    def parcel(turn):
        peer, there = place(turn)
        return pltpu.make_async_remote_copy(
            src_ref=value_ref.at[pl.ds(peer * per_device, per_device)],
            dst_ref=got_ref.at[pl.ds(me * per_device, per_device)],
            send_sem=send_sem.at[turn - 1],
            recv_sem=arrive_sem.at[turn - 1],
            device_id=there,
            device_id_type=mesh_ids,
        )

    def send(turn, carry):
        parcel(turn).start()
        return carry

    def receive(turn, carry):
        parcel(turn).wait()
        return carry

    def share(number, which, turn):
        weight, out, column, size = pieces[number]
        return (
            weight_refs[weight].at[:, pl.ds(which * size if weight_refs[weight].shape[1] > size else 0, size)],
            share_refs[out].at[pl.ds(turn * shard, shard), pl.ds(column, size)],
        )

    def given(number, which):
        source, target = share(number, which, lax.rem(t, 2))
        return pltpu.make_async_remote_copy(
            src_ref=source,
            dst_ref=target,
            send_sem=give_sem.at[which, number],
            recv_sem=take_sem.at[lax.rem(t, 2), number],
            device_id=(o, 2 * c + which, lax.div(t, 2)),
            device_id_type=mesh_ids,
        )

    def held(number, which):
        source, target = share(number, which, lax.rem(t, 2))
        return pltpu.make_async_copy(source, target, give_sem.at[which, number])

    def taken(number, turn):
        source, target = share(number, 0, turn)
        return pltpu.make_async_remote_copy(
            src_ref=source,
            dst_ref=target,
            send_sem=give_sem.at[0, number],
            recv_sem=take_sem.at[turn, number],
            device_id=(o, lax.rem(t + 1, GROUP), c),
            device_id_type=mesh_ids,
        )

    lax.fori_loop(1, devices, greet, 0)
    for turn in range(GROUP):
        there = (o, lax.rem(t + turn, GROUP), 1 - c)
        pl.semaphore_signal(barrier, inc=1, device_id=there, device_id_type=mesh_ids)
    pl.semaphore_wait(barrier, devices - 1 + GROUP)
    blocks = []
    if spread:
        out_sem, in_sem = refs[5:]
        mates = (t + 1 - 2 * lax.rem(t, 2), lax.rem(t + 2, GROUP), GROUP - 1 - t)
        for slot, mate in enumerate(mates):
            blocks.append(
                pltpu.make_async_remote_copy(
                    src_ref=block_ref,
                    dst_ref=plane_ref.at[slot],
                    send_sem=out_sem.at[slot],
                    recv_sem=in_sem.at[slot],
                    device_id=(o, mate, c),
                    device_id_type=mesh_ids,
                )
            )
            blocks[-1].start()
    lax.fori_loop(1, devices, send, 0)
    for which in range(2):
        own = t == 2 * c + which

        @pl.when(own)
        def _():
            for number in range(len(pieces)):
                held(number, which).start()

        @pl.when(jnp.logical_not(own))
        def _():
            for number in range(len(pieces)):
                given(number, which).start()

    rows = pl.ds(me * per_device, per_device)
    keep = pltpu.make_async_copy(value_ref.at[rows], got_ref.at[rows], own_sem)
    keep.start()
    keep.wait()
    for block in blocks:
        block.wait()
    for which in range(2):
        own = t == 2 * c + which

        @pl.when(own)
        def _():
            for number in range(len(pieces)):
                held(number, which).wait()

        @pl.when(jnp.logical_not(own))
        def _():
            for number in range(len(pieces)):
                given(number, which).wait_send()
                taken(number, which).wait_recv()

    lax.fori_loop(1, devices, receive, 0)


def deal(value, devices, weights, shares, pieces, block=None):
    spread = block is not None
    count = pltpu.SemaphoreType.DMA((devices - 1,))
    few = pltpu.SemaphoreType.DMA((GROUP - 1,))
    pairs = pltpu.SemaphoreType.DMA((2, len(pieces)))
    anywhere = pl.BlockSpec(memory_space=pl.ANY)
    inside = pl.BlockSpec(memory_space=pltpu.VMEM)
    outs = [jax.ShapeDtypeStruct(value.shape, value.dtype)]
    if spread:
        outs.append(jax.ShapeDtypeStruct((GROUP - 1,) + block.shape, block.dtype))
    outs += [jax.ShapeDtypeStruct((2 * weights[0].shape[0], size), bf16) for size in shares]
    kernel = functools.partial(
        deal_kernel, devices, value.shape[0] // devices, spread, pieces, len(weights), len(shares)
    )
    return pl.pallas_call(
        kernel,
        out_shape=outs,
        in_specs=[anywhere] * (2 if spread else 1) + [inside] * len(weights),
        out_specs=[anywhere] * len(outs),
        scratch_shapes=[count, count, pltpu.SemaphoreType.DMA, pairs, pairs]
        + ([few, few] if spread else []),
        compiler_params=pltpu.CompilerParams(
            collective_id=2 if spread else 1, has_side_effects=True, vmem_limit_bytes=24 << 20
        ),
        cost_estimate=pl.CostEstimate(flops=0, bytes_accessed=150 << 20, transcendentals=0),
    )(*([value, block] if spread else [value]), *weights)


def rows_of(width, column=0, backward=False):
    def place(step, order, resets):
        at = order.shape[0] - 1 - step if backward else step
        return (order[at], column)

    return pl.BlockSpec((MEMBER, width), place)


def saved_of(backward=False):
    def place(step, order, resets):
        at = order.shape[0] - 1 - step if backward else step
        return (order[at], 0, 0)

    return pl.BlockSpec((MEMBER // SPAN, HEAD_V, HEAD_K), place)


def whole_of(shape):
    return pl.BlockSpec(shape, lambda step, order, resets: (0,) * len(shape))


def over_blocks(kernel, order, resets, operands, in_specs, outs, out_specs, scratch, flops, moved):
    return pl.pallas_call(
        kernel,
        out_shape=outs,
        grid_spec=pltpu.PrefetchScalarGridSpec(
            num_scalar_prefetch=2,
            grid=(order.shape[0],),
            in_specs=in_specs,
            out_specs=out_specs,
            scratch_shapes=scratch,
        ),
        compiler_params=pltpu.CompilerParams(
            dimension_semantics=("arbitrary",), vmem_limit_bytes=40 << 20
        ),
        cost_estimate=pl.CostEstimate(flops=flops, bytes_accessed=moved, transcendentals=0),
    )(order, resets, *operands)


def shape_of(shape, dtype=f32):
    return jax.ShapeDtypeStruct(shape, dtype)


def swapped(value):
    return lax.ppermute(value, "c", [(0, 1), (1, 0)])


def neighbour(value, distance):
    return lax.ppermute(value, "t", [(i, i ^ distance) for i in range(GROUP)])


def plane_gather(value):
    middle = value.shape[0] // 2
    near = neighbour(value, 1)
    far = neighbour(value, 2)
    upper = neighbour(near[:middle], 2)
    lower = neighbour(far[middle:], 1)
    return jnp.concatenate([value, near, far, upper, lower], axis=0)


def plane_sum(produce, hold=None):
    across = produce(3, 4).astype(bf16)
    middle = across.shape[0] // 2
    upper = neighbour(across[:middle], 1)
    lower = neighbour(across[middle:], 2)
    sides = produce(1, 3)
    near, far = (sides[: 2 * middle], sides[2 * middle :])
    if hold is not None:
        upper, lower, hold = lax.optimization_barrier((upper, lower, hold))
    near_upper = neighbour(near[:middle].astype(bf16), 1)
    far_lower = neighbour(far[middle:].astype(bf16), 2)
    near_lower = neighbour((near[middle:] + lower.astype(f32)).astype(bf16), 1)
    far_upper = neighbour((far[:middle] + upper.astype(f32)).astype(bf16), 2)
    arrived_near = jnp.concatenate([near_upper, near_lower], axis=0)
    arrived_far = jnp.concatenate([far_upper, far_lower], axis=0)
    total = produce(0, 1) + arrived_near.astype(f32) + arrived_far.astype(f32)
    return total if hold is None else (total, hold)


def deal_pairs(turn):
    pairs = []
    for t in range(GROUP):
        for c in range(2):
            pairs.append((t * 2 + c, (2 * c + (t + turn) % 2) * 2 + t // 2))
    return pairs


def local(
    layer_input, cotangent, teacher, target_slot, seq_start, seq_len,
    w_query, w_key, w_value, w_gate_out, w_out, w_ffn_gate, w_ffn_up, w_ffn_down,
    w_rank_down, w_rank_up, decay_bias, gain_attn, gain_ffn, gain_head,
):
    planes = lax.axis_size("o")
    devices = planes * GROUP
    o, t, c = (lax.axis_index("o"), lax.axis_index("t"), lax.axis_index("c"))
    even = t % 2 == 0
    _, rows, width = layer_input.shape
    shard = w_query.shape[0]
    rank = w_rank_down.shape[1]
    hidden_here = w_ffn_gate.shape[1] // 2
    tokens = GROUP * rows
    blocks = tokens // SPAN
    pair = 2 * rows // devices
    half = width // 2

    def mine(value):
        return lax.dynamic_index_in_dim(value, c, 0, keepdims=False)

    def arranged(value):
        shaped = value.reshape(value.shape[0], planes, 2, 2 * shard)
        return shaped.transpose(0, 2, 1, 3).reshape(value.shape)

    def restored(value):
        shaped = value.reshape(value.shape[0], 2, planes, 2 * shard)
        return shaped.transpose(0, 2, 1, 3).reshape(value.shape)

    def either(first, second):
        return (jnp.where(even, first, second), jnp.where(even, second, first))

    def fetch(block):
        return lax.all_gather(block, ("c", "o"), axis=0, tiled=True)

    def over_cores(left, right):
        theirs = lax.dynamic_slice_in_dim(left, (1 - c) * half, half, 1)
        ours = lax.dynamic_slice_in_dim(left, c * half, half, 1)
        arrived = swapped(outer_sum(theirs, right).astype(bf16))
        return (outer_sum(ours, right) + arrived.astype(f32)).astype(bf16)

    def over_planes(total):
        return lax.psum_scatter(total, "o", scatter_dimension=0, tiled=True)

    def deliver(part_sum):
        sent = either(part_sum[:shard], part_sum[shard:])
        got = [lax.ppermute(sent[turn], ("t", "c"), deal_pairs(turn)) for turn in range(2)]
        return [piece.astype(f32) for piece in either(*got)]

    def own_columns(value):
        count = value.shape[0]

        def keep_half(array, axis, bit, pass_on):
            kept_half = lax.dynamic_index_in_dim(array, bit, axis, keepdims=False)
            given = lax.dynamic_index_in_dim(array, 1 - bit, axis, keepdims=False)
            return kept_half + pass_on(given)

        value = value.reshape(count, 2, planes, 2, shard)
        value = keep_half(value, 1, t // 2, lambda given: neighbour(given, 2))
        value = keep_half(value, 2, t % 2, lambda given: neighbour(given, 1))
        span = planes
        while span > 1:
            span //= 2
            hops = [(i, i ^ span) for i in range(planes)]
            value = value.reshape(count, 2, span, shard)
            value = keep_half(value, 1, (o // span) % 2, lambda given: lax.ppermute(given, "o", hops))
        value = value.reshape(count, shard)
        return value + swapped(value)

    targets = mine(target_slot)
    destination = targets // rows
    offset = targets % rows
    ids = jnp.arange(devices, dtype=jnp.int32)
    matches = (destination[:, None] == ids[None, :]).astype(bf16)
    index = jnp.arange(rows, dtype=jnp.int32)
    earlier = (index[:, None] > index[None, :]).astype(bf16)
    arrival = jnp.sum(project(earlier, matches) * matches.astype(f32), axis=1).astype(jnp.int32)
    slot = destination * pair + arrival
    pack = (jnp.arange(devices * pair, dtype=jnp.int32)[:, None] == slot[None, :]).astype(bf16)

    def exchange(value):
        return lax.all_to_all(value, ("o", "t"), split_axis=0, concat_axis=0, tiled=True)

    tag = jnp.pad((offset + 1).astype(bf16)[:, None], ((0, 0), (0, LANES - 1)))
    home_in = jnp.concatenate([arranged(mine(layer_input)), tag], axis=1)
    packed_in = project(pack, home_in).astype(bf16)

    extras = jnp.concatenate(
        [
            w_rank_down,
            gain_attn[:, None],
            gain_ffn[:, None],
            jnp.zeros((shard, LANES - rank - 2), bf16),
        ],
        axis=1,
    )
    wide_first = 2 * HEAD_K + 2 * HEAD_V
    got_in, first_block, out_block = deal(
        packed_in,
        devices,
        (w_query, w_key, w_value, w_gate_out, extras, w_out),
        (wide_first + LANES, HEAD_V),
        (
            (0, 0, 0, HEAD_K),
            (1, 0, HEAD_K, HEAD_K),
            (2, 0, 2 * HEAD_K, HEAD_V),
            (3, 0, 2 * HEAD_K + HEAD_V, HEAD_V),
            (4, 0, wide_first, LANES),
            (5, 1, 0, HEAD_V),
        ),
    )
    got_tag = got_in[:, width].astype(jnp.int32) - 1
    unpack = (got_tag[:, None] == index[None, :]).astype(bf16)
    layout_in = outer_sum(unpack, got_in[:, :width]).astype(bf16)
    packed_grad = project(pack, arranged(mine(cotangent))).astype(bf16)
    packed_grad, packed_in = lax.optimization_barrier((packed_grad, packed_in))
    got_grad, others, gate_up_block, down_block = deal(
        packed_grad,
        devices,
        (w_ffn_gate, w_ffn_up, w_ffn_down),
        (2 * hidden_here, hidden_here),
        ((0, 0, 0, hidden_here), (1, 0, hidden_here, hidden_here), (2, 1, 0, hidden_here)),
        layout_in,
    )
    w_first = fetch(first_block)
    wo = fetch(out_block)
    rank_down = w_first[:, wide_first : wide_first + rank]
    gain_one = w_first[:, wide_first + rank].astype(f32)
    gain_two = w_first[:, wide_first + rank + 1].astype(f32)
    ranked = jnp.concatenate([w_rank_up, decay_bias[None, :]], axis=0)
    other_ranked = swapped(ranked)
    ranked = jnp.where(t // 2 == c, ranked, other_ranked).astype(f32)
    ranked = jnp.where(even, ranked[:, :HEAD_K], ranked[:, HEAD_K:])
    rank_up, bias = (ranked[:rank], ranked[rank])
    head_gain = gain_head.astype(f32)[None, :]

    starts, lengths = (mine(seq_start), mine(seq_len))
    own_positions = (o * GROUP + t) * rows + index
    own_valid = layout_valid(starts, lengths, own_positions)[:, None]
    block_ids = jnp.arange(blocks, dtype=jnp.int32)
    block_first = o * tokens + block_ids * SPAN
    resets = jnp.any(block_first[:, None] == starts[None, :], axis=1).astype(jnp.int32)
    order = jnp.arange(GROUP, dtype=jnp.int32) ^ t

    inputs = layout_in.astype(f32)
    scale_one = rms_scale(inputs)
    unit_one = inputs * scale_one
    plane_in = jnp.concatenate([layout_in, others.reshape(-1, width)], axis=0).astype(f32)
    normed = (plane_in * rms_scale(plane_in) * gain_one).astype(bf16)
    projected = project(normed, w_first)
    rank_rows = projected[:, wide_first : wide_first + rank]
    logits = jnp.dot(rank_rows, rank_up, precision=highest) + bias
    decays = jax.nn.log_sigmoid(logits) / 16.0
    state_shape = pltpu.VMEM((HEAD_V, HEAD_K), f32)
    through_shape = pltpu.VMEM((8, HEAD_K), f32)
    key_spec = functools.partial(rows_of, HEAD_K, 1)
    value_spec = functools.partial(rows_of, HEAD_V, 1)
    gate_spec = functools.partial(rows_of, HEAD_V, 2)
    narrow = functools.partial(rows_of, HEAD_K, 0)
    broad = functools.partial(rows_of, HEAD_V, 0)
    projected, got_grad = lax.optimization_barrier((projected, got_grad))
    cumul, left = over_blocks(
        states_kernel, order, resets,
        (projected, projected, decays),
        [key_spec(), value_spec(), narrow()],
        (shape_of((tokens, HEAD_K)), shape_of((HEAD_V + 8, HEAD_K))),
        (narrow(), whole_of((HEAD_V + 8, HEAD_K))),
        [state_shape, through_shape],
        1 << 30, 6 << 20,
    )
    leaving, through = (left[:HEAD_V], left[HEAD_V : HEAD_V + 1])

    def shifted(value, distance):
        reach = planes - abs(distance)
        if distance > 0:
            hops = [(i, i + distance) for i in range(reach)]
        else:
            hops = [(i - distance, i) for i in range(reach)]
        return lax.ppermute(value, "o", hops)

    through_high = through.astype(bf16)
    through_low = (through - through_high.astype(f32)).astype(bf16)

    def carried(value, sign):
        packed = jnp.concatenate([value.astype(bf16), through_high, through_low], axis=0)
        passed = [shifted(packed, sign * d).astype(f32) for d in range(1, planes)]
        running = passed[-1][:HEAD_V]
        for nearer in passed[-2::-1]:
            running = running * (nearer[HEAD_V : HEAD_V + 1] + nearer[HEAD_V + 1 :]) + nearer[:HEAD_V]
        return running

    entering = carried(leaving, 1)
    layout_grad = outer_sum(unpack, got_grad).astype(bf16)
    upstream = layout_grad.astype(f32) * own_valid
    ffn_grad = plane_gather(upstream.astype(bf16))
    entering, ffn_grad, gate_up_block, down_block = lax.optimization_barrier(
        (entering, ffn_grad, gate_up_block, down_block)
    )
    w_gate_up = fetch(gate_up_block)
    w_down = fetch(down_block)
    gated, mixed, saved = over_blocks(
        mix_kernel, order, resets,
        (projected, projected, projected, projected, cumul, head_gain, entering),
        [narrow(), key_spec(), value_spec(), gate_spec(), narrow(), whole_of((1, HEAD_V)), whole_of((HEAD_V, HEAD_K))],
        (shape_of((tokens, HEAD_V), bf16), shape_of((tokens, HEAD_V)), shape_of((blocks, HEAD_V, HEAD_K))),
        (broad(), broad(), saved_of()),
        [state_shape],
        4 << 30, 16 << 20,
    )

    def members(value, first, last):
        return value[first * rows : last * rows]

    attended = plane_sum(lambda *d: project_back(members(gated, *d), wo))
    hidden = inputs + attended

    scale_two = rms_scale(hidden)
    unit_two = hidden * scale_two
    normed_two = plane_gather((unit_two * gain_two).astype(bf16))
    gate_up = project(normed_two, w_gate_up)
    gating, upward = (gate_up[:, :hidden_here], gate_up[:, hidden_here:])
    up_sig = jax.nn.sigmoid(gating)
    gate_silu = gating * up_sig
    product = (gate_silu * upward).astype(bf16)
    d_product = project(ffn_grad, w_down)
    d_gating = d_product * upward * up_sig * (1.0 + gating * (1.0 - up_sig))
    d_upward = d_product * gate_silu
    d_gate_up = jnp.concatenate([d_gating.astype(bf16), d_upward.astype(bf16)], axis=1)
    total_down = over_cores(ffn_grad, product)

    def second_part(*d):
        nonlocal total_down
        piece = project_back(members(d_gate_up, *d), w_gate_up)
        if d[0] == 1:
            piece, total_down = lax.optimization_barrier((piece, total_down))
        return piece

    d_normed_two = plane_sum(second_part)
    total_gate_up = over_cores(normed_two, d_gate_up)
    d_normed_two, total_gate_up = lax.optimization_barrier((d_normed_two, total_gate_up))
    part_down = over_planes(total_down)
    part_gate_up = over_planes(total_gate_up)
    grad_gain_two = jnp.sum(d_normed_two * unit_two, axis=0)
    d_hidden = upstream + norm_back(d_normed_two * gain_two, unit_two, scale_two)

    attn_grad = plane_gather(d_hidden.astype(bf16))
    attn_grad, part_down = lax.optimization_barrier((attn_grad, part_down))
    d_gated = project(attn_grad, wo)
    part_out = over_planes(over_cores(attn_grad, gated))
    product, d_gated = lax.optimization_barrier((product, d_gated))
    ffn_out = plane_sum(lambda *d: project_back(members(product, *d), w_down))
    result = ((hidden + ffn_out) * own_valid).astype(bf16)

    def both(value):
        other = swapped(value)
        return jnp.stack([jnp.where(c == 0, value, other), jnp.where(c == 0, other, value)])

    def outward(value):
        return exchange(project(unpack, value).astype(bf16))

    def homeward(value):
        return restored(outer_sum(pack, value).astype(bf16))

    d_mixed, d_gate_pre, head_part, pulled = over_blocks(
        pull_kernel, order, resets,
        (projected, projected, cumul, mixed, d_gated, head_gain),
        [narrow(), gate_spec(), narrow(), broad(), broad(), whole_of((1, HEAD_V))],
        (
            shape_of((tokens, HEAD_V)),
            shape_of((tokens, HEAD_V), bf16),
            shape_of((8, HEAD_V)),
            shape_of((HEAD_V, HEAD_K)),
        ),
        (broad(), broad(), whole_of((8, HEAD_V)), whole_of((HEAD_V, HEAD_K))),
        [through_shape],
        1 << 30, 12 << 20,
    )
    later = carried(pulled, -1)
    later, result, part_gate_up = lax.optimization_barrier((later, result, part_gate_up))
    back_output = outward(result)
    grads, d_decays = over_blocks(
        back_kernel, order, resets,
        (projected, projected, projected, cumul, saved, d_mixed, d_gate_pre, later),
        [
            narrow(backward=True), key_spec(backward=True), value_spec(backward=True), narrow(backward=True),
            saved_of(True), broad(backward=True), broad(backward=True), whole_of((HEAD_V, HEAD_K)),
        ],
        (shape_of((tokens, wide_first), bf16), shape_of((tokens, HEAD_K))),
        (rows_of(wide_first, 0, True), narrow(backward=True)),
        [state_shape],
        8 << 30, 24 << 20,
    )
    d_logits = d_decays / 16.0 * jax.nn.sigmoid(-logits)
    grad_rank_up = lax.dot_general(rank_rows, d_logits, contract_rows, precision=highest)
    grad_bias = jnp.sum(d_logits, axis=0, keepdims=True)
    rank_part = lax.dot_general(d_logits, rank_up, contract_last, precision=highest)
    rank_part = jnp.pad(rank_part, ((0, 0), (0, LANES - rank)))

    total_first = over_cores(normed, grads)

    def first_part(*d):
        nonlocal total_first
        product_part = project_back(members(grads, *d), w_first[:, :wide_first])
        piece = jnp.concatenate([product_part, members(rank_part, *d)], axis=1)
        if d[0] == 1:
            piece, total_first = lax.optimization_barrier((piece, total_first))
        return piece

    summed, back_output = plane_sum(first_part, back_output)
    part_first = over_planes(total_first)
    summed, part_out = lax.optimization_barrier((summed, part_out))
    own_output = homeward(back_output)
    both_output = both(own_output)
    grad_down = deliver(part_down)
    grad_gate_up = deliver(part_gate_up)
    grad_out = deliver(part_out)
    rank_grad = summed[:, width : width + rank].astype(bf16)
    d_normed = summed[:, :width] + project_back(rank_grad, rank_down)
    grad_gain_one = jnp.sum(d_normed * unit_one, axis=0)
    d_inputs = d_hidden + norm_back(d_normed * gain_one, unit_one, scale_one)
    back_input = outward(d_inputs.astype(bf16))
    own_normed = (unit_one * gain_one).astype(bf16)
    wide_rows = jnp.concatenate(
        [outer_sum(rank_grad, own_normed), grad_gain_one[None], grad_gain_two[None]], axis=0
    )
    own_wide = own_columns(wide_rows)

    home_valid = layout_valid(starts, lengths, targets)[:, None]
    difference = own_output.astype(f32) - mine(teacher).astype(f32)
    loss_part = jnp.sum(home_valid * difference * difference)
    small = jnp.concatenate([grad_rank_up, grad_bias], axis=0)
    member_ids = jnp.arange(GROUP, dtype=jnp.int32)[:, None, None]
    small = jnp.where(member_ids == t, small[None], 0.0).reshape(-1, HEAD_K)
    everything = jnp.concatenate(
        [
            small,
            jnp.sum(head_part, axis=0).reshape(-1, HEAD_K),
            jnp.full((1, HEAD_K), loss_part, f32),
        ],
        axis=0,
    )
    everything = everything + swapped(everything)
    for distance in (1, 2):
        everything = everything + neighbour(everything, distance)
    distance = 1
    while distance < planes:
        hops = [(i, i ^ distance) for i in range(planes)]
        everything = everything + lax.ppermute(everything, "o", hops)
        distance *= 2
    back_input, part_first, own_wide, everything, grad_down, grad_gate_up, grad_out, both_output = (
        lax.optimization_barrier(
            (back_input, part_first, own_wide, everything, grad_down, grad_gate_up, grad_out, both_output)
        )
    )
    used = GROUP * (rank + 1)
    summed_small = everything[:used].reshape(GROUP, rank + 1, HEAD_K)
    pair_small = lax.dynamic_slice_in_dim(summed_small, 2 * c, 2, 0)
    pair_small = jnp.concatenate([pair_small[0], pair_small[1]], axis=1)
    head_rows = HEAD_V // HEAD_K
    summed_head = everything[used : used + head_rows].reshape(-1)
    summed_loss = everything[used + head_rows, 0]
    own_input_grad = homeward(back_input)
    grad_first = deliver(part_first)
    loss = summed_loss / (jnp.sum(seq_len).astype(f32) * width)

    def columns(pair_of, start, size):
        return jnp.concatenate([piece[:, start : start + size] for piece in pair_of], axis=1)

    return (
        both_output,
        loss,
        both(own_input_grad),
        columns(grad_first, 0, HEAD_K),
        columns(grad_first, HEAD_K, HEAD_K),
        columns(grad_first, 2 * HEAD_K, HEAD_V),
        columns(grad_first, 2 * HEAD_K + HEAD_V, HEAD_V),
        columns(grad_out, 0, HEAD_V),
        columns(grad_gate_up, 0, hidden_here),
        columns(grad_gate_up, hidden_here, hidden_here),
        columns(grad_down, 0, hidden_here),
        own_wide[:rank].T,
        pair_small[:rank],
        pair_small[rank],
        own_wide[rank],
        own_wide[rank + 1],
        summed_head,
    )


def solution(mesh):
    seq = ("o", "t")
    count = mesh.devices.shape[0]
    split = Mesh(mesh.devices.reshape(count // GROUP, GROUP, 2), ("o", "t", "c"))
    tokens = P(None, seq, None)
    weight = P(seq, "c")
    placed = (
        (tokens, tokens, tokens, P(None, seq), P(), P())
        + (weight,) * 8
        + (P(seq, None), P(None, "c"), P("c"), P(seq), P(seq), P())
    )
    return jax.shard_map(
        local,
        mesh=split,
        in_specs=placed,
        out_specs=(tokens, P(), tokens)
        + (weight,) * 8
        + (P(seq, None), P(None, "c"), P("c"), P(seq), P(seq), P()),
        check_vma=False,
    )
```

time: 1150 us -> 965 us (0.84)
  waiting for transfers between devices: 578 us -> 320 us
  Pallas kernels: 89.9 us -> 189 us
  starting transfers between devices: 141 us -> 94.5 us
  local copies, waits for them, and re-layouts: 49.5 us -> 74.6 us
  other arithmetic: 54.3 us -> 68.3 us
  matrix products: 205 us -> 193 us
    pallas_call x0 -> x2, Pallas kernels: none -> 158 us  [deal(): pl.pallas_call(kernel, out_shape=outs, in_specs=[anywhere] * (2 if spread...]
    ppermute x26 -> x40, waiting for transfers between devices: 292 us -> 161 us  [neighbour(): return lax.ppermute(value, 't', [(i, i ^ distance) for i in range(GROUP)])]
    ppermute x6, waiting for transfers between devices: 115 us -> 41 us  [shifted(): return lax.ppermute(value, 'o', hops)]
    pallas_call x4, Pallas kernels: 89.9 us -> 31.2 us  [over_blocks(): pl.pallas_call(kernel, out_shape=outs, grid_spec=pltpu.PrefetchScalarGrid...]
    all_to_all x4 -> x2, waiting for transfers between devices: 58.1 us -> 0.01 us  [exchange(): lax.all_to_all(value, ('o', 't'), split_axis=0, concat_axis=0, tiled=True)]
    all_gather x4, waiting for transfers between devices: 0.03 us -> 57.5 us  [fetch(): return lax.all_gather(block, ('c', 'o'), axis=0, tiled=True)]
    all_to_all x4 -> x2, starting transfers between devices: 51.6 us -> 12.1 us  [exchange(): lax.all_to_all(value, ('o', 't'), split_axis=0, concat_axis=0, tiled=True)]
    ppermute x8 -> x2, waiting for transfers between devices: 20.5 us -> 1.19 us  [own_columns(): lax.ppermute(given, 'o', hops)]
  transfers between devices with their start and end apart: 70 -> 77, of which waited for: 34 -> 34; matrix products, arithmetic and copies ran while one was open for 21% -> 27% of each run, Pallas kernels for 8% -> 15%
where the time goes in v2:
time: 965 us; the launch traced here: 959 us
  waiting for transfers between devices  320 us (33%)
  matrix products  193 us (20%)
  Pallas kernels  189 us (20%)
  starting transfers between devices  94.5 us (10%)
  local copies, waits for them, and re-layouts  74.6 us (8%)
  other arithmetic  68.3 us (7%)
  between operations  18.9 us (2%)
    ppermute x40, waiting for transfers between devices, neighbour(): return lax.ppermute(value, 't', [(i, i ^ distance) for i in range(GROUP)])  161 us
    pallas_call x2, Pallas kernels, deal(): pl.pallas_call(kernel, out_shape=outs, in_specs=[anywhere] * (2 if spread...  158 us
    dot_general x13, matrix products, project_back(): lax.dot_general(left, right, contract_last, preferred_element_type=f32)  67.4 us
    dot_general x13, matrix products, outer_sum(): lax.dot_general(left, right, contract_rows, preferred_element_type=f32)  63.9 us
    all_gather x4, waiting for transfers between devices, fetch(): return lax.all_gather(block, ('c', 'o'), axis=0, tiled=True)  57.5 us
    dot_general x9, matrix products, project(): return jnp.dot(left, right, preferred_element_type=f32)  55.6 us
    ppermute x2, waiting for transfers between devices, local(): everything = everything + lax.ppermute(everything, 'o', hops)  54.1 us
    unnamed x210, local copies, waits for them, and re-layouts  43.4 us
  transfers between devices with their start and end apart: 77, of which 34 were waited for; matrix products, arithmetic and copies ran while one was open for 27% of the time, Pallas kernels for 15%

profile of v2, /device:TPU:0, one launch (start us, length us, event | category | flops | bytes accessed | tf_op | source)
XLA Modules:
  0.0 958.9 jit_solution(13699942621432494857)
XLA Ops:
  18.5 47.1 %shard_map.323 = (bf16[512,2176]{1,0:T(8,128)(2,1)S(1)}, bf16[256,1664]{1,0:T(8,128)(2,1)}, bf16[256,512]{1,0:T(8,128)(2,1)}) custom-call(bf16[512,2176]{1,0:T(8,128)(2,1)S(1)} %convolution_convert_fusion.1.refs_0_, bf16[128,512]{1,0:T(8,128)(2,1)S(1)} %copy-done.31, bf16[128,512]{1,0:T(8,128)(2,1)S(1)} %copy-done.32, bf16[128,1024]{1,0:T(8,128)(2,1)S(1)} %copy-done.28, ...), custom_call_target="tpu_custom_call" | custom-call | bytes 157286400 | tf_op jit(solution)/shard_map/pallas_call | solution.py:384
  74.0 110.8 %shard_map.324 = (bf16[512,2048]{1,0:T(8,128)(2,1)S(1)}, bf16[3,256,2048]{2,1,0:T(8,128)(2,1)S(1)}, bf16[256,2816]{1,0:T(8,128)(2,1)S(1)}, bf16[256,1408]{1,0:T(8,128)(2,1)S(1)}) custom-call(bf16[512,2048]{1,0:T(8,128)(2,1)S(1)} %convolution_convert_fusion.6.refs_0_, bf16[256,2048]{1,0:T(8,128)(2,1)S(1)} %get-tuple-element.244.refs_1_, ...), custom_call_target="tpu_custom_call" | custom-call | bytes 157286400 | tf_op jit(solution)/shard_map/pallas_call | solution.py:384
  198.6 7.8 fusion.161.key_ref.value_ref.query_ref.gate_ref
  209.4 6.0 shard_map.325
  221.0 4.9 collective-permute-start.2
  227.3 5.6 collective-permute-done.2
  232.9 10.0 %collective-permute-done.4 = bf16[256,2048]{1,0:T(8,128)(2,1)S(1)} collective-permute-done((bf16[256,2048]{1,0:T(8,128)(2,1)S(1)}, bf16[256,2048]{1,0:T(8,128)(2,1)S(1)}, u32[]{:S(2)}, u32[]{:S(2)}) %collective-permute-start.4) | collective-permute-done | bytes 1048608 | tf_op jit(solution)/shard_map/ppermute | solution.py:445
  246.0 10.3 %collective-permute-done.6 = bf16[128,2048]{1,0:T(8,128)(2,1)S(1)} collective-permute-done((bf16[128,2048]{1,0:T(8,128)(2,1)S(1)}, bf16[128,2048]{1,0:T(8,128)(2,1)S(1)}, u32[]{:S(2)}, u32[]{:S(2)}) %collective-permute-start.6) | collective-permute-done | bytes 524320 | tf_op jit(solution)/shard_map/ppermute | solution.py:445
  266.4 7.1 shard_map.326
  284.2 9.4 collective-permute-done.11
  296.6 8.7 collective-permute-done.13
  305.3 8.5 collective-permute-done.12
  319.6 21.1 %collective-permute-done.14 = bf16[256,2048]{1,0:T(8,128)(2,1)S(1)} collective-permute-done((bf16[256,2048]{1,0:T(8,128)(2,1)}, bf16[256,2048]{1,0:T(8,128)(2,1)S(1)}, u32[]{:S(2)}, u32[]{:S(2)}) %collective-permute-start.14) | collective-permute-done | bytes 1048608 | tf_op jit(solution)/shard_map/ppermute | solution.py:445
  355.1 12.8 %all-gather.11.cloned.1.call-done = bf16[2048,2816]{1,0:T(8,128)(2,1)} async-done(((bf16[256,2816]{1,0:T(8,128)(2,1)}), bf16[2048,2816]{1,0:T(8,128)(2,1)}) %all-gather.11.cloned.1.call-update) | async-done | bytes 11534352 | tf_op jit(solution)/shard_map/all_gather | solution.py:517
  367.9 18.7 %fusion.162 = f32[1024,2816]{1,0:T(8,128)} fusion(bf16[1024,2048]{1,0:T(8,128)(2,1)} %constant_dynamic-update-slice_fusion.7, bf16[2048,2816]{1,0:T(8,128)(2,1)} %all-gather.11.cloned.1.call-done), kind=kOutput, calls=%fused_computation.342 | convolution fusion | flops 11811160064 | bytes 27262976 | tf_op jit(solution)/shard_map/dot_general | solution.py:41
  386.6 41.5 %all-gather.9.cloned.1.call-done = bf16[2048,1408]{1,0:T(8,128)(2,1)} async-done(((bf16[256,1408]{1,0:T(8,128)(2,1)}), bf16[2048,1408]{1,0:T(8,128)(2,1)}) %all-gather.9.cloned.1.call-update) | async-done | bytes 5767184 | tf_op jit(solution)/shard_map/all_gather | solution.py:517
  428.1 16.2 %multiply_convert_fusion.1 = (bf16[1024,1408]{1,0:T(8,128)(2,1)}, bf16[1024,1408]{1,0:T(8,128)(2,1)}, bf16[1024,1408]{1,0:T(8,128)(2,1)S(1)}) fusion(f32[1024,2816]{1,0:T(8,128)} %fusion.162, bf16[1024,2048]{1,0:T(8,128)(2,1)} %copy-done.61, bf16[2048,1408]{1,0:T(8,128)(2,1)} %all-gather.9.cloned.1.call-done), kind=kOutput, calls=%fused_computation.14 | convolution fusion | flops 5927206912 | bytes 30146560 | tf_op jit(solution)/shard_map/dot_general | solution.py:41
  444.4 4.9 convolution_convert_fusion.3
  449.5 11.2 %convolution_convert_fusion = bf16[1024,2816]{1,0:T(8,128)(2,1)} fusion(bf16[1024,1408]{1,0:T(8,128)(2,1)} %get-tuple-element.167, bf16[1024,1408]{1,0:T(8,128)(2,1)} %get-tuple-element.168, bf16[1024,2048]{1,0:T(8,128)(2,1)} %constant_dynamic-update-slice_fusion.7, s32[]{:T(128)S(6)} %select_n.243), kind=kOutput, calls=%fused_computation.18 | convolution fusion | flops 5919997952 | bytes 13631492 | tf_op jit(solution)/shard_map/dot_general | solution.py:49
  461.0 10.5 %fusion.15 = f32[512,2048]{1,0:T(8,128)} fusion(bf16[2048,2816]{1,0:T(8,128)(2,1)} %all-gather.11.cloned.1.call-done, bf16[1024,1408]{1,0:T(8,128)(2,1)S(1)} %copy-done.90, bf16[1024,1408]{1,0:T(8,128)(2,1)S(1)} %copy-done.89), kind=kOutput, calls=%fused_computation.43 | convolution fusion | flops 5911347200 | bytes 21495808 | tf_op jit(solution)/shard_map/dot_general | solution.py:45
  471.5 6.3 add_convert_fusion.2
  478.3 8.4 convolution_convert_fusion.9
  489.8 11.1 %collective-permute-done.22 = bf16[128,2048]{1,0:T(8,128)(2,1)S(1)} collective-permute-done((bf16[128,2048]{1,0:T(8,128)(2,1)S(1)}, bf16[128,2048]{1,0:T(8,128)(2,1)S(1)}, u32[]{:S(2)}, u32[]{:S(2)}) %collective-permute-start.22) | collective-permute-done | bytes 524320 | tf_op jit(solution)/shard_map/ppermute | solution.py:445
  506.5 10.6 %collective-permute-done.21 = bf16[128,2048]{1,0:T(8,128)(2,1)S(1)} collective-permute-done((bf16[128,2048]{1,0:T(8,128)(2,1)S(1)}, bf16[128,2048]{1,0:T(8,128)(2,1)S(1)}, u32[]{:S(2)}, u32[]{:S(2)}) %collective-permute-start.21) | collective-permute-done | bytes 524320 | tf_op jit(solution)/shard_map/ppermute | solution.py:445
  517.1 9.5 collective-permute-done.19
  528.2 9.3 convert_add_fusion.1
  537.5 11.6 %add_convert_fusion = bf16[1024,2816]{1,0:T(8,128)(2,1)} fusion(bf16[1024,2816]{1,0:T(8,128)(2,1)} %collective-permute-done.25, bf16[1024,1408]{1,0:T(8,128)(2,1)} %get-tuple-element.167, bf16[1024,1408]{1,0:T(8,128)(2,1)} %get-tuple-element.168, bf16[1024,2048]{1,0:T(8,128)(2,1)S(1)} %copy-done.59, s32[]{:T(128)S(6)} %select_n.242), kind=kOutput, calls=%fused_computation | convolution fusion | flops 5925765120 | bytes 19398660 | tf_op jit(solution)/shard_map/dot_general | solution.py:49
  552.8 4.9 constant_dynamic-update-slice_fusion.16
  560.7 19.6 %collective-permute-done.26 = bf16[256,2048]{1,0:T(8,128)(2,1)S(1)} collective-permute-done((bf16[256,2048]{1,0:T(8,128)(2,1)}, bf16[256,2048]{1,0:T(8,128)(2,1)S(1)}, u32[]{:S(2)}, u32[]{:S(2)}) %collective-permute-start.26) | collective-permute-done | bytes 1048608 | tf_op jit(solution)/shard_map/ppermute | solution.py:445
  594.0 5.0 collective-permute-done.29
  599.8 5.4 fusion.163.grad_ref
  605.2 5.5 shard_map.327
  619.7 5.0 fusion.160
  631.9 33.6 %collective-permute-done.31 = bf16[514,256]{1,0:T(8,128)(2,1)S(1)} collective-permute-done((bf16[514,256]{1,0:T(8,128)(2,1)S(1)}, bf16[514,256]{1,0:T(8,128)(2,1)S(1)}, u32[]{:S(2)}, u32[]{:S(2)}) %collective-permute-start.31) | collective-permute-done | bytes 263200 | tf_op jit(solution)/shard_map/ppermute | solution.py:662
  681.9 7.4 collective-permute-done.35
  689.5 7.0 multiply_convert_fusion.3
  698.7 12.5 %shard_map.328 = (bf16[1024,1536]{1,0:T(8,128)(2,1)S(1)}, f32[1024,256]{1,0:T(8,128)S(1)}) custom-call(s32[4]{0:T(128)S(1)} %iota_xor_fusion.order, s32[16]{0:T(128)S(1)} %convert_element_type.362.resets, f32[1024,1664]{1,0:T(8,128)} %copy-done.2, f32[1024,1664]{1,0:T(8,128)} %copy-done.2, f32[1024,1664]{1,0:T(8,128)} %copy-done.2, ...), custom_call_target="tpu_custom_call" | custom-call | flops 8589934592 | bytes 25165824 | tf_op jit(solution)/shard_map/pallas_call | solution.py:419
  720.1 7.7 convolution_convert_fusion.2
  727.8 4.9 fusion.19
  739.2 6.0 fusion.6
  750.0 6.3 add_convert_fusion.1
  776.2 6.2 fusion.8
  783.4 6.4 collective-permute-done.53
  805.7 7.7 all-to-all-start.1
  822.5 5.1 collective-permute-done.47
  833.8 43.7 %collective-permute-done.55 = f32[71,256]{1,0:T(8,128)S(1)} collective-permute-done((f32[71,256]{1,0:T(8,128)S(1)}, f32[71,256]{1,0:T(8,128)S(1)}, u32[]{:S(2)}, u32[]{:S(2)}) %collective-permute-start.55) | collective-permute-done | bytes 72736 | tf_op jit(solution)/shard_map/ppermute | solution.py:831
  877.5 4.7 collective-permute-start.56
  883.6 10.4 %collective-permute-done.56 = f32[71,256]{1,0:T(8,128)S(1)} collective-permute-done((f32[71,256]{1,0:T(8,128)S(1)}, f32[71,256]{1,0:T(8,128)S(1)}, u32[]{:S(2)}, u32[]{:S(2)}) %collective-permute-start.56) | collective-permute-done | bytes 72736 | tf_op jit(solution)/shard_map/ppermute | solution.py:831
  (526 shorter events, 285.0 us)
Async XLA Ops:
  7.2 184.8 %all-gather.5.cloned.1.call-start = ((), (), s32[]{:S(2)}) async-start(), calls=%async_computation.6 | async-start | bytes 7667712 | tf_op jit(solution)/shard_map/all_gather | solution.py:517
  67.0 208.9 %all-gather.7.cloned.1.call-start = ((), (), s32[]{:S(2)}) async-start(), calls=%async_computation.7 | async-start | bytes 2359296 | tf_op jit(solution)/shard_map/all_gather | solution.py:517
  67.1 121.6 %collective-permute-start = (bf16[17,512]{1,0:T(8,128)(2,1)S(1)}, bf16[17,512]{1,0:T(8,128)(2,1)S(1)}, u32[]{:S(2)}, u32[]{:S(2)}) collective-permute-start(bf16[17,512]{1,0:T(8,128)(2,1)S(1)} %constant_dynamic-update-slice_fusion), channel_id=1, source_target_pairs={{0,1},{1,0},{2,3},{3,2},{4,5},{5,4},{6,7},{7,6},{8,9},{9,8},{10,11... | collective-permute-start | bytes 52232 | tf_op jit(solution)/shard_map/ppermute | solution.py:441
  68.5 299.4 %all-gather.11.cloned.1.call-start = ((), (), s32[]{:S(2)}) async-start(), calls=%async_computation.9 | async-start | bytes 12976128 | tf_op jit(solution)/shard_map/all_gather | solution.py:517
  217.7 25.3 %collective-permute-start.4 = (bf16[256,2048]{1,0:T(8,128)(2,1)S(1)}, bf16[256,2048]{1,0:T(8,128)(2,1)S(1)}, u32[]{:S(2)}, u32[]{:S(2)}) collective-permute-start(bf16[256,2048]{1,0:T(8,128)(2,1)S(1)} %get-tuple-element.164), channel_id=1, source_target_pairs={{0,2},{2,0},{4,6},{6,4},{1,3},{3,1},{5,7},{7,5},{8,10},{10,8},{12,... | collective-permute-start | bytes 3145736 | tf_op jit(solution)/shard_map/ppermute | solution.py:445
  218.4 27.0 %collective-permute-start.5 = (bf16[256,2048]{1,0:T(8,128)(2,1)S(1)}, bf16[256,2048]{1,0:T(8,128)(2,1)S(1)}, u32[]{:S(2)}, u32[]{:S(2)}) collective-permute-start(bf16[256,2048]{1,0:T(8,128)(2,1)S(1)} %get-tuple-element.164), channel_id=1, source_target_pairs={{0,4},{2,6},{4,0},{6,2},{1,5},{3,7},{5,1},{7,3},{8,12},{10,14},{12... | collective-permute-start | bytes 3145736 | tf_op jit(solution)/shard_map/ppermute | solution.py:445
  260.6 167.6 %all-gather.9.cloned.1.call-start = ((), (), s32[]{:S(2)}) async-start(), calls=%async_computation.8 | async-start | bytes 6488064 | tf_op jit(solution)/shard_map/all_gather | solution.py:517
  261.1 338.6 %reduce-scatter.5.cloned.1.call-start = ((), (), s32[]{:S(2)}) async-start(), calls=%async_computation.10 | async-start | bytes 3604480 | tf_op jit(solution)/shard_map/reduce_scatter | solution.py:526
  281.4 23.9 %collective-permute-start.13 = (bf16[128,2048]{1,0:T(8,128)(2,1)S(1)}, bf16[128,2048]{1,0:T(8,128)(2,1)S(1)}, u32[]{:S(2)}, u32[]{:S(2)}) collective-permute-start(bf16[128,2048]{1,0:T(8,128)(2,1)S(1)} %get-tuple-element.188), channel_id=1, source_target_pairs={{0,4},{2,6},{4,0},{6,2},{1,5},{3,7},{5,1},{7,3},{8,12},{10,14},{12... | collective-permute-start | bytes 1572872 | tf_op jit(solution)/shard_map/ppermute | solution.py:445
  282.7 22.6 %collective-permute-start.8 = (bf16[128,2048]{1,0:T(8,128)(2,1)S(1)}, bf16[128,2048]{1,0:T(8,128)(2,1)S(1)}, u32[]{:S(2)}, u32[]{:S(2)}) collective-permute-start(bf16[128,2048]{1,0:T(8,128)(2,1)S(1)} %get-tuple-element.189), channel_id=1, source_target_pairs={{0,2},{2,0},{4,6},{6,4},{1,3},{3,1},{5,7},{7,5},{8,10},{10,8},{12,... | collective-permute-start | bytes 1572872 | tf_op jit(solution)/shard_map/ppermute | solution.py:445
  294.4 19.5 %collective-permute-start.12 = (bf16[128,2048]{1,0:T(8,128)(2,1)S(1)}, bf16[128,2048]{1,0:T(8,128)(2,1)S(1)}, u32[]{:S(2)}, u32[]{:S(2)}) collective-permute-start(bf16[128,2048]{1,0:T(8,128)(2,1)S(1)} %get-tuple-element.176), channel_id=1, source_target_pairs={{0,4},{2,6},{4,0},{6,2},{1,5},{3,7},{5,1},{7,3},{8,12},{10,14},{12... | collective-permute-start | bytes 1572872 | tf_op jit(solution)/shard_map/ppermute | solution.py:445
  295.2 18.6 %collective-permute-start.10 = (bf16[128,2048]{1,0:T(8,128)(2,1)S(1)}, bf16[128,2048]{1,0:T(8,128)(2,1)S(1)}, u32[]{:S(2)}, u32[]{:S(2)}) collective-permute-start(bf16[128,2048]{1,0:T(8,128)(2,1)S(1)} %get-tuple-element.177), channel_id=1, source_target_pairs={{0,2},{2,0},{4,6},{6,4},{1,3},{3,1},{5,7},{7,5},{8,10},{10,8},{12,... | collective-permute-start | bytes 1572872 | tf_op jit(solution)/shard_map/ppermute | solution.py:445
  317.9 22.8 %collective-permute-start.14 = (bf16[256,2048]{1,0:T(8,128)(2,1)}, bf16[256,2048]{1,0:T(8,128)(2,1)S(1)}, u32[]{:S(2)}, u32[]{:S(2)}) collective-permute-start(bf16[256,2048]{1,0:T(8,128)(2,1)} %get-tuple-element.162), channel_id=1, source_target_pairs={{0,2},{2,0},{4,6},{6,4},{1,3},{3,1},{5,7},{7,5},{8,10},{10,8},{12,... | collective-permute-start | bytes 3145736 | tf_op jit(solution)/shard_map/ppermute | solution.py:445
  318.9 22.6 %collective-permute-start.15 = (bf16[256,2048]{1,0:T(8,128)(2,1)}, bf16[256,2048]{1,0:T(8,128)(2,1)}, u32[]{:S(2)}, u32[]{:S(2)}) collective-permute-start(bf16[256,2048]{1,0:T(8,128)(2,1)} %get-tuple-element.162), channel_id=1, source_target_pairs={{0,4},{2,6},{4,0},{6,2},{1,5},{3,7},{5,1},{7,3},{8,12},{10,14},{12... | collective-permute-start | bytes 3145736 | tf_op jit(solution)/shard_map/ppermute | solution.py:445
  449.2 22.2 %collective-permute-start.18 = (bf16[1024,1408]{1,0:T(8,128)(2,1)}, bf16[1024,1408]{1,0:T(8,128)(2,1)}, u32[]{:S(2)}, u32[]{:S(2)}) collective-permute-start(bf16[1024,1408]{1,0:T(8,128)(2,1)} %convolution_convert_fusion.3), channel_id=1, source_target_pairs={{0,1},{1,0},{2,3},{3,2},{4,5},{5,4},{6,7},{7,6},{8,9},{9,8},{10,11... | collective-permute-start | bytes 8650760 | tf_op jit(solution)/shard_map/ppermute | solution.py:441
  460.7 76.8 %collective-permute-start.25 = (bf16[1024,2816]{1,0:T(8,128)(2,1)}, bf16[1024,2816]{1,0:T(8,128)(2,1)}, u32[]{:S(2)}, u32[]{:S(2)}) collective-permute-start(bf16[1024,2816]{1,0:T(8,128)(2,1)} %convolution_convert_fusion), channel_id=1, source_target_pairs={{0,1},{1,0},{2,3},{3,2},{4,5},{5,4},{6,7},{7,6},{8,9},{9,8},{10,11... | collective-permute-start | bytes 17301512 | tf_op jit(solution)/shard_map/ppermute | solution.py:441
  477.8 218.6 %reduce-scatter.7.cloned.1.call-start = ((), (), s32[]{:S(2)}) async-start(), calls=%async_computation.11 | async-start | bytes 7208960 | tf_op jit(solution)/shard_map/reduce_scatter | solution.py:526
  503.1 23.4 %collective-permute-start.19 = (bf16[128,2048]{1,0:T(8,128)(2,1)S(1)}, bf16[128,2048]{1,0:T(8,128)(2,1)S(1)}, u32[]{:S(2)}, u32[]{:S(2)}) collective-permute-start(bf16[128,2048]{1,0:T(8,128)(2,1)S(1)} %get-tuple-element.187), channel_id=1, source_target_pairs={{0,2},{2,0},{4,6},{6,4},{1,3},{3,1},{5,7},{7,5},{8,10},{10,8},{12,... | collective-permute-start | bytes 1572872 | tf_op jit(solution)/shard_map/ppermute | solution.py:445
  504.4 22.1 %collective-permute-start.24 = (bf16[128,2048]{1,0:T(8,128)(2,1)S(1)}, bf16[128,2048]{1,0:T(8,128)(2,1)S(1)}, u32[]{:S(2)}, u32[]{:S(2)}) collective-permute-start(bf16[128,2048]{1,0:T(8,128)(2,1)S(1)} %get-tuple-element.186), channel_id=1, source_target_pairs={{0,4},{2,6},{4,0},{6,2},{1,5},{3,7},{5,1},{7,3},{8,12},{10,14},{12... | collective-permute-start | bytes 1572872 | tf_op jit(solution)/shard_map/ppermute | solution.py:445
  505.9 22.3 %collective-permute-start.23 = (bf16[128,2048]{1,0:T(8,128)(2,1)S(1)}, bf16[128,2048]{1,0:T(8,128)(2,1)S(1)}, u32[]{:S(2)}, u32[]{:S(2)}) collective-permute-start(bf16[128,2048]{1,0:T(8,128)(2,1)S(1)} %get-tuple-element.174), channel_id=1, source_target_pairs={{0,4},{2,6},{4,0},{6,2},{1,5},{3,7},{5,1},{7,3},{8,12},{10,14},{12... | collective-permute-start | bytes 1572872 | tf_op jit(solution)/shard_map/ppermute | solution.py:445
  549.1 250.8 %reduce-scatter.9.cloned.1.call-start = ((), (), s32[]{:S(2)}) async-start(), calls=%async_computation.12 | async-start | bytes 1310720 | tf_op jit(solution)/shard_map/reduce_scatter | solution.py:526
  557.7 22.6 %collective-permute-start.26 = (bf16[256,2048]{1,0:T(8,128)(2,1)}, bf16[256,2048]{1,0:T(8,128)(2,1)S(1)}, u32[]{:S(2)}, u32[]{:S(2)}) collective-permute-start(bf16[256,2048]{1,0:T(8,128)(2,1)} %get-tuple-element.159), channel_id=1, source_target_pairs={{0,2},{2,0},{4,6},{6,4},{1,3},{3,1},{5,7},{7,5},{8,10},{10,8},{12,... | collective-permute-start | bytes 3145736 | tf_op jit(solution)/shard_map/ppermute | solution.py:445
  558.2 29.5 %collective-permute-start.27 = (bf16[256,2048]{1,0:T(8,128)(2,1)}, bf16[256,2048]{1,0:T(8,128)(2,1)}, u32[]{:S(2)}, u32[]{:S(2)}) collective-permute-start(bf16[256,2048]{1,0:T(8,128)(2,1)} %get-tuple-element.159), channel_id=1, source_target_pairs={{0,4},{2,6},{4,0},{6,2},{1,5},{3,7},{5,1},{7,3},{8,12},{10,14},{12... | collective-permute-start | bytes 3145736 | tf_op jit(solution)/shard_map/ppermute | solution.py:445
  610.8 20.1 %collective-permute-start.32 = (bf16[514,256]{1,0:T(8,128)(2,1)S(1)}, bf16[514,256]{1,0:T(8,128)(2,1)}, u32[]{:S(2)}, u32[]{:S(2)}) collective-permute-start(bf16[514,256]{1,0:T(8,128)(2,1)S(1)} %pad_maximum_fusion.14), channel_id=1, source_target_pairs={{8,0},{16,8},{24,16},{9,1},{17,9},{25,17},{10,2},{18,10},{26,18},{... | collective-permute-start | bytes 789512 | tf_op jit(solution)/shard_map/ppermute | solution.py:662
  612.1 53.4 %collective-permute-start.31 = (bf16[514,256]{1,0:T(8,128)(2,1)S(1)}, bf16[514,256]{1,0:T(8,128)(2,1)S(1)}, u32[]{:S(2)}, u32[]{:S(2)}) collective-permute-start(bf16[514,256]{1,0:T(8,128)(2,1)S(1)} %pad_maximum_fusion.14), channel_id=1, source_target_pairs={{16,0},{24,8},{17,1},{25,9},{18,2},{26,10},{19,3},{27,11},{20,4},{... | collective-permute-start | bytes 789512 | tf_op jit(solution)/shard_map/ppermute | solution.py:662
  613.4 58.6 %collective-permute-start.30 = (bf16[514,256]{1,0:T(8,128)(2,1)S(1)}, bf16[514,256]{1,0:T(8,128)(2,1)}, u32[]{:S(2)}, u32[]{:S(2)}) collective-permute-start(bf16[514,256]{1,0:T(8,128)(2,1)S(1)} %pad_maximum_fusion.14), channel_id=1, source_target_pairs={{24,0},{25,1},{26,2},{27,3},{28,4},{29,5},{30,6},{31,7}} | collective-permute-start | bytes 789512 | tf_op jit(solution)/shard_map/ppermute | solution.py:662
  617.8 48.8 %collective-permute-start.36 = (bf16[128,2048]{1,0:T(8,128)(2,1)}, bf16[128,2048]{1,0:T(8,128)(2,1)}, u32[]{:S(2)}, u32[]{:S(2)}) collective-permute-start(bf16[128,2048]{1,0:T(8,128)(2,1)} %get-tuple-element.200), channel_id=1, source_target_pairs={{0,2},{2,0},{4,6},{6,4},{1,3},{3,1},{5,7},{7,5},{8,10},{10,8},{12,... | collective-permute-start | bytes 1572872 | tf_op jit(solution)/shard_map/ppermute | solution.py:445
  619.3 48.6 %collective-permute-start.34 = (bf16[128,2048]{1,0:T(8,128)(2,1)}, bf16[128,2048]{1,0:T(8,128)(2,1)}, u32[]{:S(2)}, u32[]{:S(2)}) collective-permute-start(bf16[128,2048]{1,0:T(8,128)(2,1)} %get-tuple-element.201), channel_id=1, source_target_pairs={{0,4},{2,6},{4,0},{6,2},{1,5},{3,7},{5,1},{7,3},{8,12},{10,14},{12... | collective-permute-start | bytes 1572872 | tf_op jit(solution)/shard_map/ppermute | solution.py:445
  630.9 43.9 %collective-permute-start.46 = (bf16[1024,512]{1,0:T(8,128)(2,1)}, bf16[1024,512]{1,0:T(8,128)(2,1)S(1)}, u32[]{:S(2)}, u32[]{:S(2)}) collective-permute-start(bf16[1024,512]{1,0:T(8,128)(2,1)} %fusion.51), channel_id=1, source_target_pairs={{0,1},{1,0},{2,3},{3,2},{4,5},{5,4},{6,7},{7,6},{8,9},{9,8},{10,11... | collective-permute-start | bytes 3145736 | tf_op jit(solution)/shard_map/ppermute | solution.py:441
  715.4 49.2 %all-to-all-start = ((bf16[16,32,2048]{2,1,0:T(8,128)(2,1)}), bf16[16,32,2048]{2,1,0:T(8,128)(2,1)}, u32[]{:S(2)}, u32[]{:S(2)}) async-start(bf16[16,32,2048]{2,1,0:T(8,128)(2,1)} %bitcast.125), calls=%async_computation.2 | async-start | bytes 4194304 | tf_op jit(solution)/shard_map/all_to_all | solution.py:565
  719.8 182.3 %reduce-scatter.11.cloned.1.call-start = ((), (), s32[]{:S(2)}) async-start(), calls=%async_computation.13 | async-start | bytes 3932160 | tf_op jit(solution)/shard_map/reduce_scatter | solution.py:526
  727.8 20.0 %collective-permute-start.39 = (bf16[1024,1536]{1,0:T(8,128)(2,1)}, bf16[1024,1536]{1,0:T(8,128)(2,1)}, u32[]{:S(2)}, u32[]{:S(2)}) collective-permute-start(bf16[1024,1536]{1,0:T(8,128)(2,1)} %convolution_convert_fusion.2), channel_id=1, source_target_pairs={{0,1},{1,0},{2,3},{3,2},{4,5},{5,4},{6,7},{7,6},{8,9},{9,8},{10,11... | collective-permute-start | bytes 9437192 | tf_op jit(solution)/shard_map/ppermute | solution.py:441
  733.8 30.8 %collective-permute-start.41 = (bf16[128,2176]{1,0:T(8,128)(2,1)}, bf16[128,2176]{1,0:T(8,128)(2,1)S(1)}, u32[]{:S(2)}, u32[]{:S(2)}) collective-permute-start(bf16[128,2176]{1,0:T(8,128)(2,1)} %get-tuple-element.199), channel_id=1, source_target_pairs={{0,2},{2,0},{4,6},{6,4},{1,3},{3,1},{5,7},{7,5},{8,10},{10,8},{12,... | collective-permute-start | bytes 1671176 | tf_op jit(solution)/shard_map/ppermute | solution.py:445
  735.5 29.0 %collective-permute-start.42 = (bf16[128,2176]{1,0:T(8,128)(2,1)}, bf16[128,2176]{1,0:T(8,128)(2,1)}, u32[]{:S(2)}, u32[]{:S(2)}) collective-permute-start(bf16[128,2176]{1,0:T(8,128)(2,1)} %get-tuple-element.198), channel_id=1, source_target_pairs={{0,4},{2,6},{4,0},{6,2},{1,5},{3,7},{5,1},{7,3},{8,12},{10,14},{12... | collective-permute-start | bytes 1671176 | tf_op jit(solution)/shard_map/ppermute | solution.py:445
  759.9 31.7 %collective-permute-start.40 = (bf16[128,2176]{1,0:T(8,128)(2,1)}, bf16[128,2176]{1,0:T(8,128)(2,1)S(1)}, u32[]{:S(2)}, u32[]{:S(2)}) collective-permute-start(bf16[128,2176]{1,0:T(8,128)(2,1)} %get-tuple-element.179), channel_id=1, source_target_pairs={{0,2},{2,0},{4,6},{6,4},{1,3},{3,1},{5,7},{7,5},{8,10},{10,8},{12,... | collective-permute-start | bytes 1671176 | tf_op jit(solution)/shard_map/ppermute | solution.py:445
  760.5 35.6 %collective-permute-start.45 = (bf16[128,2176]{1,0:T(8,128)(2,1)}, bf16[128,2176]{1,0:T(8,128)(2,1)}, u32[]{:S(2)}, u32[]{:S(2)}) collective-permute-start(bf16[128,2176]{1,0:T(8,128)(2,1)} %get-tuple-element.178), channel_id=1, source_target_pairs={{0,4},{2,6},{4,0},{6,2},{1,5},{3,7},{5,1},{7,3},{8,12},{10,14},{12... | collective-permute-start | bytes 1671176 | tf_op jit(solution)/shard_map/ppermute | solution.py:445
  767.5 28.6 %collective-permute-start.43 = (bf16[128,2176]{1,0:T(8,128)(2,1)}, bf16[128,2176]{1,0:T(8,128)(2,1)}, u32[]{:S(2)}, u32[]{:S(2)}) collective-permute-start(bf16[128,2176]{1,0:T(8,128)(2,1)} %get-tuple-element.171), channel_id=1, source_target_pairs={{0,2},{2,0},{4,6},{6,4},{1,3},{3,1},{5,7},{7,5},{8,10},{10,8},{12,... | collective-permute-start | bytes 1671176 | tf_op jit(solution)/shard_map/ppermute | solution.py:445
  768.6 27.5 %collective-permute-start.44 = (bf16[128,2176]{1,0:T(8,128)(2,1)}, bf16[128,2176]{1,0:T(8,128)(2,1)}, u32[]{:S(2)}, u32[]{:S(2)}) collective-permute-start(bf16[128,2176]{1,0:T(8,128)(2,1)} %get-tuple-element.170), channel_id=1, source_target_pairs={{0,4},{2,6},{4,0},{6,2},{1,5},{3,7},{5,1},{7,3},{8,12},{10,14},{12... | collective-permute-start | bytes 1671176 | tf_op jit(solution)/shard_map/ppermute | solution.py:445
  789.9 37.7 %collective-permute-start.58 = (bf16[128,1408]{1,0:T(8,128)(2,1)}, bf16[128,1408]{1,0:T(8,128)(2,1)}, u32[]{:S(2)}, u32[]{:S(2)}) collective-permute-start(bf16[128,1408]{1,0:T(8,128)(2,1)} %get-tuple-element.220), channel_id=1, source_target_pairs={{0,2},{1,6},{2,0},{3,4},{4,3},{5,7},{6,1},{7,5},{8,10},{9,14},{10,... | collective-permute-start | bytes 1081352 | tf_op jit(solution)/shard_map/ppermute | solution.py:530
  791.6 39.7 %collective-permute-start.57 = (bf16[128,1408]{1,0:T(8,128)(2,1)}, bf16[128,1408]{1,0:T(8,128)(2,1)}, u32[]{:S(2)}, u32[]{:S(2)}) collective-permute-start(bf16[128,1408]{1,0:T(8,128)(2,1)} %get-tuple-element.221), channel_id=1, source_target_pairs={{0,0},{1,4},{2,2},{3,6},{4,1},{5,5},{6,3},{7,7},{8,8},{9,12},{10,1... | collective-permute-start | bytes 1081352 | tf_op jit(solution)/shard_map/ppermute | solution.py:530
  796.1 24.7 %collective-permute-start.54 = (f32[71,256]{1,0:T(8,128)}, f32[71,256]{1,0:T(8,128)}, u32[]{:S(2)}, u32[]{:S(2)}) collective-permute-start(f32[71,256]{1,0:T(8,128)} %add.407), channel_id=1, source_target_pairs={{0,4},{2,6},{4,0},{6,2},{1,5},{3,7},{5,1},{7,3},{8,12},{10,14},{12... | collective-permute-start | bytes 218120 | tf_op jit(solution)/shard_map/ppermute | solution.py:445
  805.7 96.4 %all-to-all-start.1 = ((bf16[16,32,2048]{2,1,0:T(8,128)(2,1)}), bf16[16,32,2048]{2,1,0:T(8,128)(2,1)}, u32[]{:S(2)}, u32[]{:S(2)}) async-start(bf16[16,32,2048]{2,1,0:T(8,128)(2,1)} %bitcast.126), calls=%async_computation.4 | async-start | bytes 4194304 | tf_op jit(solution)/shard_map/all_to_all | solution.py:565
  819.3 63.0 %collective-permute-start.60 = (bf16[128,2816]{1,0:T(8,128)(2,1)S(1)}, bf16[128,2816]{1,0:T(8,128)(2,1)S(1)}, u32[]{:S(2)}, u32[]{:S(2)}) collective-permute-start(bf16[128,2816]{1,0:T(8,128)(2,1)S(1)} %get-tuple-element.196), channel_id=1, source_target_pairs={{0,2},{1,6},{2,0},{3,4},{4,3},{5,7},{6,1},{7,5},{8,10},{9,14},{10,... | collective-permute-start | bytes 2162696 | tf_op jit(solution)/shard_map/ppermute | solution.py:530
  820.8 61.5 %collective-permute-start.59 = (bf16[128,2816]{1,0:T(8,128)(2,1)S(1)}, bf16[128,2816]{1,0:T(8,128)(2,1)S(1)}, u32[]{:S(2)}, u32[]{:S(2)}) collective-permute-start(bf16[128,2816]{1,0:T(8,128)(2,1)S(1)} %get-tuple-element.197), channel_id=1, source_target_pairs={{0,0},{1,4},{2,2},{3,6},{4,1},{5,5},{6,3},{7,7},{8,8},{9,12},{10,1... | collective-permute-start | bytes 2162696 | tf_op jit(solution)/shard_map/ppermute | solution.py:530
  827.5 49.9 %collective-permute-start.55 = (f32[71,256]{1,0:T(8,128)S(1)}, f32[71,256]{1,0:T(8,128)S(1)}, u32[]{:S(2)}, u32[]{:S(2)}) collective-permute-start(f32[71,256]{1,0:T(8,128)S(1)} %add.408), channel_id=1, source_target_pairs={{0,8},{8,0},{16,24},{24,16},{1,9},{9,1},{17,25},{25,17},{2,10},{10... | collective-permute-start | bytes 218120 | tf_op jit(solution)/shard_map/ppermute | solution.py:831
  827.6 54.5 %collective-permute-start.48 = (f32[18,4,128]{2,1,0:T(4,128)S(1)}, f32[18,4,128]{2,1,0:T(4,128)S(1)}, u32[]{:S(2)}, u32[]{:S(2)}) collective-permute-start(f32[18,4,128]{2,1,0:T(4,128)S(1)} %dynamic-slice_bitcast_fusion), channel_id=1, source_target_pairs={{0,2},{2,0},{4,6},{6,4},{1,3},{3,1},{5,7},{7,5},{8,10},{10,8},{12,... | collective-permute-start | bytes 110600 | tf_op jit(solution)/shard_map/ppermute | solution.py:445
  833.7 68.0 %collective-permute-start.63 = (bf16[256,2048]{0,1:T(8,128)(2,1)S(1)}, bf16[256,2048]{0,1:T(8,128)(2,1)S(1)}, u32[]{:S(2)}, u32[]{:S(2)}) collective-permute-start(bf16[256,2048]{0,1:T(8,128)(2,1)S(1)} %bitcast.127), channel_id=1, source_target_pairs={{0,1},{1,0},{2,3},{3,2},{4,5},{5,4},{6,7},{7,6},{8,9},{9,8},{10,11... | collective-permute-start | bytes 3145736 | tf_op jit(solution)/shard_map/ppermute | solution.py:441
  919.5 24.1 %collective-permute-start.64 = (bf16[256,2048]{0,1:T(8,128)(2,1)}, bf16[256,2048]{0,1:T(8,128)(2,1)}, u32[]{:S(2)}, u32[]{:S(2)}) collective-permute-start(bf16[256,2048]{0,1:T(8,128)(2,1)} %bitcast.128), channel_id=1, source_target_pairs={{0,1},{1,0},{2,3},{3,2},{4,5},{5,4},{6,7},{7,6},{8,9},{9,8},{10,11... | collective-permute-start | bytes 3145736 | tf_op jit(solution)/shard_map/ppermute | solution.py:441
  (125 other events, 2210.6 us)
Sparse Core Ops, SparseCore 0:
  67.1 124.7 all-gather.4
  193.6 28.0 all-gather.6
  260.7 107.1 all-gather.10
  369.4 58.7 all-gather.8
  477.9 54.8 reduce-scatter.4
  549.2 116.5 reduce-scatter.6
  677.2 24.6 reduce-scatter.8
  783.6 91.4 reduce-scatter.10

commit v3 on v2

--- a/solution.py
+++ b/solution.py
@@ -395,6 +395,58 @@
     )(*([value, block] if spread else [value]), *weights)
 
 
+def restore_kernel(planes, pack_ref, got_ref, out_ref):
+    block = got_ref.shape[1] // (2 * planes)
+    for number in range(2 * planes):
+        r, o = (number // planes, number % planes)
+        piece = lax.dot_general(
+            pack_ref[...], got_ref[:, number * block : (number + 1) * block], contract_rows,
+            preferred_element_type=f32,
+        )
+        at = (o * 2 + r) * block
+        out_ref[:, at : at + block] = piece.astype(bf16)
+
+
+def restore_rows(pack, got, planes):
+    inside = pl.BlockSpec(memory_space=pltpu.VMEM)
+    return pl.pallas_call(
+        functools.partial(restore_kernel, planes),
+        out_shape=jax.ShapeDtypeStruct((pack.shape[1], got.shape[1]), bf16),
+        in_specs=[inside, inside],
+        out_specs=inside,
+        compiler_params=pltpu.CompilerParams(vmem_limit_bytes=24 << 20),
+        cost_estimate=pl.CostEstimate(flops=1 << 29, bytes_accessed=4 << 20, transcendentals=0),
+    )(pack, got)
+
+
+def stack_kernel(core, own_ref, other_ref, out_ref):
+    mine = pl.program_id(0) == core[0]
+
+    @pl.when(mine)
+    def _():
+        out_ref[0] = own_ref[...]
+
+    @pl.when(jnp.logical_not(mine))
+    def _():
+        out_ref[0] = other_ref[...]
+
+
+def stack_cores(own, other, core):
+    whole = pl.BlockSpec(own.shape, lambda step, core: (0, 0))
+    return pl.pallas_call(
+        stack_kernel,
+        out_shape=jax.ShapeDtypeStruct((2,) + own.shape, own.dtype),
+        grid_spec=pltpu.PrefetchScalarGridSpec(
+            num_scalar_prefetch=1,
+            grid=(2,),
+            in_specs=[whole, whole],
+            out_specs=pl.BlockSpec((1,) + own.shape, lambda step, core: (step, 0, 0)),
+        ),
+        compiler_params=pltpu.CompilerParams(vmem_limit_bytes=24 << 20),
+        cost_estimate=pl.CostEstimate(flops=0, bytes_accessed=4 << 20, transcendentals=0),
+    )(jnp.full((1,), core, jnp.int32), own, other)
+
+
 def rows_of(width, column=0, backward=False):
     def place(step, order, resets):
         at = order.shape[0] - 1 - step if backward else step
@@ -454,23 +506,25 @@
     return jnp.concatenate([value, near, far, upper, lower], axis=0)
 
 
-def plane_sum(produce, hold=None):
+def plane_sum(produce, beside=None, early=None, hold=None):
     across = produce(3, 4).astype(bf16)
     middle = across.shape[0] // 2
     upper = neighbour(across[:middle], 1)
     lower = neighbour(across[middle:], 2)
     sides = produce(1, 3)
     near, far = (sides[: 2 * middle], sides[2 * middle :])
-    if hold is not None:
-        upper, lower, hold = lax.optimization_barrier((upper, lower, hold))
+    own, beside = lax.optimization_barrier((produce(0, 1), beside))
+    own, upper, lower, early = lax.optimization_barrier((own, upper, lower, early))
     near_upper = neighbour(near[:middle].astype(bf16), 1)
     far_lower = neighbour(far[middle:].astype(bf16), 2)
     near_lower = neighbour((near[middle:] + lower.astype(f32)).astype(bf16), 1)
     far_upper = neighbour((far[:middle] + upper.astype(f32)).astype(bf16), 2)
     arrived_near = jnp.concatenate([near_upper, near_lower], axis=0)
     arrived_far = jnp.concatenate([far_upper, far_lower], axis=0)
-    total = produce(0, 1) + arrived_near.astype(f32) + arrived_far.astype(f32)
-    return total if hold is None else (total, hold)
+    if hold is not None:
+        arrived_near, arrived_far, hold = lax.optimization_barrier((arrived_near, arrived_far, hold))
+    total = own + arrived_near.astype(f32) + arrived_far.astype(f32)
+    return total if hold is None else (total, beside, early, hold)
 
 
 def deal_pairs(turn):
@@ -506,10 +560,6 @@
         shaped = value.reshape(value.shape[0], planes, 2, 2 * shard)
         return shaped.transpose(0, 2, 1, 3).reshape(value.shape)
 
-    def restored(value):
-        shaped = value.reshape(value.shape[0], 2, planes, 2 * shard)
-        return shaped.transpose(0, 2, 1, 3).reshape(value.shape)
-
     def either(first, second):
         return (jnp.where(even, first, second), jnp.where(even, second, first))
 
@@ -529,26 +579,6 @@
         sent = either(part_sum[:shard], part_sum[shard:])
         got = [lax.ppermute(sent[turn], ("t", "c"), deal_pairs(turn)) for turn in range(2)]
         return [piece.astype(f32) for piece in either(*got)]
-
-    def own_columns(value):
-        count = value.shape[0]
-
-        def keep_half(array, axis, bit, pass_on):
-            kept_half = lax.dynamic_index_in_dim(array, bit, axis, keepdims=False)
-            given = lax.dynamic_index_in_dim(array, 1 - bit, axis, keepdims=False)
-            return kept_half + pass_on(given)
-
-        value = value.reshape(count, 2, planes, 2, shard)
-        value = keep_half(value, 1, t // 2, lambda given: neighbour(given, 2))
-        value = keep_half(value, 2, t % 2, lambda given: neighbour(given, 1))
-        span = planes
-        while span > 1:
-            span //= 2
-            hops = [(i, i ^ span) for i in range(planes)]
-            value = value.reshape(count, 2, span, shard)
-            value = keep_half(value, 1, (o // span) % 2, lambda given: lax.ppermute(given, "o", hops))
-        value = value.reshape(count, shard)
-        return value + swapped(value)
 
     targets = mine(target_slot)
     destination = targets // rows
@@ -607,6 +637,8 @@
     )
     w_first = fetch(first_block)
     wo = fetch(out_block)
+    w_gate_up = fetch(gate_up_block)
+    w_down = fetch(down_block)
     rank_down = w_first[:, wide_first : wide_first + rank]
     gain_one = w_first[:, wide_first + rank].astype(f32)
     gain_two = w_first[:, wide_first + rank + 1].astype(f32)
@@ -675,12 +707,8 @@
     entering = carried(leaving, 1)
     layout_grad = outer_sum(unpack, got_grad).astype(bf16)
     upstream = layout_grad.astype(f32) * own_valid
-    ffn_grad = plane_gather(upstream.astype(bf16))
-    entering, ffn_grad, gate_up_block, down_block = lax.optimization_barrier(
-        (entering, ffn_grad, gate_up_block, down_block)
-    )
-    w_gate_up = fetch(gate_up_block)
-    w_down = fetch(down_block)
+    own_grad = upstream.astype(bf16)
+    ffn_grad = jnp.concatenate([own_grad] + [neighbour(own_grad, d) for d in (1, 2, 3)], axis=0)
     gated, mixed, saved = over_blocks(
         mix_kernel, order, resets,
         (projected, projected, projected, projected, cumul, head_gain, entering),
@@ -695,6 +723,7 @@
         return value[first * rows : last * rows]
 
     attended = plane_sum(lambda *d: project_back(members(gated, *d), wo))
+    attended, ffn_grad = lax.optimization_barrier((attended, ffn_grad))
     hidden = inputs + attended
 
     scale_two = rms_scale(hidden)
@@ -705,44 +734,49 @@
     up_sig = jax.nn.sigmoid(gating)
     gate_silu = gating * up_sig
     product = (gate_silu * upward).astype(bf16)
+    product, gating, upward = lax.optimization_barrier((product, gating, upward))
+    up_sig = jax.nn.sigmoid(gating)
+    gate_silu = gating * up_sig
+    total_down = over_cores(ffn_grad, product)
+    total_down, w_down = lax.optimization_barrier((total_down, w_down))
     d_product = project(ffn_grad, w_down)
     d_gating = d_product * upward * up_sig * (1.0 + gating * (1.0 - up_sig))
     d_upward = d_product * gate_silu
     d_gate_up = jnp.concatenate([d_gating.astype(bf16), d_upward.astype(bf16)], axis=1)
-    total_down = over_cores(ffn_grad, product)
 
     def second_part(*d):
-        nonlocal total_down
-        piece = project_back(members(d_gate_up, *d), w_gate_up)
-        if d[0] == 1:
-            piece, total_down = lax.optimization_barrier((piece, total_down))
-        return piece
-
-    d_normed_two = plane_sum(second_part)
-    total_gate_up = over_cores(normed_two, d_gate_up)
-    d_normed_two, total_gate_up = lax.optimization_barrier((d_normed_two, total_gate_up))
+        return project_back(members(d_gate_up, *d), w_gate_up)
+
     part_down = over_planes(total_down)
+    d_normed_two, total_gate_up, _, part_down = plane_sum(
+        second_part, over_cores(normed_two, d_gate_up), hold=part_down
+    )
     part_gate_up = over_planes(total_gate_up)
     grad_gain_two = jnp.sum(d_normed_two * unit_two, axis=0)
     d_hidden = upstream + norm_back(d_normed_two * gain_two, unit_two, scale_two)
 
-    attn_grad = plane_gather(d_hidden.astype(bf16))
-    attn_grad, part_down = lax.optimization_barrier((attn_grad, part_down))
+    low_hidden, product = lax.optimization_barrier((d_hidden.astype(bf16), product))
+    attn_grad = plane_gather(low_hidden)
+    out_across = project_back(members(product, 3, 4), w_down).astype(bf16)
+    out_sides = project_back(members(product, 1, 3), w_down).astype(bf16)
+    out_own = project_back(members(product, 0, 1), w_down)
+    attn_grad, out_across, out_sides, out_own = lax.optimization_barrier(
+        (attn_grad, out_across, out_sides, out_own)
+    )
+    out_parts = [
+        neighbour(out_sides[:rows], 1), neighbour(out_sides[rows:], 2), neighbour(out_across, 3)
+    ]
     d_gated = project(attn_grad, wo)
     part_out = over_planes(over_cores(attn_grad, gated))
-    product, d_gated = lax.optimization_barrier((product, d_gated))
-    ffn_out = plane_sum(lambda *d: project_back(members(product, *d), w_down))
-    result = ((hidden + ffn_out) * own_valid).astype(bf16)
 
     def both(value):
-        other = swapped(value)
-        return jnp.stack([jnp.where(c == 0, value, other), jnp.where(c == 0, other, value)])
+        return stack_cores(value, swapped(value), c)
 
     def outward(value):
         return exchange(project(unpack, value).astype(bf16))
 
     def homeward(value):
-        return restored(outer_sum(pack, value).astype(bf16))
+        return restore_rows(pack, value, planes)
 
     d_mixed, d_gate_pre, head_part, pulled = over_blocks(
         pull_kernel, order, resets,
@@ -759,7 +793,12 @@
         1 << 30, 12 << 20,
     )
     later = carried(pulled, -1)
-    later, result, part_gate_up = lax.optimization_barrier((later, result, part_gate_up))
+    later, out_sides, out_across, out_own, part_gate_up = lax.optimization_barrier(
+        (later, out_sides, out_across, out_own, part_gate_up)
+    )
+    for piece in out_parts:
+        out_own = out_own + piece.astype(f32)
+    result = ((hidden + out_own) * own_valid).astype(bf16)
     back_output = outward(result)
     grads, d_decays = over_blocks(
         back_kernel, order, resets,
@@ -782,31 +821,22 @@
     total_first = over_cores(normed, grads)
 
     def first_part(*d):
-        nonlocal total_first
         product_part = project_back(members(grads, *d), w_first[:, :wide_first])
-        piece = jnp.concatenate([product_part, members(rank_part, *d)], axis=1)
-        if d[0] == 1:
-            piece, total_first = lax.optimization_barrier((piece, total_first))
-        return piece
-
-    summed, back_output = plane_sum(first_part, back_output)
+        return jnp.concatenate([product_part, members(rank_part, *d)], axis=1)
+
+    summed, total_first, back_output, _ = plane_sum(first_part, total_first, back_output, d_hidden)
     part_first = over_planes(total_first)
-    summed, part_out = lax.optimization_barrier((summed, part_out))
     own_output = homeward(back_output)
     both_output = both(own_output)
-    grad_down = deliver(part_down)
-    grad_gate_up = deliver(part_gate_up)
-    grad_out = deliver(part_out)
     rank_grad = summed[:, width : width + rank].astype(bf16)
     d_normed = summed[:, :width] + project_back(rank_grad, rank_down)
     grad_gain_one = jnp.sum(d_normed * unit_one, axis=0)
     d_inputs = d_hidden + norm_back(d_normed * gain_one, unit_one, scale_one)
-    back_input = outward(d_inputs.astype(bf16))
+    packed_input = project(unpack, d_inputs.astype(bf16)).astype(bf16)
     own_normed = (unit_one * gain_one).astype(bf16)
     wide_rows = jnp.concatenate(
         [outer_sum(rank_grad, own_normed), grad_gain_one[None], grad_gain_two[None]], axis=0
     )
-    own_wide = own_columns(wide_rows)
 
     home_valid = layout_valid(starts, lengths, targets)[:, None]
     difference = own_output.astype(f32) - mine(teacher).astype(f32)
@@ -822,7 +852,16 @@
         ],
         axis=0,
     )
+    packed_input, everything = lax.optimization_barrier((packed_input, everything))
+    back_input = exchange(packed_input)
+    everything = jnp.concatenate([everything, wide_rows.reshape(-1, HEAD_K)], axis=0)
     everything = everything + swapped(everything)
+    everything, part_down, part_gate_up, part_out = lax.optimization_barrier(
+        (everything, part_down, part_gate_up, part_out)
+    )
+    grad_down = deliver(part_down)
+    grad_gate_up = deliver(part_gate_up)
+    grad_out = deliver(part_out)
     for distance in (1, 2):
         everything = everything + neighbour(everything, distance)
     distance = 1
@@ -830,11 +869,26 @@
         hops = [(i, i ^ distance) for i in range(planes)]
         everything = everything + lax.ppermute(everything, "o", hops)
         distance *= 2
-    back_input, part_first, own_wide, everything, grad_down, grad_gate_up, grad_out, both_output = (
-        lax.optimization_barrier(
-            (back_input, part_first, own_wide, everything, grad_down, grad_gate_up, grad_out, both_output)
-        )
-    )
+    def columns(pair_of, start, size):
+        return jnp.concatenate([piece[:, start : start + size] for piece in pair_of], axis=1)
+
+    grad_first = deliver(part_first)
+    finished = (
+        columns(grad_first, 0, HEAD_K),
+        columns(grad_first, HEAD_K, HEAD_K),
+        columns(grad_first, 2 * HEAD_K, HEAD_V),
+        columns(grad_first, 2 * HEAD_K + HEAD_V, HEAD_V),
+        columns(grad_out, 0, HEAD_V),
+        columns(grad_gate_up, 0, hidden_here),
+        columns(grad_gate_up, hidden_here, hidden_here),
+        columns(grad_down, 0, hidden_here),
+    )
+    back_input, finished, everything, both_output = lax.optimization_barrier(
+        (back_input, finished, everything, both_output)
+    )
+    own_column = (t // 2) * half + (o * 2 + t % 2) * shard
+    wide_sum = everything[GROUP * (rank + 1) + HEAD_V // HEAD_K + 1 :].reshape(rank + 2, width)
+    own_wide = lax.dynamic_slice_in_dim(wide_sum, own_column, shard, 1)
     used = GROUP * (rank + 1)
     summed_small = everything[:used].reshape(GROUP, rank + 1, HEAD_K)
     pair_small = lax.dynamic_slice_in_dim(summed_small, 2 * c, 2, 0)
@@ -843,24 +897,13 @@
     summed_head = everything[used : used + head_rows].reshape(-1)
     summed_loss = everything[used + head_rows, 0]
     own_input_grad = homeward(back_input)
-    grad_first = deliver(part_first)
     loss = summed_loss / (jnp.sum(seq_len).astype(f32) * width)
-
-    def columns(pair_of, start, size):
-        return jnp.concatenate([piece[:, start : start + size] for piece in pair_of], axis=1)
 
     return (
         both_output,
         loss,
         both(own_input_grad),
-        columns(grad_first, 0, HEAD_K),
-        columns(grad_first, HEAD_K, HEAD_K),
-        columns(grad_first, 2 * HEAD_K, HEAD_V),
-        columns(grad_first, 2 * HEAD_K + HEAD_V, HEAD_V),
-        columns(grad_out, 0, HEAD_V),
-        columns(grad_gate_up, 0, hidden_here),
-        columns(grad_gate_up, hidden_here, hidden_here),
-        columns(grad_down, 0, hidden_here),
+        *finished,
         own_wide[:rank].T,
         pair_small[:rank],
         pair_small[rank],

time: 965 us -> 826 us (0.86)
  waiting for transfers between devices: 320 us -> 234 us
  local copies, waits for them, and re-layouts: 74.6 us -> 40.1 us
  matrix products: 193 us -> 170 us
    all_gather x4, waiting for transfers between devices: 57.5 us -> 3.11 us  [fetch(): return lax.all_gather(block, ('c', 'o'), axis=0, tiled=True)]
    ppermute x2, waiting for transfers between devices: 54.1 us -> 17.6 us  [local(): everything = everything + lax.ppermute(everything, 'o', hops)]
    unnamed x210 -> x195, local copies, waits for them, and re-layouts: 43.4 us -> 27 us
    dot_general x13, matrix products: 67.4 us -> 56.8 us  [project_back(): lax.dot_general(left, right, contract_last, preferred_element_type=f32)]
    dot_general x13 -> x11, matrix products: 63.9 us -> 53.6 us  [outer_sum(): lax.dot_general(left, right, contract_rows, preferred_element_type=f32)]
    ppermute x40 -> x34, waiting for transfers between devices: 161 us -> 156 us  [neighbour(): return lax.ppermute(value, 't', [(i, i ^ distance) for i in range(GROUP)])]
    ppermute x40 -> x34, starting transfers between devices: 43.3 us -> 47.6 us  [neighbour(): return lax.ppermute(value, 't', [(i, i ^ distance) for i in range(GROUP)])]
  transfers between devices with their start and end apart: 77 -> 68, of which waited for: 34 -> 31; matrix products, arithmetic and copies ran while one was open for 27% -> 28% of each run, Pallas kernels for 15% -> 17%
where the time goes in v3:
time: 826 us; the launch traced here: 821 us
  waiting for transfers between devices  234 us (28%)
  Pallas kernels  194 us (23%)
  matrix products  170 us (21%)
  starting transfers between devices  97.3 us (12%)
  other arithmetic  66.2 us (8%)
  local copies, waits for them, and re-layouts  40.1 us (5%)
  between operations  18.8 us (2%)
    pallas_call x2, Pallas kernels, deal(): pl.pallas_call(kernel, out_shape=outs, in_specs=[anywhere] * (2 if spread...  158 us
    ppermute x34, waiting for transfers between devices, neighbour(): return lax.ppermute(value, 't', [(i, i ^ distance) for i in range(GROUP)])  156 us
    dot_general x13, matrix products, project_back(): lax.dot_general(left, right, contract_last, preferred_element_type=f32)  56.8 us
    dot_general x11, matrix products, outer_sum(): lax.dot_general(left, right, contract_rows, preferred_element_type=f32)  53.6 us
    dot_general x9, matrix products, project(): return jnp.dot(left, right, preferred_element_type=f32)  53.4 us
    ppermute x34, starting transfers between devices, neighbour(): return lax.ppermute(value, 't', [(i, i ^ distance) for i in range(GROUP)])  47.6 us
    ppermute x6, waiting for transfers between devices, shifted(): return lax.ppermute(value, 'o', hops)  36.2 us
    pallas_call x4, Pallas kernels, over_blocks(): pl.pallas_call(kernel, out_shape=outs, grid_spec=pltpu.PrefetchScalarGrid...  30.7 us
  transfers between devices with their start and end apart: 68, of which 31 were waited for; matrix products, arithmetic and copies ran while one was open for 28% of the time, Pallas kernels for 17%

profile of v3, /device:TPU:0, one launch (start us, length us, event | category | flops | bytes accessed | tf_op | source)
XLA Modules:
  0.0 820.8 jit_solution(14261699277588905176)
XLA Ops:
  12.2 47.2 %shard_map.323 = (bf16[512,2176]{1,0:T(8,128)(2,1)S(1)}, bf16[256,1664]{1,0:T(8,128)(2,1)}, bf16[256,512]{1,0:T(8,128)(2,1)}) custom-call(bf16[512,2176]{1,0:T(8,128)(2,1)S(1)} %convolution_convert_fusion.1.refs_0_, bf16[128,512]{1,0:T(8,128)(2,1)S(1)} %copy-done.24, bf16[128,512]{1,0:T(8,128)(2,1)S(1)} %copy-done.25, bf16[128,1024]{1,0:T(8,128)(2,1)S(1)} %copy-done.21, ...), custom_call_target="tpu_custom_call" | custom-call | bytes 157286400 | tf_op jit(solution)/shard_map/pallas_call | solution.py:384
  64.7 110.7 %shard_map.324 = (bf16[512,2048]{1,0:T(8,128)(2,1)S(1)}, bf16[3,256,2048]{2,1,0:T(8,128)(2,1)S(1)}, bf16[256,2816]{1,0:T(8,128)(2,1)S(1)}, bf16[256,1408]{1,0:T(8,128)(2,1)}) custom-call(bf16[512,2048]{1,0:T(8,128)(2,1)S(1)} %convolution_convert_fusion.6.refs_0_, bf16[256,2048]{1,0:T(8,128)(2,1)S(1)} %convolution_convert_fusion.11.refs_1_, ...), custom_call_target="tpu_custom_call" | custom-call | bytes 157286400 | tf_op jit(solution)/shard_map/pallas_call | solution.py:384
  184.8 4.5 fusion.2
  189.3 7.7 fusion.164.key_ref.value_ref.query_ref.gate_ref
  200.0 5.6 shard_map.325
  219.0 8.8 %collective-permute-start.1 = (bf16[514,256]{1,0:T(8,128)(2,1)S(1)}, bf16[514,256]{1,0:T(8,128)(2,1)S(1)}, u32[]{:S(2)}, u32[]{:S(2)}) collective-permute-start(bf16[514,256]{1,0:T(8,128)(2,1)S(1)} %pad_maximum_fusion.17), channel_id=1, source_target_pairs={{0,24},{1,25},{2,26},{3,27},{4,28},{5,29},{6,30},{7,31}} | collective-permute-start | bytes 789512 | tf_op jit(solution)/shard_map/ppermute | solution.py:694
  228.0 11.6 %collective-permute-done.1 = bf16[514,256]{1,0:T(8,128)(2,1)S(1)} collective-permute-done((bf16[514,256]{1,0:T(8,128)(2,1)S(1)}, bf16[514,256]{1,0:T(8,128)(2,1)S(1)}, u32[]{:S(2)}, u32[]{:S(2)}) %collective-permute-start.1) | collective-permute-done | bytes 263200 | tf_op jit(solution)/shard_map/ppermute | solution.py:694
  239.8 7.2 shard_map.326
  254.1 20.1 %collective-permute-done.4 = bf16[128,2048]{1,0:T(8,128)(2,1)S(1)} collective-permute-done((bf16[128,2048]{1,0:T(8,128)(2,1)S(1)}, bf16[128,2048]{1,0:T(8,128)(2,1)S(1)}, u32[]{:S(2)}, u32[]{:S(2)}) %collective-permute-start.4) | collective-permute-done | bytes 524320 | tf_op jit(solution)/shard_map/ppermute | solution.py:497
  283.4 5.6 collective-permute-done.6
  290.6 7.5 collective-permute-done.7
  306.6 22.8 %collective-permute-done.13 = bf16[256,2048]{1,0:T(8,128)(2,1)S(1)} collective-permute-done((bf16[256,2048]{1,0:T(8,128)(2,1)}, bf16[256,2048]{1,0:T(8,128)(2,1)S(1)}, u32[]{:S(2)}, u32[]{:S(2)}) %collective-permute-start.13) | collective-permute-done | bytes 1048608 | tf_op jit(solution)/shard_map/ppermute | solution.py:497
  336.9 6.0 collective-permute-done.15
  345.7 17.3 %fusion.165 = f32[1024,2816]{1,0:T(8,128)S(1)} fusion(bf16[1024,2048]{1,0:T(8,128)(2,1)} %constant_dynamic-update-slice_fusion.2, bf16[2048,2816]{1,0:T(8,128)(2,1)} %all-gather.9.cloned.1.call-done), kind=kOutput, calls=%fused_computation.333 | convolution fusion | flops 11811160064 | bytes 27262976 | tf_op jit(solution)/shard_map/dot_general | solution.py:41
  363.0 5.4 fusion.148
  368.4 4.9 convolution_convert_fusion.3
  373.3 5.6 collective-permute-done.17
  378.9 8.4 %add_convert_fusion.2 = bf16[1024,1408]{1,0:T(8,128)(2,1)} fusion(bf16[1024,1408]{1,0:T(8,128)(2,1)} %collective-permute-done.17, bf16[1024,1408]{1,0:T(8,128)(2,1)} %copy-done.44, bf16[1024,2048]{1,0:T(8,128)(2,1)} %pad_maximum_fusion.3, s32[]{:T(128)S(6)} %select_n.185), kind=kOutput, calls=%fused_computation.14 | convolution fusion | flops 2957115392 | bytes 10747908 | tf_op jit(solution)/shard_map/dot_general | solution.py:49
  389.7 14.2 %multiply_convert_fusion.1 = (bf16[1024,1408]{1,0:T(8,128)(2,1)S(1)}, bf16[1024,1408]{1,0:T(8,128)(2,1)S(1)}) fusion(f32[1024,1408]{1,0:T(8,128)} %get-tuple-element.111, f32[1024,1408]{1,0:T(8,128)} %get-tuple-element.110, bf16[1024,2048]{1,0:T(8,128)(2,1)} %pad_maximum_fusion.3, bf16[2048,1408]{1,0:T(8,128)(2,1)} %all-gather.11.cloned.1.call-done), kind=kOutput, calls=%fused_computation.12 | convolution fusion | flops 5924323328 | bytes 27262976 | tf_op jit(solution)/shard_map/dot_general | solution.py:41
  403.9 8.5 %convolution_convert_fusion = bf16[1024,2816]{1,0:T(8,128)(2,1)} fusion(bf16[1024,1408]{1,0:T(8,128)(2,1)S(1)} %get-tuple-element.188, bf16[1024,1408]{1,0:T(8,128)(2,1)S(1)} %get-tuple-element.187, bf16[1024,2048]{1,0:T(8,128)(2,1)S(1)} %copy-done.52, s32[]{:T(128)S(6)} %select_n.186), kind=kOutput, calls=%fused_computation.16 | convolution fusion | flops 5919997952 | bytes 13631492 | tf_op jit(solution)/shard_map/dot_general | solution.py:49
  412.8 9.5 %fusion.57 = f32[256,2048]{1,0:T(8,128)} fusion(bf16[2048,2816]{1,0:T(8,128)(2,1)} %all-gather.9.cloned.1.call-done, bf16[1024,1408]{1,0:T(8,128)(2,1)} %copy-done.84, bf16[1024,1408]{1,0:T(8,128)(2,1)} %copy-done.81), kind=kOutput, calls=%fused_computation.98 | convolution fusion | flops 2955673600 | bytes 19398656 | tf_op jit(solution)/shard_map/dot_general | solution.py:45
  422.3 10.3 %add_convert_fusion = bf16[1024,2816]{1,0:T(8,128)(2,1)} fusion(bf16[1024,2816]{1,0:T(8,128)(2,1)} %collective-permute-done.18, bf16[1024,1408]{1,0:T(8,128)(2,1)S(1)} %copy-done.85, bf16[1024,1408]{1,0:T(8,128)(2,1)S(1)} %copy-done.82, bf16[1024,2048]{1,0:T(8,128)(2,1)S(1)} %copy-done.53, s32[]{:T(128)S(6)} %select_n.185), kind=kOutput, calls=%fused_computation | convolution fusion | flops 5925765120 | bytes 19398660 | tf_op jit(solution)/shard_map/dot_general | solution.py:49
  433.2 8.0 convolution_convert_fusion.8
  444.2 9.1 %fusion.163 = (bf16[512,2048]{1,0:T(8,128)(2,1)S(1)}, f32[512,2048]{1,0:T(8,128)S(1)}) fusion(bf16[2048,2816]{1,0:T(8,128)(2,1)} %all-gather.9.cloned.1.call-done, bf16[1024,1408]{1,0:T(8,128)(2,1)S(1)} %copy-done.86, bf16[1024,1408]{1,0:T(8,128)(2,1)S(1)} %copy-done.83), kind=kOutput, calls=%fused_computation.331 | convolution fusion | flops 5912395776 | bytes 23592960 | tf_op jit(solution)/shard_map/dot_general | solution.py:45
  462.5 6.5 collective-permute-done.24
  469.8 9.3 %collective-permute-done.23 = bf16[128,2048]{1,0:T(8,128)(2,1)} collective-permute-done((bf16[128,2048]{1,0:T(8,128)(2,1)}, bf16[128,2048]{1,0:T(8,128)(2,1)}, u32[]{:S(2)}, u32[]{:S(2)}) %collective-permute-start.23) | collective-permute-done | bytes 524320 | tf_op jit(solution)/shard_map/ppermute | solution.py:497
  490.3 4.3 fusion.147
  495.7 5.8 fusion.93
  508.0 8.9 %collective-permute-done.25 = bf16[256,2048]{1,0:T(8,128)(2,1)S(1)} collective-permute-done((bf16[256,2048]{1,0:T(8,128)(2,1)S(1)}, bf16[256,2048]{1,0:T(8,128)(2,1)S(1)}, u32[]{:S(2)}, u32[]{:S(2)}) %collective-permute-start.25) | collective-permute-done | bytes 1048608 | tf_op jit(solution)/shard_map/ppermute | solution.py:497
  520.6 8.0 collective-permute-done.27
  531.3 5.3 shard_map.327
  545.7 24.5 %collective-permute-done.30 = bf16[514,256]{1,0:T(8,128)(2,1)S(1)} collective-permute-done((bf16[514,256]{1,0:T(8,128)(2,1)S(1)}, bf16[514,256]{1,0:T(8,128)(2,1)S(1)}, u32[]{:S(2)}, u32[]{:S(2)}) %collective-permute-start.30) | collective-permute-done | bytes 263200 | tf_op jit(solution)/shard_map/ppermute | solution.py:694
  581.6 7.5 reduce-scatter.7.cloned.1.call-done
  589.1 18.2 %collective-permute-done.36 = bf16[256,2048]{1,0:T(8,128)(2,1)} collective-permute-done((bf16[256,2048]{1,0:T(8,128)(2,1)}, bf16[256,2048]{1,0:T(8,128)(2,1)}, u32[]{:S(2)}, u32[]{:S(2)}) %collective-permute-start.36) | collective-permute-done | bytes 1048608 | tf_op jit(solution)/shard_map/ppermute | solution.py:497
  607.3 5.5 convolution_convert_fusion.5
  612.8 10.7 %all-to-all-start = ((bf16[16,32,2048]{2,1,0:T(8,128)(2,1)}), bf16[16,32,2048]{2,1,0:T(8,128)(2,1)S(1)}, u32[]{:S(2)}, u32[]{:S(2)}) async-start(bf16[16,32,2048]{2,1,0:T(8,128)(2,1)} %bitcast.85), calls=%async_computation.2 | async-start | bytes 4194304 | tf_op jit(solution)/shard_map/all_to_all | solution.py:595
  627.4 12.5 %shard_map.328 = (bf16[1024,1536]{1,0:T(8,128)(2,1)S(1)}, f32[1024,256]{1,0:T(8,128)S(1)}) custom-call(s32[4]{0:T(128)S(1)} %copy-done.27, s32[16]{0:T(128)S(1)} %copy-done.29, f32[1024,1664]{1,0:T(8,128)} %copy-done, f32[1024,1664]{1,0:T(8,128)} %copy-done, f32[1024,1664]{1,0:T(8,128)} %copy-done, f32[1024,256]{1,0:T(8,128)S(1)} %copy-done.5, ...), custom_call_target="tpu_custom_call" | custom-call | flops 8589934592 | bytes 25165824 | tf_op jit(solution)/shard_map/pallas_call | solution.py:471
  643.3 4.8 convolution_convert_fusion.2
  663.7 5.0 fusion.7
  671.4 6.5 add_convert_fusion.1
  691.0 5.5 collective-permute-done.40
  704.0 4.6 convolution_convert_fusion.4
  709.2 6.6 all-to-all-start.1
  723.4 7.2 collective-permute-done.47
  732.4 10.3 %collective-permute-start.53 = (f32[215,256]{1,0:T(8,128)S(1)}, f32[215,256]{1,0:T(8,128)S(1)}, u32[]{:S(2)}, u32[]{:S(2)}) collective-permute-start(f32[215,256]{1,0:T(8,128)S(1)} %add.346), channel_id=1, source_target_pairs={{0,4},{2,6},{4,0},{6,2},{1,5},{3,7},{5,1},{7,3},{8,12},{10,14},{12... | collective-permute-start | bytes 660488 | tf_op jit(solution)/shard_map/ppermute | solution.py:497
  744.2 26.1 %collective-permute-done.53 = f32[215,256]{1,0:T(8,128)S(1)} collective-permute-done((f32[215,256]{1,0:T(8,128)S(1)}, f32[215,256]{1,0:T(8,128)S(1)}, u32[]{:S(2)}, u32[]{:S(2)}) %collective-permute-start.53) | collective-permute-done | bytes 220192 | tf_op jit(solution)/shard_map/ppermute | solution.py:497
  774.2 9.8 %collective-permute-done.54 = f32[215,256]{1,0:T(8,128)S(1)} collective-permute-done((f32[215,256]{1,0:T(8,128)S(1)}, f32[215,256]{1,0:T(8,128)S(1)}, u32[]{:S(2)}, u32[]{:S(2)}) %collective-permute-start.54) | collective-permute-done | bytes 220192 | tf_op jit(solution)/shard_map/ppermute | solution.py:870
  790.0 7.8 collective-permute-done.55
  (481 shorter events, 214.1 us)
Async XLA Ops:
  7.2 175.6 %all-gather.5.cloned.1.call-start = ((), (), s32[]{:S(2)}) async-start(), calls=%async_computation.6 | async-start | bytes 7667712 | tf_op jit(solution)/shard_map/all_gather | solution.py:567
  59.5 188.6 %all-gather.7.cloned.1.call-start = ((), (), s32[]{:S(2)}) async-start(), calls=%async_computation.7 | async-start | bytes 2359296 | tf_op jit(solution)/shard_map/all_gather | solution.py:567
  60.2 285.5 %all-gather.9.cloned.1.call-start = ((), (), s32[]{:S(2)}) async-start(), calls=%async_computation.8 | async-start | bytes 12976128 | tf_op jit(solution)/shard_map/all_gather | solution.py:567
  178.2 211.5 %all-gather.11.cloned.1.call-start = ((), (), s32[]{:S(2)}) async-start(), calls=%async_computation.9 | async-start | bytes 6488064 | tf_op jit(solution)/shard_map/all_gather | solution.py:567
  209.7 18.3 %collective-permute-start.3 = (bf16[514,256]{1,0:T(8,128)(2,1)S(1)}, bf16[514,256]{1,0:T(8,128)(2,1)S(1)}, u32[]{:S(2)}, u32[]{:S(2)}) collective-permute-start(bf16[514,256]{1,0:T(8,128)(2,1)S(1)} %pad_maximum_fusion.17), channel_id=1, source_target_pairs={{0,8},{8,16},{16,24},{1,9},{9,17},{17,25},{2,10},{10,18},{18,26},{... | collective-permute-start | bytes 789512 | tf_op jit(solution)/shard_map/ppermute | solution.py:694
  215.5 62.6 %collective-permute-start.10 = (bf16[256,2048]{1,0:T(8,128)(2,1)}, bf16[256,2048]{1,0:T(8,128)(2,1)}, u32[]{:S(2)}, u32[]{:S(2)}) collective-permute-start(bf16[256,2048]{1,0:T(8,128)(2,1)} %get-tuple-element.249), channel_id=1, source_target_pairs={{0,2},{2,0},{4,6},{6,4},{1,3},{3,1},{5,7},{7,5},{8,10},{10,8},{12,... | collective-permute-start | bytes 3145736 | tf_op jit(solution)/shard_map/ppermute | solution.py:497
  216.2 62.3 %collective-permute-start.11 = (bf16[256,2048]{1,0:T(8,128)(2,1)}, bf16[256,2048]{1,0:T(8,128)(2,1)}, u32[]{:S(2)}, u32[]{:S(2)}) collective-permute-start(bf16[256,2048]{1,0:T(8,128)(2,1)} %get-tuple-element.249), channel_id=1, source_target_pairs={{0,4},{2,6},{4,0},{6,2},{1,5},{3,7},{5,1},{7,3},{8,12},{10,14},{12... | collective-permute-start | bytes 3145736 | tf_op jit(solution)/shard_map/ppermute | solution.py:497
  219.0 60.7 %collective-permute-start.12 = (bf16[256,2048]{1,0:T(8,128)(2,1)}, bf16[256,2048]{1,0:T(8,128)(2,1)}, u32[]{:S(2)}, u32[]{:S(2)}) collective-permute-start(bf16[256,2048]{1,0:T(8,128)(2,1)} %get-tuple-element.249), channel_id=1, source_target_pairs={{0,6},{2,4},{4,2},{6,0},{1,7},{3,5},{5,3},{7,1},{8,14},{10,12},{12... | collective-permute-start | bytes 3145736 | tf_op jit(solution)/shard_map/ppermute | solution.py:497
  219.0 20.6 %collective-permute-start.1 = (bf16[514,256]{1,0:T(8,128)(2,1)S(1)}, bf16[514,256]{1,0:T(8,128)(2,1)S(1)}, u32[]{:S(2)}, u32[]{:S(2)}) collective-permute-start(bf16[514,256]{1,0:T(8,128)(2,1)S(1)} %pad_maximum_fusion.17), channel_id=1, source_target_pairs={{0,24},{1,25},{2,26},{3,27},{4,28},{5,29},{6,30},{7,31}} | collective-permute-start | bytes 789512 | tf_op jit(solution)/shard_map/ppermute | solution.py:694
  250.7 23.5 %collective-permute-start.4 = (bf16[128,2048]{1,0:T(8,128)(2,1)S(1)}, bf16[128,2048]{1,0:T(8,128)(2,1)S(1)}, u32[]{:S(2)}, u32[]{:S(2)}) collective-permute-start(bf16[128,2048]{1,0:T(8,128)(2,1)S(1)} %get-tuple-element.220), channel_id=1, source_target_pairs={{0,2},{2,0},{4,6},{6,4},{1,3},{3,1},{5,7},{7,5},{8,10},{10,8},{12,... | collective-permute-start | bytes 1572872 | tf_op jit(solution)/shard_map/ppermute | solution.py:497
  251.4 24.4 %collective-permute-start.5 = (bf16[128,2048]{1,0:T(8,128)(2,1)S(1)}, bf16[128,2048]{1,0:T(8,128)(2,1)S(1)}, u32[]{:S(2)}, u32[]{:S(2)}) collective-permute-start(bf16[128,2048]{1,0:T(8,128)(2,1)S(1)} %get-tuple-element.219), channel_id=1, source_target_pairs={{0,4},{2,6},{4,0},{6,2},{1,5},{3,7},{5,1},{7,3},{8,12},{10,14},{12... | collective-permute-start | bytes 1572872 | tf_op jit(solution)/shard_map/ppermute | solution.py:497
  274.2 14.9 %collective-permute-start.6 = (bf16[128,2048]{1,0:T(8,128)(2,1)S(1)}, bf16[128,2048]{1,0:T(8,128)(2,1)S(1)}, u32[]{:S(2)}, u32[]{:S(2)}) collective-permute-start(bf16[128,2048]{1,0:T(8,128)(2,1)S(1)} %get-tuple-element.205), channel_id=1, source_target_pairs={{0,2},{2,0},{4,6},{6,4},{1,3},{3,1},{5,7},{7,5},{8,10},{10,8},{12,... | collective-permute-start | bytes 1572872 | tf_op jit(solution)/shard_map/ppermute | solution.py:497
  278.2 20.0 %collective-permute-start.7 = (bf16[128,2048]{1,0:T(8,128)(2,1)S(1)}, bf16[128,2048]{1,0:T(8,128)(2,1)S(1)}, u32[]{:S(2)}, u32[]{:S(2)}) collective-permute-start(bf16[128,2048]{1,0:T(8,128)(2,1)S(1)} %get-tuple-element.197), channel_id=1, source_target_pairs={{0,2},{2,0},{4,6},{6,4},{1,3},{3,1},{5,7},{7,5},{8,10},{10,8},{12,... | collective-permute-start | bytes 1572872 | tf_op jit(solution)/shard_map/ppermute | solution.py:497
  278.5 22.4 %collective-permute-start.8 = (bf16[128,2048]{1,0:T(8,128)(2,1)S(1)}, bf16[128,2048]{1,0:T(8,128)(2,1)S(1)}, u32[]{:S(2)}, u32[]{:S(2)}) collective-permute-start(bf16[128,2048]{1,0:T(8,128)(2,1)S(1)} %get-tuple-element.196), channel_id=1, source_target_pairs={{0,4},{2,6},{4,0},{6,2},{1,5},{3,7},{5,1},{7,3},{8,12},{10,14},{12... | collective-permute-start | bytes 1572872 | tf_op jit(solution)/shard_map/ppermute | solution.py:497
  304.8 24.6 %collective-permute-start.13 = (bf16[256,2048]{1,0:T(8,128)(2,1)}, bf16[256,2048]{1,0:T(8,128)(2,1)S(1)}, u32[]{:S(2)}, u32[]{:S(2)}) collective-permute-start(bf16[256,2048]{1,0:T(8,128)(2,1)} %get-tuple-element.182), channel_id=1, source_target_pairs={{0,2},{2,0},{4,6},{6,4},{1,3},{3,1},{5,7},{7,5},{8,10},{10,8},{12,... | collective-permute-start | bytes 3145736 | tf_op jit(solution)/shard_map/ppermute | solution.py:497
  306.3 24.5 %collective-permute-start.14 = (bf16[256,2048]{1,0:T(8,128)(2,1)}, bf16[256,2048]{1,0:T(8,128)(2,1)}, u32[]{:S(2)}, u32[]{:S(2)}) collective-permute-start(bf16[256,2048]{1,0:T(8,128)(2,1)} %get-tuple-element.182), channel_id=1, source_target_pairs={{0,4},{2,6},{4,0},{6,2},{1,5},{3,7},{5,1},{7,3},{8,12},{10,14},{12... | collective-permute-start | bytes 3145736 | tf_op jit(solution)/shard_map/ppermute | solution.py:497
  330.3 155.7 %reduce-scatter.5.cloned.1.call-start = ((), (), s32[]{:S(2)}) async-start(), calls=%async_computation.10 | async-start | bytes 3604480 | tf_op jit(solution)/shard_map/reduce_scatter | solution.py:576
  412.7 176.4 %reduce-scatter.7.cloned.1.call-start = ((), (), s32[]{:S(2)}) async-start(), calls=%async_computation.11 | async-start | bytes 7208960 | tf_op jit(solution)/shard_map/reduce_scatter | solution.py:576
  432.7 284.1 %reduce-scatter.11.cloned.1.call-start = ((), (), s32[]{:S(2)}) async-start(), calls=%async_computation.13 | async-start | bytes 1310720 | tf_op jit(solution)/shard_map/reduce_scatter | solution.py:576
  454.2 14.8 %collective-permute-start.24 = (bf16[128,2048]{1,0:T(8,128)(2,1)S(1)}, bf16[128,2048]{1,0:T(8,128)(2,1)S(1)}, u32[]{:S(2)}, u32[]{:S(2)}) collective-permute-start(bf16[128,2048]{1,0:T(8,128)(2,1)S(1)} %get-tuple-element.202), channel_id=1, source_target_pairs={{0,4},{2,6},{4,0},{6,2},{1,5},{3,7},{5,1},{7,3},{8,12},{10,14},{12... | collective-permute-start | bytes 1572872 | tf_op jit(solution)/shard_map/ppermute | solution.py:497
  457.8 21.3 %collective-permute-start.23 = (bf16[128,2048]{1,0:T(8,128)(2,1)}, bf16[128,2048]{1,0:T(8,128)(2,1)}, u32[]{:S(2)}, u32[]{:S(2)}) collective-permute-start(bf16[128,2048]{1,0:T(8,128)(2,1)} %get-tuple-element.194), channel_id=1, source_target_pairs={{0,4},{2,6},{4,0},{6,2},{1,5},{3,7},{5,1},{7,3},{8,12},{10,14},{12... | collective-permute-start | bytes 1572872 | tf_op jit(solution)/shard_map/ppermute | solution.py:497
  460.2 20.2 %collective-permute-start.21 = (bf16[128,2048]{1,0:T(8,128)(2,1)}, bf16[128,2048]{1,0:T(8,128)(2,1)}, u32[]{:S(2)}, u32[]{:S(2)}) collective-permute-start(bf16[128,2048]{1,0:T(8,128)(2,1)} %get-tuple-element.203), channel_id=1, source_target_pairs={{0,2},{2,0},{4,6},{6,4},{1,3},{3,1},{5,7},{7,5},{8,10},{10,8},{12,... | collective-permute-start | bytes 1572872 | tf_op jit(solution)/shard_map/ppermute | solution.py:497
  460.7 23.0 %collective-permute-start.22 = (bf16[128,2048]{1,0:T(8,128)(2,1)}, bf16[128,2048]{1,0:T(8,128)(2,1)}, u32[]{:S(2)}, u32[]{:S(2)}) collective-permute-start(bf16[128,2048]{1,0:T(8,128)(2,1)} %get-tuple-element.195), channel_id=1, source_target_pairs={{0,2},{2,0},{4,6},{6,4},{1,3},{3,1},{5,7},{7,5},{8,10},{10,8},{12,... | collective-permute-start | bytes 1572872 | tf_op jit(solution)/shard_map/ppermute | solution.py:497
  494.6 22.3 %collective-permute-start.25 = (bf16[256,2048]{1,0:T(8,128)(2,1)S(1)}, bf16[256,2048]{1,0:T(8,128)(2,1)S(1)}, u32[]{:S(2)}, u32[]{:S(2)}) collective-permute-start(bf16[256,2048]{1,0:T(8,128)(2,1)S(1)} %get-tuple-element.121), channel_id=1, source_target_pairs={{0,2},{2,0},{4,6},{6,4},{1,3},{3,1},{5,7},{7,5},{8,10},{10,8},{12,... | collective-permute-start | bytes 3145736 | tf_op jit(solution)/shard_map/ppermute | solution.py:497
  495.2 23.5 %collective-permute-start.26 = (bf16[256,2048]{1,0:T(8,128)(2,1)S(1)}, bf16[256,2048]{1,0:T(8,128)(2,1)S(1)}, u32[]{:S(2)}, u32[]{:S(2)}) collective-permute-start(bf16[256,2048]{1,0:T(8,128)(2,1)S(1)} %get-tuple-element.121), channel_id=1, source_target_pairs={{0,4},{2,6},{4,0},{6,2},{1,5},{3,7},{5,1},{7,3},{8,12},{10,14},{12... | collective-permute-start | bytes 3145736 | tf_op jit(solution)/shard_map/ppermute | solution.py:497
  536.7 33.6 %collective-permute-start.30 = (bf16[514,256]{1,0:T(8,128)(2,1)S(1)}, bf16[514,256]{1,0:T(8,128)(2,1)S(1)}, u32[]{:S(2)}, u32[]{:S(2)}) collective-permute-start(bf16[514,256]{1,0:T(8,128)(2,1)S(1)} %pad_maximum_fusion.16), channel_id=1, source_target_pairs={{16,0},{24,8},{17,1},{25,9},{18,2},{26,10},{19,3},{27,11},{20,4},{... | collective-permute-start | bytes 789512 | tf_op jit(solution)/shard_map/ppermute | solution.py:694
  538.0 34.7 %collective-permute-start.31 = (bf16[514,256]{1,0:T(8,128)(2,1)S(1)}, bf16[514,256]{1,0:T(8,128)(2,1)}, u32[]{:S(2)}, u32[]{:S(2)}) collective-permute-start(bf16[514,256]{1,0:T(8,128)(2,1)S(1)} %pad_maximum_fusion.16), channel_id=1, source_target_pairs={{8,0},{16,8},{24,16},{9,1},{17,9},{25,17},{10,2},{18,10},{26,18},{... | collective-permute-start | bytes 789512 | tf_op jit(solution)/shard_map/ppermute | solution.py:694
  539.3 36.3 %collective-permute-start.29 = (bf16[514,256]{1,0:T(8,128)(2,1)S(1)}, bf16[514,256]{1,0:T(8,128)(2,1)}, u32[]{:S(2)}, u32[]{:S(2)}) collective-permute-start(bf16[514,256]{1,0:T(8,128)(2,1)S(1)} %pad_maximum_fusion.16), channel_id=1, source_target_pairs={{24,0},{25,1},{26,2},{27,3},{28,4},{29,5},{30,6},{31,7}} | collective-permute-start | bytes 789512 | tf_op jit(solution)/shard_map/ppermute | solution.py:694
  543.1 34.4 %collective-permute-start.45 = (bf16[1024,512]{1,0:T(8,128)(2,1)}, bf16[1024,512]{1,0:T(8,128)(2,1)}, u32[]{:S(2)}, u32[]{:S(2)}) collective-permute-start(bf16[1024,512]{1,0:T(8,128)(2,1)} %fusion.51), channel_id=1, source_target_pairs={{0,1},{1,0},{2,3},{3,2},{4,5},{5,4},{6,7},{7,6},{8,9},{9,8},{10,11... | collective-permute-start | bytes 3145736 | tf_op jit(solution)/shard_map/ppermute | solution.py:493
  544.7 44.5 %collective-permute-start.35 = (bf16[256,2048]{1,0:T(8,128)(2,1)}, bf16[256,2048]{1,0:T(8,128)(2,1)}, u32[]{:S(2)}, u32[]{:S(2)}) collective-permute-start(bf16[256,2048]{1,0:T(8,128)(2,1)} %get-tuple-element.200), channel_id=1, source_target_pairs={{0,2},{2,0},{4,6},{6,4},{1,3},{3,1},{5,7},{7,5},{8,10},{10,8},{12,... | collective-permute-start | bytes 3145736 | tf_op jit(solution)/shard_map/ppermute | solution.py:497
  571.0 36.3 %collective-permute-start.36 = (bf16[256,2048]{1,0:T(8,128)(2,1)}, bf16[256,2048]{1,0:T(8,128)(2,1)}, u32[]{:S(2)}, u32[]{:S(2)}) collective-permute-start(bf16[256,2048]{1,0:T(8,128)(2,1)} %get-tuple-element.201), channel_id=1, source_target_pairs={{0,4},{2,6},{4,0},{6,2},{1,5},{3,7},{5,1},{7,3},{8,12},{10,14},{12... | collective-permute-start | bytes 3145736 | tf_op jit(solution)/shard_map/ppermute | solution.py:497
  572.7 34.6 %collective-permute-start.37 = (bf16[256,2048]{1,0:T(8,128)(2,1)}, bf16[256,2048]{1,0:T(8,128)(2,1)}, u32[]{:S(2)}, u32[]{:S(2)}) collective-permute-start(bf16[256,2048]{1,0:T(8,128)(2,1)} %convolution_convert_fusion.12), channel_id=1, source_target_pairs={{0,6},{2,4},{4,2},{6,0},{1,7},{3,5},{5,3},{7,1},{8,14},{10,12},{12... | collective-permute-start | bytes 3145736 | tf_op jit(solution)/shard_map/ppermute | solution.py:497
  612.8 65.1 %all-to-all-start = ((bf16[16,32,2048]{2,1,0:T(8,128)(2,1)}), bf16[16,32,2048]{2,1,0:T(8,128)(2,1)S(1)}, u32[]{:S(2)}, u32[]{:S(2)}) async-start(bf16[16,32,2048]{2,1,0:T(8,128)(2,1)} %bitcast.85), calls=%async_computation.2 | async-start | bytes 4194304 | tf_op jit(solution)/shard_map/all_to_all | solution.py:595
  623.4 161.1 %reduce-scatter.9.cloned.1.call-start = ((), (), s32[]{:S(2)}) async-start(), calls=%async_computation.12 | async-start | bytes 3932160 | tf_op jit(solution)/shard_map/reduce_scatter | solution.py:576
  651.0 26.9 %collective-permute-start.33 = (bf16[128,2176]{1,0:T(8,128)(2,1)}, bf16[128,2176]{1,0:T(8,128)(2,1)}, u32[]{:S(2)}, u32[]{:S(2)}) collective-permute-start(bf16[128,2176]{1,0:T(8,128)(2,1)} %get-tuple-element.215), channel_id=1, source_target_pairs={{0,2},{2,0},{4,6},{6,4},{1,3},{3,1},{5,7},{7,5},{8,10},{10,8},{12,... | collective-permute-start | bytes 1671176 | tf_op jit(solution)/shard_map/ppermute | solution.py:497
  652.9 24.9 %collective-permute-start.34 = (bf16[128,2176]{1,0:T(8,128)(2,1)}, bf16[128,2176]{1,0:T(8,128)(2,1)}, u32[]{:S(2)}, u32[]{:S(2)}) collective-permute-start(bf16[128,2176]{1,0:T(8,128)(2,1)} %get-tuple-element.214), channel_id=1, source_target_pairs={{0,4},{2,6},{4,0},{6,2},{1,5},{3,7},{5,1},{7,3},{8,12},{10,14},{12... | collective-permute-start | bytes 1671176 | tf_op jit(solution)/shard_map/ppermute | solution.py:497
  654.4 15.8 %collective-permute-start.32 = (bf16[1024,1536]{1,0:T(8,128)(2,1)}, bf16[1024,1536]{1,0:T(8,128)(2,1)}, u32[]{:S(2)}, u32[]{:S(2)}) collective-permute-start(bf16[1024,1536]{1,0:T(8,128)(2,1)} %convolution_convert_fusion.2), channel_id=1, source_target_pairs={{0,1},{1,0},{2,3},{3,2},{4,5},{5,4},{6,7},{7,6},{8,9},{9,8},{10,11... | collective-permute-start | bytes 9437192 | tf_op jit(solution)/shard_map/ppermute | solution.py:493
  660.9 30.2 %collective-permute-start.41 = (bf16[128,2176]{1,0:T(8,128)(2,1)}, bf16[128,2176]{1,0:T(8,128)(2,1)}, u32[]{:S(2)}, u32[]{:S(2)}) collective-permute-start(bf16[128,2176]{1,0:T(8,128)(2,1)} %get-tuple-element.198), channel_id=1, source_target_pairs={{0,4},{2,6},{4,0},{6,2},{1,5},{3,7},{5,1},{7,3},{8,12},{10,14},{12... | collective-permute-start | bytes 1671176 | tf_op jit(solution)/shard_map/ppermute | solution.py:497
  661.4 36.3 %collective-permute-start.38 = (bf16[128,2176]{1,0:T(8,128)(2,1)}, bf16[128,2176]{1,0:T(8,128)(2,1)}, u32[]{:S(2)}, u32[]{:S(2)}) collective-permute-start(bf16[128,2176]{1,0:T(8,128)(2,1)} %get-tuple-element.199), channel_id=1, source_target_pairs={{0,2},{2,0},{4,6},{6,4},{1,3},{3,1},{5,7},{7,5},{8,10},{10,8},{12,... | collective-permute-start | bytes 1671176 | tf_op jit(solution)/shard_map/ppermute | solution.py:497
  681.7 14.8 %collective-permute-start.40 = (bf16[128,2176]{1,0:T(8,128)(2,1)}, bf16[128,2176]{1,0:T(8,128)(2,1)S(1)}, u32[]{:S(2)}, u32[]{:S(2)}) collective-permute-start(bf16[128,2176]{1,0:T(8,128)(2,1)} %get-tuple-element.192), channel_id=1, source_target_pairs={{0,4},{2,6},{4,0},{6,2},{1,5},{3,7},{5,1},{7,3},{8,12},{10,14},{12... | collective-permute-start | bytes 1671176 | tf_op jit(solution)/shard_map/ppermute | solution.py:497
  708.7 23.7 %collective-permute-start.56 = (bf16[256,2048]{1,0:T(8,128)(2,1)S(1)}, bf16[256,2048]{1,0:T(8,128)(2,1)S(1)}, u32[]{:S(2)}, u32[]{:S(2)}) collective-permute-start(bf16[256,2048]{1,0:T(8,128)(2,1)S(1)} %shard_map.329.own_ref), channel_id=1, source_target_pairs={{0,1},{1,0},{2,3},{3,2},{4,5},{5,4},{6,7},{7,6},{8,9},{9,8},{10,11... | collective-permute-start | bytes 3145736 | tf_op jit(solution)/shard_map/ppermute | solution.py:493
  709.2 93.0 %all-to-all-start.1 = ((bf16[16,32,2048]{2,1,0:T(8,128)(2,1)}), bf16[16,32,2048]{2,1,0:T(8,128)(2,1)}, u32[]{:S(2)}, u32[]{:S(2)}) async-start(bf16[16,32,2048]{2,1,0:T(8,128)(2,1)} %bitcast.86), calls=%async_computation.3 | async-start | bytes 4194304 | tf_op jit(solution)/shard_map/all_to_all | solution.py:595
  716.8 15.4 %collective-permute-start.52 = (f32[215,256]{1,0:T(8,128)S(1)}, f32[215,256]{1,0:T(8,128)S(1)}, u32[]{:S(2)}, u32[]{:S(2)}) collective-permute-start(f32[215,256]{1,0:T(8,128)S(1)} %fusion.145), channel_id=1, source_target_pairs={{0,2},{2,0},{4,6},{6,4},{1,3},{3,1},{5,7},{7,5},{8,10},{10,8},{12,... | collective-permute-start | bytes 660488 | tf_op jit(solution)/shard_map/ppermute | solution.py:497
  718.8 25.3 %collective-permute-start.50 = (bf16[128,1408]{1,0:T(8,128)(2,1)S(1)}, bf16[128,1408]{1,0:T(8,128)(2,1)S(1)}, u32[]{:S(2)}, u32[]{:S(2)}) collective-permute-start(bf16[128,1408]{1,0:T(8,128)(2,1)S(1)} %get-tuple-element.235), channel_id=1, source_target_pairs={{0,0},{1,4},{2,2},{3,6},{4,1},{5,5},{6,3},{7,7},{8,8},{9,12},{10,1... | collective-permute-start | bytes 1081352 | tf_op jit(solution)/shard_map/ppermute | solution.py:580
  721.6 22.5 %collective-permute-start.51 = (bf16[128,1408]{1,0:T(8,128)(2,1)S(1)}, bf16[128,1408]{1,0:T(8,128)(2,1)S(1)}, u32[]{:S(2)}, u32[]{:S(2)}) collective-permute-start(bf16[128,1408]{1,0:T(8,128)(2,1)S(1)} %get-tuple-element.236), channel_id=1, source_target_pairs={{0,2},{1,6},{2,0},{3,4},{4,3},{5,7},{6,1},{7,5},{8,10},{9,14},{10,... | collective-permute-start | bytes 1081352 | tf_op jit(solution)/shard_map/ppermute | solution.py:580
  730.6 53.5 %collective-permute-start.48 = (bf16[128,2816]{1,0:T(8,128)(2,1)S(1)}, bf16[128,2816]{1,0:T(8,128)(2,1)S(1)}, u32[]{:S(2)}, u32[]{:S(2)}) collective-permute-start(bf16[128,2816]{1,0:T(8,128)(2,1)S(1)} %get-tuple-element.212), channel_id=1, source_target_pairs={{0,0},{1,4},{2,2},{3,6},{4,1},{5,5},{6,3},{7,7},{8,8},{9,12},{10,1... | collective-permute-start | bytes 2162696 | tf_op jit(solution)/shard_map/ppermute | solution.py:580
  732.2 51.9 %collective-permute-start.49 = (bf16[128,2816]{1,0:T(8,128)(2,1)S(1)}, bf16[128,2816]{1,0:T(8,128)(2,1)S(1)}, u32[]{:S(2)}, u32[]{:S(2)}) collective-permute-start(bf16[128,2816]{1,0:T(8,128)(2,1)S(1)} %get-tuple-element.213), channel_id=1, source_target_pairs={{0,2},{1,6},{2,0},{3,4},{4,3},{5,7},{6,1},{7,5},{8,10},{9,14},{10,... | collective-permute-start | bytes 2162696 | tf_op jit(solution)/shard_map/ppermute | solution.py:580
  732.4 37.9 %collective-permute-start.53 = (f32[215,256]{1,0:T(8,128)S(1)}, f32[215,256]{1,0:T(8,128)S(1)}, u32[]{:S(2)}, u32[]{:S(2)}) collective-permute-start(f32[215,256]{1,0:T(8,128)S(1)} %add.346), channel_id=1, source_target_pairs={{0,4},{2,6},{4,0},{6,2},{1,5},{3,7},{5,1},{7,3},{8,12},{10,14},{12... | collective-permute-start | bytes 660488 | tf_op jit(solution)/shard_map/ppermute | solution.py:497
  (111 other events, 1961.0 us)
Sparse Core Ops, SparseCore 0:
  59.6 123.1 all-gather.4
  184.4 27.6 all-gather.6
  214.2 107.7 all-gather.8
  330.4 59.1 all-gather.10
  412.8 54.8 reduce-scatter.4
  469.9 119.2 reduce-scatter.6
  592.0 31.8 reduce-scatter.10
  683.9 87.6 reduce-scatter.8
